TPU v7x, 128 devices: a whole 4x4x4 slice. The times are simulated.
128 devices in a mesh: region: 4 (over x_lo, core), sector: 32 (over y, x_hi, z).
Axes of the slice: x: 4 (x_hi: 2, x_lo: 2; x = x_hi * 2 + x_lo), y: 4, z: 4, core: 2. Of those that a mesh axis runs over, the one named last changes fastest.
Arguments:
- env_left: bfloat16 [4, 8, 2048, 2048], P('region', None, 'sector'), may hold values from -6 to 6
- site_tensor: bfloat16 [4, 2048, 2, 2048], P('region', 'sector'), may hold values from -0.125 to 0.125
- mpo_tensor: float32 [4, 8, 8, 2, 2], P('region'), may hold values from -1 to 1
- env_right: bfloat16 [4, 8, 2048, 2048], P('region', None, 'sector'), may hold values from -0.046875 to 0.046875
- bond_tensor: bfloat16 [4, 2048, 2048], P('region'), may hold values from -0.125 to 0.125
Outputs:
- env_next: bfloat16 [4, 8, 2048, 2048], P('region', None, 'sector')
- bond_image: bfloat16 [4, 2048, 2048], P('region', 'sector')
All inputs are finite; a program needn't handle non-finite values.
Results may differ from a plain program's by a relative error of at most 0.0065.
Values may be sent and summed in bfloat16 or wider, within the bound.
No kernel may reach another device: no remote copies, remote signals or barrier semaphores. Data moves between devices by JAX's collectives and lax.ppermute only.
A program may use at most 128 MiB of HBM per device.

v0:
```python
import jax
import jax.numpy as jnp
from jax import lax
from jax.sharding import PartitionSpec as P


def shifted(block, axis, distance):
    devices = range(lax.axis_size(axis))
    route = [((i - distance) % len(devices), i) for i in devices]
    return lax.ppermute(block, axis, route)


def bond_side(env_right, bond_tensor):
    right_next = shifted(env_right, "region", -1)[0]
    return jnp.einsum(
        "wbc,kc->wbk", right_next, bond_tensor[0], preferred_element_type=jnp.float32
    ).astype(jnp.bfloat16)


def absorb_side(env_left, site_tensor, mpo_tensor):
    gathered = lax.all_gather(site_tensor, "sector", axis=1, tiled=True)[0]
    half_done = jnp.einsum(
        "wak,ksc->wasc", env_left[0], gathered, preferred_element_type=jnp.float32
    )
    carried = jnp.einsum(
        "vwst,vatc->wsac", mpo_tensor[0], half_done, precision=lax.Precision.HIGHEST
    ).astype(jnp.bfloat16)
    width_mpo, states, row_total, columns = carried.shape
    return (gathered, carried.reshape(width_mpo * states, row_total, columns))


def local(env_left, site_tensor, mpo_tensor, env_right, bond_tensor):
    width_mpo = env_left.shape[1]
    states = site_tensor.shape[2]
    gathered, carried = absorb_side(env_left, site_tensor, mpo_tensor)
    bond_right = bond_side(env_right, bond_tensor)
    carried_moved = lax.all_to_all(carried, "sector", split_axis=2, concat_axis=1, tiled=True)
    bond_moved = lax.all_to_all(bond_right, "sector", split_axis=2, concat_axis=1, tiled=True)
    full_rows = carried_moved.shape[1]
    local_cols = carried_moved.shape[2]
    carried_moved = carried_moved.reshape(width_mpo, states, full_rows, local_cols)
    env_new = jnp.einsum(
        "wsac,asb->wcb", carried_moved, gathered, preferred_element_type=jnp.float32
    ).astype(jnp.bfloat16)
    image_rows = lax.psum_scatter(
        jnp.einsum("wka,wbk->ab", env_new, bond_moved, preferred_element_type=jnp.float32),
        "sector",
        scatter_dimension=0,
        tiled=True,
    )
    return (env_new[None], image_rows.astype(jnp.bfloat16)[None])


def solution(mesh):
    return jax.shard_map(
        local,
        mesh=mesh,
        in_specs=(
            P("region", None, "sector", None),
            P("region", "sector", None, None),
            P("region", None, None, None, None),
            P("region", None, "sector", None),
            P("region", None, None),
        ),
        out_specs=(P("region", None, "sector", None), P("region", "sector", None)),
        check_vma=False,
    )
```

profile of v0, /device:TPU:0, one launch (start us, length us, event | category | flops | bytes accessed | tf_op | source)
XLA Modules:
  0.0 603.3 jit_solution(3661465449919293755)
XLA Ops:
  7.2 0.0 all-gather.2.cloned.1.call-start
  7.2 2.0 copy.15
  9.2 0.0 all-gather.2.cloned.1.call-update
  9.2 1.1 collective-permute-start
  10.3 0.8 copy.17
  11.1 26.9 %collective-permute-done = bf16[1,8,64,2048]{3,2,1,0:T(8,128)(2,1)} collective-permute-done((bf16[1,8,64,2048]{3,2,1,0:T(8,128)(2,1)}, bf16[1,8,64,2048]{3,2,1,0:T(8,128)(2,1)}, u32[]{:S(2)}, u32[]{:S(2)}) %collective-permute-start) | collective-permute-done | bytes 2097184 | tf_op jit(solution)/shard_map/ppermute | solution.py:10
  38.0 8.6 %fusion.15 = bf16[8,64,2048]{2,1,0:T(8,128)(2,1)S(1)} fusion(bf16[1,2048,2048]{2,1,0:T(8,128)(2,1)} %param.9, bf16[1,8,64,2048]{3,2,1,0:T(8,128)(2,1)} %collective-permute-done), kind=kOutput, calls=%fused_computation.13 | convolution fusion | flops 4296015872 | bytes 12582912 | tf_op jit(solution)/shard_map/wbc,kc->wbk/dot_general | solution.py:15
  46.6 4.3 copy.22
  50.9 7.9 %reshape.23 = bf16[32,2,16384]{2,1,0:T(2,128)(2,1)} reshape(bf16[2048,8,64]{2,1,0:T(8,128)(2,1)} %bitcast.75) | data formatting | bytes 4194304
  58.7 10.6 %all-to-all-start.1 = ((bf16[32,2,16384]{2,1,0:T(2,128)(2,1)}), bf16[32,2,16384]{2,1,0:T(2,128)(2,1)S(1)}, u32[]{:S(2)}, u32[]{:S(2)}) async-start(bf16[32,2,16384]{2,1,0:T(2,128)(2,1)} %reshape.23), calls=%async_computation.1 | async-start | bytes 4194304 | tf_op jit(solution)/shard_map/all_to_all | solution.py:38
  69.4 126.7 %all-gather.2.cloned.1.call-done = bf16[1,2048,2,2048]{3,1,2,0:T(8,128)(2,1)} async-done(((bf16[1,64,2,2048]{3,1,2,0:T(8,128)(2,1)}), bf16[1,2048,2,2048]{3,1,2,0:T(8,128)(2,1)}) %all-gather.2.cloned.1.call-update) | async-done | bytes 16777232 | tf_op jit(solution)/shard_map/all_gather | solution.py:21
  196.1 13.2 %fusion.2 = f32[8,64,2,2048]{3,0,2,1:T(8,128)S(1)} fusion(bf16[1,2048,2,2048]{3,1,2,0:T(8,128)(2,1)} %all-gather.2.cloned.1.call-done, bf16[8,64,2048,1]{2,1,0,3:T(8,128)(2,1)} %bitcast.79), kind=kOutput, calls=%fused_computation.2 | convolution fusion | flops 8589934592 | bytes 27262976 | tf_op jit(solution)/shard_map/wak,ksc->wasc/dot_general | solution.py:22
  209.3 7.6 %fusion.10 = bf16[8,2,64,2048]{3,0,1,2:T(8,128)(2,1)S(1)} fusion(f32[8,64,2,2048]{3,0,2,1:T(8,128)S(1)} %fusion.2, f32[8,8,2,2]{0,1,3,2:T(8,128)S(1)} %copy.17), kind=kOutput, calls=%fused_computation.12 | convolution fusion | flops 404750336 | bytes 12583936 | tf_op jit(solution)/shard_map/vwst,vatc->wsac/dot_general | solution.py:25
  216.9 4.3 copy.18
  221.2 10.9 %copy.19 = bf16[16,64,2048]{1,0,2:T(8,128)(2,1)} copy(bf16[16,64,2048]{2,1,0:T(8,128)(2,1)} %bitcast.74) | data formatting | bytes 8388608 | tf_op jit(solution)/shard_map/reshape | solution.py:29
  232.1 13.9 %reshape.21 = bf16[32,2,32768]{2,1,0:T(2,128)(2,1)} reshape(bf16[2048,16,64]{2,1,0:T(8,128)(2,1)} %bitcast.72) | data formatting | bytes 8388608
  246.0 0.0 all-to-all-done.1
  246.0 5.9 all-to-all-start
  251.9 0.3 reduce-scatter.2.cloned.1.call-start
  252.2 4.0 reshape.24
  256.2 6.9 %copy.35 = bf16[8,64,32,64]{1,2,3,0:T(8,128)(2,1)} copy(bf16[8,64,32,64]{1,0,3,2:T(8,128)(2,1)} %bitcast.76) | data formatting | bytes 4194304 | tf_op jit(solution)/shard_map/all_to_all | solution.py:38
  263.1 5.8 all_to_all.30
  268.8 36.1 %all-to-all-done = bf16[32,2,32768]{2,1,0:T(2,128)(2,1)} async-done(((bf16[32,2,32768]{2,1,0:T(2,128)(2,1)}), bf16[32,2,32768]{2,1,0:T(2,128)(2,1)}, u32[]{:S(2)}, u32[]{:S(2)}) %all-to-all-start) | async-done | bytes 4194336 | tf_op jit(solution)/shard_map/all_to_all | solution.py:37
  304.9 13.7 %reshape.22 = bf16[2048,16,64]{2,1,0:T(8,128)(2,1)} reshape(bf16[32,2,32768]{2,1,0:T(2,128)(2,1)} %all-to-all-done) | data formatting | bytes 8388608
  318.6 12.0 %copy.21 = bf16[16,32,64,64]{2,1,3,0:T(8,128)(2,1)} copy(bf16[16,32,64,64]{2,0,3,1:T(8,128)(2,1)} %bitcast.73) | data formatting | bytes 8388608 | tf_op jit(solution)/shard_map/all_to_all | solution.py:37
  330.6 12.3 %reshape.12 = bf16[8,2,2048,64]{2,3,1,0:T(8,128)(2,1)} reshape(bf16[16,32,64,64]{2,1,3,0:T(8,128)(2,1)} %copy.21) | data formatting | bytes 8388608 | tf_op jit(solution)/shard_map/reshape | solution.py:41
  342.9 13.6 %bitcast_convert_fusion.1 = bf16[8,64,2048]{2,1,0:T(8,128)(2,1)S(1)} fusion(bf16[8,2,2048,64]{2,3,1,0:T(8,128)(2,1)} %reshape.12, bf16[1,2048,2,2048]{3,1,2,0:T(8,128)(2,1)} %all-gather.2.cloned.1.call-done), kind=kOutput, calls=%fused_computation.10 | convolution fusion | flops 8590983168 | bytes 23068672 | tf_op jit(solution)/shard_map/wsac,asb->wcb/dot_general | solution.py:42
  356.5 0.0 copy-start
  356.5 1.3 copy-done
  357.8 8.1 %convolution_bitcast_fusion = f32[2048,2048]{1,0:T(8,128)} fusion(bf16[8,64,2048]{2,1,0:T(8,128)(2,1)S(1)} %bitcast_convert_fusion.1, bf16[8,2048,64]{1,2,0:T(8,128)(2,1)S(1)} %all_to_all.30), kind=kOutput, calls=%fused_computation.4 | convolution fusion | flops 4294967296 | bytes 20971520 | tf_op jit(solution)/shard_map/wka,wbk->ab/dot_general | solution.py:46
  366.0 0.0 reduce-scatter.2.cloned.1.call-update
  366.0 228.7 %reduce-scatter.2.cloned.1.call-done = f32[64,2048]{1,0:T(8,128)} async-done(((f32[2048,2048]{1,0:T(8,128)}), f32[64,2048]{1,0:T(8,128)}) %reduce-scatter.2.cloned.1.call-update) | async-done | bytes 524304 | tf_op jit(solution)/shard_map/reduce_scatter | solution.py:45
  594.7 1.8 convert_bitcast_fusion
Async XLA Ops:
  7.2 188.9 %all-gather.2.cloned.1.call-start = ((), (), s32[]{:S(2)}) async-start(), calls=%async_computation.3 | async-start | bytes 17301504 | tf_op jit(solution)/shard_map/all_gather | solution.py:21
  9.2 28.7 %collective-permute-start = (bf16[1,8,64,2048]{3,2,1,0:T(8,128)(2,1)}, bf16[1,8,64,2048]{3,2,1,0:T(8,128)(2,1)}, u32[]{:S(2)}, u32[]{:S(2)}) collective-permute-start(bf16[1,8,64,2048]{3,2,1,0:T(8,128)(2,1)} %param.8), channel_id=1, source_target_pairs={{32,0},{64,32},{96,64},{0,96},{33,1},{65,33},{97,65},{1,97},{34,2}... | collective-permute-start | bytes 6291464 | tf_op jit(solution)/shard_map/ppermute | solution.py:10
  58.7 187.3 %all-to-all-start.1 = ((bf16[32,2,16384]{2,1,0:T(2,128)(2,1)}), bf16[32,2,16384]{2,1,0:T(2,128)(2,1)S(1)}, u32[]{:S(2)}, u32[]{:S(2)}) async-start(bf16[32,2,16384]{2,1,0:T(2,128)(2,1)} %reshape.23), calls=%async_computation.1 | async-start | bytes 4194304 | tf_op jit(solution)/shard_map/all_to_all | solution.py:38
  246.0 58.9 %all-to-all-start = ((bf16[32,2,32768]{2,1,0:T(2,128)(2,1)}), bf16[32,2,32768]{2,1,0:T(2,128)(2,1)}, u32[]{:S(2)}, u32[]{:S(2)}) async-start(bf16[32,2,32768]{2,1,0:T(2,128)(2,1)} %reshape.21), calls=%async_computation | async-start | bytes 8388608 | tf_op jit(solution)/shard_map/all_to_all | solution.py:37
  251.9 342.8 %reduce-scatter.2.cloned.1.call-start = ((), (), s32[]{:S(2)}) async-start(), calls=%async_computation.4 | async-start | bytes 17301504 | tf_op jit(solution)/shard_map/reduce_scatter | solution.py:45
  356.5 1.3 copy-start
Sparse Core Ops, SparseCore 0:
  11.1 184.9 all-gather.1
  366.1 228.5 reduce-scatter.1
where the time goes:
time: 605 us; the launch traced here: 603 us
  waiting for transfers between devices  418 us (69%)
  local copies, waits for them, and re-layouts  100 us (17%)
  matrix products  51.1 us (8%)
  starting transfers between devices  17.9 us (3%)
  between operations  14.1 us (2%)
    reduce_scatter x1, waiting for transfers between devices, local(): lax.psum_scatter(jnp.einsum('wka,wbk->ab', env_new, bond_moved, preferred...  229 us
    all_gather x1, waiting for transfers between devices, absorb_side(): gathered = lax.all_gather(site_tensor, 'sector', axis=1, tiled=True)[0]  127 us
    unnamed x7, local copies, waits for them, and re-layouts  42.8 us
    all_to_all x1, waiting for transfers between devices, local(): lax.all_to_all(carried, 'sector', split_axis=2, concat_axis=1, tiled=True)  36.1 us
    ppermute x1, waiting for transfers between devices, shifted(): return lax.ppermute(block, axis, route)  26.9 us
    dot_general x1, matrix products, local(): jnp.einsum('wsac,asb->wcb', carried_moved, gathered, preferred_element_ty...  13.6 us
    dot_general x1, matrix products, absorb_side(): jnp.einsum('wak,ksc->wasc', env_left[0], gathered, preferred_element_type...  13.2 us
    all_to_all x2, local copies, waits for them, and re-layouts, local(): lax.all_to_all(bond_right, 'sector', split_axis=2, concat_axis=1, tiled=T...  12.6 us
  transfers between devices with their start and end apart: 5, of which 4 were waited for; matrix products, arithmetic and copies ran while one was open for 14% of the time, Pallas kernels for 0%

commit v1 on v0

v1 whole, which is shorter than its diff:
```python
import jax
import jax.numpy as jnp
from jax import lax
from jax.experimental import pallas as pl
from jax.experimental.pallas import tpu as pltpu
from jax.sharding import Mesh, PartitionSpec as P

F32, BF16 = jnp.float32, jnp.bfloat16
VMEM_LIMIT = 56 << 20


def hop(block, axis, distance):
    n = lax.axis_size(axis)
    return lax.ppermute(block, axis, [(i, (i + distance) % n) for i in range(n)])


def dot(a, b, dims):
    return lax.dot_general(a, b, (dims, ((), ())), preferred_element_type=F32)


def collect_kernel(at_ref, *refs):
    ins, outs, sem = refs[:16], refs[16:20], refs[20]
    x = at_ref[1]

    def copies(flip):
        made = []
        for state in range(2):
            own = at_ref[2] if state == 0 else at_ref[0]
            for n, (plane, distance) in enumerate([(p, d) for p in range(2) for d in range(4)]):
                where = outs[2 * state + (plane + flip) % 2].at[lax.rem(own + distance, 4)]
                made.append(pltpu.make_async_copy(ins[8 * state + n], where, sem.at[8 * state + n]))
        return made

    for flip in range(2):

        @pl.when(x == flip)
        def _():
            for copy in copies(flip):
                copy.start()
            for copy in copies(flip):
                copy.wait()


def collect(at, blocks):
    shape = jax.ShapeDtypeStruct((4,) + blocks[0].shape, blocks[0].dtype)
    anywhere = pl.BlockSpec(memory_space=pl.ANY)
    return pl.pallas_call(
        collect_kernel,
        out_shape=(shape,) * 4,
        in_specs=[pl.BlockSpec(memory_space=pltpu.SMEM)] + [anywhere] * 16,
        out_specs=(pl.BlockSpec(memory_space=pltpu.VMEM),) * 4,
        scratch_shapes=[pltpu.SemaphoreType.DMA((16,))],
        compiler_params=pltpu.CompilerParams(vmem_limit_bytes=16 << 20),
        cost_estimate=pl.CostEstimate(flops=0, bytes_accessed=8 << 20, transcendentals=0),
        name="collect",
    )(at, *blocks)


def around(near, other, axis):
    near_1, near_3 = hop(near, axis, -1), hop(near, axis, 1)
    other_3, other_1 = hop(other, axis, 1), hop(other, axis, -1)
    near_2 = hop(near_1, axis, -1)
    other_2 = hop(other_3, axis, 1)
    return [near, near_1, near_2, near_3, other, other_1, other_2, other_3]


def gather_site(at, rows):
    first, second = rows[0], rows[1]
    first_other, second_other = hop(first, "x", 1), hop(second, "x", 1)
    blocks = around(first, first_other, "z") + around(second, second_other, "y")
    a_0, a_1, b_0, b_1 = collect(at, blocks)
    return around(a_0, a_1, "y") + around(b_0, b_1, "z")


def site_copies(at_ref, blocks, buffer, sem, column, tile):
    made = []
    for n, (x, distance) in enumerate([(p, d) for p in range(2) for d in range(4)]):
        y, z = lax.rem(at_ref[0] + distance, 4), lax.rem(at_ref[2] + distance, 4)
        columns = pl.ds(pl.multiple_of(column, tile), tile)
        made.append(pltpu.make_async_copy(blocks[n].at[:, :, columns], buffer.at[y, x, :, 0], sem.at[n]))
        made.append(pltpu.make_async_copy(blocks[8 + n].at[:, :, columns], buffer.at[:, x, z, 1], sem.at[8 + n]))
    return made


def bond_kernel(r_ref, b_ref, o_ref):
    rows = o_ref.shape[1]
    full = dot(r_ref[...], b_ref[...], ((1,), (1,)))
    low = lax.broadcasted_iota(jnp.int32, (rows, 128), 1) < 64
    for j in range(o_ref.shape[0] // 2):
        for w in range(full.shape[0] // rows // 2):
            a = full[2 * w * rows : (2 * w + 1) * rows, 128 * j : 128 * j + 128]
            b = full[(2 * w + 1) * rows : (2 * w + 2) * rows, 128 * j : 128 * j + 128]
            lanes = pl.ds(128 * w, 128)
            o_ref[2 * j, :, lanes] = jnp.where(low, a, pltpu.roll(b, 64, 1)).astype(BF16)
            o_ref[2 * j + 1, :, lanes] = jnp.where(low, pltpu.roll(a, 64, 1), b).astype(BF16)


def bond_right(right_next, bond):
    w, rows, c = right_next.shape
    k = bond.shape[0]
    tile = 256
    return pl.pallas_call(
        bond_kernel,
        out_shape=jax.ShapeDtypeStruct((k // 64, rows, w * 64), BF16),
        grid=(k // tile,),
        in_specs=[
            pl.BlockSpec((w * rows, c), lambda i: (0, 0)),
            pl.BlockSpec((tile, c), lambda i: (i, 0)),
        ],
        out_specs=pl.BlockSpec((tile // 64, rows, w * 64), lambda i: (i, 0, 0)),
        compiler_params=pltpu.CompilerParams(vmem_limit_bytes=VMEM_LIMIT),
        cost_estimate=pl.CostEstimate(flops=2 * w * rows * c * k, bytes_accessed=12 << 20, transcendentals=0),
        name="bond_right",
    )(right_next.reshape(w * rows, c), bond)


def absorb_kernel(at_ref, m_ref, l_ref, *refs):
    blocks, o_ref, buffer, even_ref, odd_ref, sem = refs[:16], *refs[16:]
    tile, w = buffer.shape[-1], o_ref.shape[1]
    rows = l_ref.shape[0] // w
    i, last = pl.program_id(0), pl.num_programs(0) - 1

    def copies(step):
        slot = lax.rem(step, 2)
        return site_copies(at_ref, blocks, buffer.at[slot], sem.at[slot], step * tile, tile)

    @pl.when(i == 0)
    def _():
        for copy in copies(i):
            copy.start()

    @pl.when(i + 1 < last)
    def _():
        for copy in copies(i + 1):
            copy.start()

    @pl.when(i < last)
    def _():
        for copy in copies(i):
            copy.wait()

    def half(h_ref, slot):
        for t in range(2):
            site = buffer[slot, :, :, :, t].reshape(l_ref.shape[1], tile)
            h_ref[t] = dot(l_ref[...], site, ((1,), (0,)))

    def mix(h_ref):
        for v in range(w):
            sums = []
            for s in range(2):
                total = None
                for u in range(w):
                    for t in range(2):
                        term = m_ref[((u * w + v) * 2 + s) * 2 + t] * h_ref[t, u * rows : (u + 1) * rows, :]
                        total = term if total is None else total + term
                sums.append(total)
            turned = jnp.concatenate(sums, 0).T
            o_ref[:, v] = turned.reshape(tile // 64, 64, 2 * rows).astype(BF16)

    @pl.when(lax.rem(i, 2) == 0)
    def _():
        half(even_ref, 0)
        mix(odd_ref)

    @pl.when(lax.rem(i, 2) == 1)
    def _():
        half(odd_ref, 1)
        mix(even_ref)


def absorb(at, mpo, left, site):
    w, rows, k = left.shape
    columns = site[0].shape[-1]
    tile = 256
    scalars = pl.BlockSpec(memory_space=pltpu.SMEM)
    return pl.pallas_call(
        absorb_kernel,
        out_shape=jax.ShapeDtypeStruct((columns // 64, w, 64, 2 * rows), BF16),
        grid=(columns // tile + 1,),
        in_specs=[scalars, scalars, pl.BlockSpec((w * rows, k), lambda i: (0, 0))]
        + [pl.BlockSpec(memory_space=pl.ANY)] * 16,
        out_specs=pl.BlockSpec((tile // 64, w, 64, 2 * rows), lambda i: (jnp.maximum(i - 1, 0), 0, 0, 0)),
        scratch_shapes=[
            pltpu.VMEM((2, 4, 2, 4, 2, 64, tile), BF16),
            pltpu.VMEM((2, w * rows, tile), F32),
            pltpu.VMEM((2, w * rows, tile), F32),
            pltpu.SemaphoreType.DMA((2, 16)),
        ],
        compiler_params=pltpu.CompilerParams(vmem_limit_bytes=VMEM_LIMIT),
        cost_estimate=pl.CostEstimate(flops=4 * w * rows * k * columns, bytes_accessed=22 << 20, transcendentals=0),
        name="absorb",
    )(at, mpo.reshape(-1), left.reshape(w * rows, k), *site)


PIECES = (256, 256, 512, 512, 512)


def image_kernel(at_ref, c_ref, b_ref, *refs):
    blocks, e_ref, outs = refs[:16], refs[16], refs[17:27]
    buffer, lhs_ref, image_ref, sem, out_sem = refs[27:]
    parts, depth = c_ref.shape[0], c_ref.shape[2]
    tile = buffer.shape[-1]
    half = b_ref.shape[1] // 2
    i, count = pl.program_id(0), pl.num_programs(0)

    def copies(step):
        slot = lax.rem(step, 2)
        place = lax.rem(2 * at_ref[0] + step, count)
        return site_copies(at_ref, blocks, buffer.at[slot], sem.at[slot], place * tile, tile)

    def stores(step, static):
        slot = lax.rem(step, 2)
        src, done = image_ref.at[slot], out_sem.at[slot]
        place = lax.rem(2 * at_ref[0] + step, count)
        first = ((4, 0), (4, 256), (2, 0), (2, 256), (0, 0), (1, 0), (3, 0), (3, 256))[static]
        made = [pltpu.make_async_copy(src.at[0], outs[first[0]].at[pl.ds(first[1], tile)], done.at[0])]
        for piece, distance in ((2, 1), (3, 3), (4, 0)):
            rows = src.at[1, pl.ds(64 * lax.rem(at_ref[2] + distance, 4), 64)]
            made.append(pltpu.make_async_copy(rows, outs[5 + piece].at[place], done.at[piece]))
        far = src.at[1, pl.ds(64 * lax.rem(at_ref[2] + 2, 4), 64)]
        return made, far, place, done

    def each(step, act):
        for static in range(8):

            @pl.when(step == static)
            def _(static=static):
                made, far, place, done = stores(step, static)
                for copy in made:
                    act(copy)

                @pl.when(place < 4)
                def _():
                    act(pltpu.make_async_copy(far, outs[5].at[place], done.at[1]))

                @pl.when(place >= 4)
                def _():
                    act(pltpu.make_async_copy(far, outs[6].at[place - 4], done.at[1]))

    @pl.when(i == 0)
    def _():
        for copy in copies(i):
            copy.start()
        for p in range(parts):
            lhs_ref[:, depth * p : depth * (p + 1)] = c_ref[p]

    @pl.when(i + 1 < count)
    def _():
        for copy in copies(i + 1):
            copy.start()

    for copy in copies(i):
        copy.wait()

    slot = lax.rem(i, 2)
    env = dot(lhs_ref[...], buffer[slot].reshape(lhs_ref.shape[1], tile), ((1,), (0,)))
    e_ref[...] = env.astype(BF16)
    turned = env.T.astype(BF16)

    @pl.when(i >= 2)
    def _():
        each(i - 2, lambda copy: copy.wait())

    image_ref[slot, 0] = dot(turned, b_ref[:, :half], ((1,), (0,))).astype(BF16)
    image_ref[slot, 1] = dot(turned, b_ref[:, half:], ((1,), (0,))).astype(BF16)
    each(i, lambda copy: copy.start())

    @pl.when(i == count - 1)
    def _():
        each(i - 1, lambda copy: copy.wait())
        each(i, lambda copy: copy.wait())


def image(at, carried, site, bond):
    parts, rows, depth = carried.shape
    columns = site[0].shape[-1]
    tile, half = 256, columns // 2
    anywhere = pl.BlockSpec(memory_space=pl.ANY)
    grid = columns // tile
    return pl.pallas_call(
        image_kernel,
        out_shape=(
            jax.ShapeDtypeStruct((rows, columns), BF16),
            *(jax.ShapeDtypeStruct((n, half), BF16) for n in PIECES),
            *(jax.ShapeDtypeStruct((n // 64, 64, half), BF16) for n in PIECES),
        ),
        grid_spec=pltpu.PrefetchScalarGridSpec(
            num_scalar_prefetch=1,
            grid=(grid,),
            in_specs=[
                pl.BlockSpec((parts, rows, depth), lambda i, at: (0, 0, 0)),
                pl.BlockSpec(bond.shape, lambda i, at: (0, 0)),
            ]
            + [anywhere] * 16,
            out_specs=[pl.BlockSpec((rows, tile), lambda i, at: (0, lax.rem(2 * at[0] + i, grid)))] + [anywhere] * 10,
            scratch_shapes=[
                pltpu.VMEM((2, 4, 2, 4, 2, 64, tile), BF16),
                pltpu.VMEM((rows, parts * depth), BF16),
                pltpu.VMEM((2, 2, tile, half), BF16),
                pltpu.SemaphoreType.DMA((2, 16)),
                pltpu.SemaphoreType.DMA((2, 5)),
            ],
        ),
        compiler_params=pltpu.CompilerParams(vmem_limit_bytes=VMEM_LIMIT),
        cost_estimate=pl.CostEstimate(flops=2 * rows * columns * (parts * depth + columns), bytes_accessed=32 << 20, transcendentals=0),
        name="image",
    )(at, carried, bond, *site)


def add(*terms):
    total = terms[0].astype(F32)
    for term in terms[1:]:
        total = total + term.astype(F32)
    return total.astype(BF16)


def sum_line(far_low, far_high, right, left, own, axis):
    n = right.shape[0] // 2
    up, down = hop(far_low, axis, 1), hop(far_high, axis, -1)
    right_1, left_0 = hop(right[n:], axis, 1), hop(left[:n], axis, -1)
    right_0, left_1 = hop(add(right[:n], up), axis, 1), hop(add(left[n:], down), axis, -1)
    return jnp.concatenate([add(own[:n], right_0, left_0), add(own[n:], right_1, left_1)])


def sum_short(blocks, axis):
    own = lax.axis_index(axis)
    right, far, left, mine = (lax.dynamic_index_in_dim(blocks, (own + d) % 4, 0, keepdims=False) for d in (1, 2, 3, 0))
    return add(mine, hop(right, axis, 1), hop(left, axis, -1), hop(far, axis, 2))


def scatter_image(pieces):
    half = pieces[0].shape[-1]
    a = sum_line(*pieces[:5], "y")
    b = sum_line(*pieces[5:], "z")
    a = sum_short(a.reshape(2, 4, 64, half).transpose(1, 0, 2, 3), "z")
    b = sum_short(b.reshape(4, 2, 64, half), "y")
    both = jnp.concatenate([a, b], 2)
    own = lax.axis_index("x")
    theirs = hop(lax.dynamic_index_in_dim(both, 1 - own, 0, keepdims=False), "x", 1)
    return add(lax.dynamic_index_in_dim(both, own, 0, keepdims=False), theirs)


def local(env_left, site_tensor, mpo_tensor, env_right, bond_tensor):
    sector = ("y", "x", "z")
    at = jnp.stack([lax.axis_index(name) for name in sector]).astype(jnp.int32)
    route = [((i + 1) % 4, i) for i in range(4)]
    right_next = lax.ppermute(env_right, "region", route)[0]
    bond = bond_right(right_next, bond_tensor[0])
    site = gather_site(at, site_tensor[0].transpose(1, 0, 2))
    *site, bond = lax.optimization_barrier((*site, bond))
    bond = lax.all_to_all(bond, sector, split_axis=0, concat_axis=0, tiled=True)
    carried = absorb(at, mpo_tensor[0], env_left[0], site)
    carried = lax.all_to_all(carried, sector, split_axis=0, concat_axis=0, tiled=True)
    parts, w, columns, depth = carried.shape
    env_new, *pieces = image(
        at,
        carried.reshape(parts, w * columns, depth),
        site,
        bond.reshape(-1, bond.shape[-1]).T,
    )
    return (env_new.reshape(1, w, columns, -1), scatter_image(pieces)[None])


def solution(mesh):
    fine = Mesh(mesh.devices.reshape(4, 4, 2, 4), ("region", "y", "x", "z"))
    sector = ("y", "x", "z")
    return jax.shard_map(
        local,
        mesh=fine,
        in_specs=(
            P("region", None, sector, None),
            P("region", sector, None, None),
            P("region", None, None, None, None),
            P("region", None, sector, None),
            P("region", None, None),
        ),
        out_specs=(P("region", None, sector, None), P("region", sector, None)),
        check_vma=False,
    )
```

time: 605 us -> 336 us (0.56)
  waiting for transfers between devices: 418 us -> 159 us
  local copies, waits for them, and re-layouts: 100 us -> 11 us
  Pallas kernels: 0 us -> 72.3 us
  starting transfers between devices: 17.9 us -> 84 us
  matrix products: 51.1 us -> 0 us
  between operations: 14.1 us -> 1.04 us
    reduce_scatter x1 -> x0, waiting for transfers between devices: 229 us -> none  [local(): lax.psum_scatter(jnp.einsum('wka,wbk->ab', env_new, bond_moved, preferred...]
    all_gather x1 -> x0, waiting for transfers between devices: 127 us -> none  [absorb_side(): gathered = lax.all_gather(site_tensor, 'sector', axis=1, tiled=True)[0]]
    ppermute x1 -> x46, waiting for transfers between devices: 26.9 us -> 106 us  [the longest x45 106 us: hop(): lax.ppermute(block, axis, [(i, (i + distance) % n) for i in range(n)])]
    pallas_call x0 -> x4, Pallas kernels: none -> 72.3 us  [the longest x1 33.9 us: image(): pl.pallas_call(image_kernel, out_shape=(jax.ShapeDtypeStruct((rows, colum...]
    ppermute x1 -> x46, starting transfers between devices: 1.08 us -> 67.6 us  [the longest x45 67.6 us: hop(): lax.ppermute(block, axis, [(i, (i + distance) % n) for i in range(n)])]
    dot_general x5 -> x0, matrix products: 51.1 us -> none  [the longest x1 13.6 us: local(): jnp.einsum('wsac,asb->wcb', carried_moved, gathered, preferred_element_ty...]
    unnamed x7 -> x46, local copies, waits for them, and re-layouts: 42.8 us -> 4.47 us
    all_to_all x3 -> x0, local copies, waits for them, and re-layouts: 24.6 us -> none  [the longest x2 12.6 us: local(): lax.all_to_all(bond_right, 'sector', split_axis=2, concat_axis=1, tiled=T...]
  transfers between devices with their start and end apart: 5 -> 48, of which waited for: 4 -> 28; matrix products, arithmetic and copies ran while one was open for 14% -> 3% of each run, Pallas kernels for 0% -> 11%
where the time goes in v1:
time: 336 us; the launch traced here: 332 us
  waiting for transfers between devices  159 us (47%)
  starting transfers between devices  84 us (25%)
  Pallas kernels  72.3 us (22%)
  local copies, waits for them, and re-layouts  11 us (3%)
  other arithmetic  4.54 us (1%)
    ppermute x45, waiting for transfers between devices, hop(): lax.ppermute(block, axis, [(i, (i + distance) % n) for i in range(n)])  106 us
    ppermute x45, starting transfers between devices, hop(): lax.ppermute(block, axis, [(i, (i + distance) % n) for i in range(n)])  67.6 us
    all_to_all x1, waiting for transfers between devices, local(): lax.all_to_all(carried, sector, split_axis=0, concat_axis=0, tiled=True)  50.9 us
    pallas_call x1, Pallas kernels, image(): pl.pallas_call(image_kernel, out_shape=(jax.ShapeDtypeStruct((rows, colum...  33.9 us
    pallas_call x1, Pallas kernels, absorb(): pl.pallas_call(absorb_kernel, out_shape=jax.ShapeDtypeStruct((columns //...  25.5 us
    pallas_call x1, Pallas kernels, bond_right(): pl.pallas_call(bond_kernel, out_shape=jax.ShapeDtypeStruct((k // 64, rows...  11 us
    all_to_all x1, starting transfers between devices, local(): bond = lax.all_to_all(bond, sector, split_axis=0, concat_axis=0, tiled=True)  8.41 us
    all_to_all x1, starting transfers between devices, local(): lax.all_to_all(carried, sector, split_axis=0, concat_axis=0, tiled=True)  7.94 us
  transfers between devices with their start and end apart: 48, of which 28 were waited for; matrix products, arithmetic and copies ran while one was open for 3% of the time, Pallas kernels for 11%

profile of v1, /device:TPU:0, one launch (start us, length us, event | category | flops | bytes accessed | tf_op | source)
XLA Modules:
  0.0 331.5 jit_solution(17847351280296681889)
XLA Ops:
  1.9 3.2 collective-permute-start.10
  5.5 4.1 %collective-permute-start = (bf16[64,2048]{1,0:T(8,128)(2,1)S(1)}, bf16[64,2048]{1,0:T(8,128)(2,1)S(1)}, u32[]{:S(2)}, u32[]{:S(2)}) collective-permute-start(bf16[64,2048]{1,0:T(8,128)(2,1)S(1)} %get-tuple-element.77.refs_0_), channel_id=1, source_target_pairs={{0,3},{1,0},{2,1},{3,2},{4,7},{5,4},{6,5},{7,6},{8,11},{9,8},{10,9... | collective-permute-start | bytes 786440 | tf_op jit(solution)/shard_map/ppermute | solution.py:14
  9.6 3.0 collective-permute-start.7
  14.3 2.7 collective-permute-done.3.refs_4_
  17.0 1.8 collective-permute-start.12
  18.8 1.9 collective-permute-start.5
  20.7 1.7 collective-permute-start.11
  22.4 2.2 collective-permute-start.4
  24.6 2.0 collective-permute-start.1
  26.5 1.8 collective-permute-start.8
  30.0 1.7 collective-permute-done.4.refs_5_
  31.7 2.9 collective-permute-done.1.refs_2_
  37.2 2.0 collect.1
  39.3 2.3 collective-permute-start.14
  41.6 2.0 collective-permute-start.20
  43.6 17.7 %collective-permute-done.14.refs_1_ = bf16[4,64,2048]{2,1,0:T(8,128)(2,1)S(1)} collective-permute-done((bf16[4,64,2048]{2,1,0:T(8,128)(2,1)S(1)}, bf16[4,64,2048]{2,1,0:T(8,128)(2,1)S(1)}, u32[]{:S(2)}, u32[]{:S(2)}) %collective-permute-start.14) | collective-permute-done | bytes 1048608 | tf_op jit(solution)/shard_map/ppermute | solution.py:14
  62.3 5.0 %collective-permute-done.18.refs_7_ = bf16[4,64,2048]{2,1,0:T(8,128)(2,1)} collective-permute-done((bf16[4,64,2048]{2,1,0:T(8,128)(2,1)S(1)}, bf16[4,64,2048]{2,1,0:T(8,128)(2,1)}, u32[]{:S(2)}, u32[]{:S(2)}) %collective-permute-start.18) | collective-permute-done | bytes 1048608 | tf_op jit(solution)/shard_map/ppermute | solution.py:14
  67.3 3.6 %collective-permute-done.24.refs_15_ = bf16[4,64,2048]{2,1,0:T(8,128)(2,1)} collective-permute-done((bf16[4,64,2048]{2,1,0:T(8,128)(2,1)S(1)}, bf16[4,64,2048]{2,1,0:T(8,128)(2,1)}, u32[]{:S(2)}, u32[]{:S(2)}) %collective-permute-start.24) | collective-permute-done | bytes 1048608 | tf_op jit(solution)/shard_map/ppermute | solution.py:14
  70.9 16.1 %collective-permute-done.16.refs_3_ = bf16[4,64,2048]{2,1,0:T(8,128)(2,1)S(1)} collective-permute-done((bf16[4,64,2048]{2,1,0:T(8,128)(2,1)S(1)}, bf16[4,64,2048]{2,1,0:T(8,128)(2,1)S(1)}, u32[]{:S(2)}, u32[]{:S(2)}) %collective-permute-start.16) | collective-permute-done | bytes 1048608 | tf_op jit(solution)/shard_map/ppermute | solution.py:14
  87.0 2.1 collective-permute-start.19
  89.1 3.8 %collective-permute-done.22.refs_11_ = bf16[4,64,2048]{2,1,0:T(8,128)(2,1)S(1)} collective-permute-done((bf16[4,64,2048]{2,1,0:T(8,128)(2,1)S(1)}, bf16[4,64,2048]{2,1,0:T(8,128)(2,1)S(1)}, u32[]{:S(2)}, u32[]{:S(2)}) %collective-permute-start.22) | collective-permute-done | bytes 1048608 | tf_op jit(solution)/shard_map/ppermute | solution.py:14
  92.9 2.1 collective-permute-start.25
  95.0 11.0 %bond_right.1 = bf16[32,64,512]{2,1,0:T(8,128)(2,1)} custom-call(bf16[512,2048]{1,0:T(8,128)(2,1)} %bitcast.59, bf16[2048,2048]{1,0:T(8,128)(2,1)} %bitcast.57), custom_call_target="tpu_custom_call" | custom-call | flops 4294967296 | bytes 12582912 | tf_op jit(solution)/shard_map/bond_right/pallas_call | solution.py:102
  106.0 3.6 %collective-permute-done.15.refs_2_ = bf16[4,64,2048]{2,1,0:T(8,128)(2,1)S(1)} collective-permute-done((bf16[4,64,2048]{2,1,0:T(8,128)(2,1)S(1)}, bf16[4,64,2048]{2,1,0:T(8,128)(2,1)S(1)}, u32[]{:S(2)}, u32[]{:S(2)}) %collective-permute-start.15) | collective-permute-done | bytes 1048608 | tf_op jit(solution)/shard_map/ppermute | solution.py:14
  112.0 5.7 %collective-permute-done.21.refs_10_ = bf16[4,64,2048]{2,1,0:T(8,128)(2,1)S(1)} collective-permute-done((bf16[4,64,2048]{2,1,0:T(8,128)(2,1)}, bf16[4,64,2048]{2,1,0:T(8,128)(2,1)S(1)}, u32[]{:S(2)}, u32[]{:S(2)}) %collective-permute-start.21) | collective-permute-done | bytes 1048608 | tf_op jit(solution)/shard_map/ppermute | solution.py:14
  118.7 8.4 %all-to-all-start.1 = ((bf16[32,64,512]{2,1,0:T(8,128)(2,1)}), bf16[32,64,512]{2,1,0:T(8,128)(2,1)S(1)}, u32[]{:S(2)}, u32[]{:S(2)}) async-start(bf16[32,64,512]{2,1,0:T(8,128)(2,1)} %bond_right.1), calls=%async_computation.1 | async-start | bytes 4194304 | tf_op jit(solution)/shard_map/all_to_all | solution.py:351
  128.0 25.5 %absorb.1 = bf16[32,8,64,128]{3,2,1,0:T(8,128)(2,1)} custom-call(s32[3]{0:T(128)} %copy-done, f32[256]{0:T(256)} %reshape_squeeze.9.m_ref, bf16[512,2048]{1,0:T(8,128)(2,1)} %bitcast.58, bf16[4,64,2048]{2,1,0:T(8,128)(2,1)} %copy-done.1, bf16[4,64,2048]{2,1,0:T(8,128)(2,1)} %copy-done.14, bf16[4,64,2048]{2,1,0:T(8,128)(2,1)} %copy-done.18, ...), custom_call_target="tpu_custom_call" | custom-call | flops 8589934592 | bytes 23068672 | tf_op jit(solution)/shard_map/absorb/pallas_call | solution.py:176
  153.5 2.0 all-to-all-done.1
  155.5 7.9 %all-to-all-start = ((bf16[32,8,64,128]{3,2,1,0:T(8,128)(2,1)}), bf16[32,8,64,128]{3,2,1,0:T(8,128)(2,1)}, u32[]{:S(2)}, u32[]{:S(2)}) async-start(bf16[32,8,64,128]{3,2,1,0:T(8,128)(2,1)} %absorb.1), calls=%async_computation | async-start | bytes 8388608 | tf_op jit(solution)/shard_map/all_to_all | solution.py:353
  163.5 2.5 copy.12
  166.0 50.9 %all-to-all-done = bf16[32,8,64,128]{3,2,1,0:T(8,128)(2,1)} async-done(((bf16[32,8,64,128]{3,2,1,0:T(8,128)(2,1)}), bf16[32,8,64,128]{3,2,1,0:T(8,128)(2,1)}, u32[]{:S(2)}, u32[]{:S(2)}) %all-to-all-start) | async-done | bytes 4194336 | tf_op jit(solution)/shard_map/all_to_all | solution.py:353
  216.9 33.9 %image.1 = (bf16[512,2048]{1,0:T(8,128)(2,1)}, bf16[256,1024]{1,0:T(8,128)(2,1)}, bf16[256,1024]{1,0:T(8,128)(2,1)}, bf16[512,1024]{1,0:T(8,128)(2,1)}, bf16[512...) custom-call(s32[3]{0:T(128)} %copy-done, ...), custom_call_target="tpu_custom_call" | custom-call | flops 12884901888 | bytes 33554432 | tf_op jit(solution)/shard_map/image/pallas_call | solution.py:280
  250.8 3.6 %collective-permute-start.40 = (bf16[4,64,1024]{2,1,0:T(8,128)(2,1)}, bf16[4,64,1024]{2,1,0:T(8,128)(2,1)S(1)}, u32[]{:S(2)}, u32[]{:S(2)}) collective-permute-start(bf16[4,64,1024]{2,1,0:T(8,128)(2,1)} %get-tuple-element.65), channel_id=1, source_target_pairs={{0,3},{1,0},{2,1},{3,2},{4,7},{5,4},{6,5},{7,6},{8,11},{9,8},{10,9... | collective-permute-start | bytes 1572872 | tf_op jit(solution)/shard_map/ppermute | solution.py:14
  255.6 3.3 collective-permute-start.38
  261.4 5.7 %collective-permute-done.40 = bf16[4,64,1024]{2,1,0:T(8,128)(2,1)S(1)} collective-permute-done((bf16[4,64,1024]{2,1,0:T(8,128)(2,1)}, bf16[4,64,1024]{2,1,0:T(8,128)(2,1)S(1)}, u32[]{:S(2)}, u32[]{:S(2)}) %collective-permute-start.40) | collective-permute-done | bytes 524320 | tf_op jit(solution)/shard_map/ppermute | solution.py:14
  267.8 2.8 collective-permute-done.36
  273.2 4.3 %collective-permute-done.27 = bf16[256,1024]{1,0:T(8,128)(2,1)S(1)} collective-permute-done((bf16[256,1024]{1,0:T(8,128)(2,1)S(1)}, bf16[256,1024]{1,0:T(8,128)(2,1)S(1)}, u32[]{:S(2)}, u32[]{:S(2)}) %collective-permute-start.27) | collective-permute-done | bytes 524320 | tf_op jit(solution)/shard_map/ppermute | solution.py:14
  279.8 2.1 collective-permute-done.39
  284.2 2.3 collective-permute-start.28
  288.5 3.5 %collective-permute-done.29 = bf16[256,1024]{1,0:T(8,128)(2,1)S(1)} collective-permute-done((bf16[256,1024]{1,0:T(8,128)(2,1)S(1)}, bf16[256,1024]{1,0:T(8,128)(2,1)S(1)}, u32[]{:S(2)}, u32[]{:S(2)}) %collective-permute-start.29) | collective-permute-done | bytes 524320 | tf_op jit(solution)/shard_map/ppermute | solution.py:14
  292.0 3.0 collective-permute-start.43
  295.1 7.4 %collective-permute-done.32 = bf16[256,1024]{1,0:T(8,128)(2,1)S(1)} collective-permute-done((bf16[256,1024]{1,0:T(8,128)(2,1)S(1)}, bf16[256,1024]{1,0:T(8,128)(2,1)S(1)}, u32[]{:S(2)}, u32[]{:S(2)}) %collective-permute-start.32) | collective-permute-done | bytes 524320 | tf_op jit(solution)/shard_map/ppermute | solution.py:14
  304.2 6.0 %collective-permute-start.33 = (bf16[2,64,1024]{2,1,0:T(8,128)(2,1)}, bf16[2,64,1024]{2,1,0:T(8,128)(2,1)}, u32[]{:S(2)}, u32[]{:S(2)}) collective-permute-start(bf16[2,64,1024]{2,1,0:T(8,128)(2,1)} %get-tuple-element.71), channel_id=1, source_target_pairs={{0,1},{1,2},{2,3},{3,0},{4,5},{5,6},{6,7},{7,4},{8,9},{9,10},{10,1... | collective-permute-start | bytes 786440 | tf_op jit(solution)/shard_map/ppermute | solution.py:14
  310.2 1.8 collective-permute-start.34
  313.7 3.0 collective-permute-done.33
  316.9 4.0 %collective-permute-done.35 = bf16[2,64,1024]{2,1,0:T(8,128)(2,1)} collective-permute-done((bf16[2,64,1024]{2,1,0:T(8,128)(2,1)}, bf16[2,64,1024]{2,1,0:T(8,128)(2,1)}, u32[]{:S(2)}, u32[]{:S(2)}) %collective-permute-start.35) | collective-permute-done | bytes 262176 | tf_op jit(solution)/shard_map/ppermute | solution.py:14
  322.3 4.1 %collective-permute-start.45 = (bf16[64,2048]{1,0:T(8,128)(2,1)S(1)}, bf16[64,2048]{1,0:T(8,128)(2,1)S(1)}, u32[]{:S(2)}, u32[]{:S(2)}) collective-permute-start(bf16[64,2048]{1,0:T(8,128)(2,1)S(1)} %fusion.9), channel_id=1, source_target_pairs={{0,4},{4,0},{1,5},{5,1},{2,6},{6,2},{3,7},{7,3},{8,12},{12,8},{9,1... | collective-permute-start | bytes 786440 | tf_op jit(solution)/shard_map/ppermute | solution.py:14
  326.4 4.4 %collective-permute-done.45 = bf16[64,2048]{1,0:T(8,128)(2,1)S(1)} collective-permute-done((bf16[64,2048]{1,0:T(8,128)(2,1)S(1)}, bf16[64,2048]{1,0:T(8,128)(2,1)S(1)}, u32[]{:S(2)}, u32[]{:S(2)}) %collective-permute-start.45) | collective-permute-done | bytes 262176 | tf_op jit(solution)/shard_map/ppermute | solution.py:14
  (120 shorter events, 32.3 us)
Async XLA Ops:
  1.9 10.8 %collective-permute-start.10 = (bf16[64,2048]{1,0:T(8,128)(2,1)S(1)}, bf16[64,2048]{1,0:T(8,128)(2,1)S(1)}, u32[]{:S(2)}, u32[]{:S(2)}) collective-permute-start(bf16[64,2048]{1,0:T(8,128)(2,1)S(1)} %get-tuple-element.76.refs_8_), channel_id=1, source_target_pairs={{0,4},{4,0},{1,5},{5,1},{2,6},{6,2},{3,7},{7,3},{8,12},{12,8},{9,1... | collective-permute-start | bytes 786440 | tf_op jit(solution)/shard_map/ppermute | solution.py:14
  5.1 11.9 %collective-permute-start.3 = (bf16[64,2048]{1,0:T(8,128)(2,1)S(1)}, bf16[64,2048]{1,0:T(8,128)(2,1)S(1)}, u32[]{:S(2)}, u32[]{:S(2)}) collective-permute-start(bf16[64,2048]{1,0:T(8,128)(2,1)S(1)} %get-tuple-element.77.refs_0_), channel_id=1, source_target_pairs={{0,4},{4,0},{1,5},{5,1},{2,6},{6,2},{3,7},{7,3},{8,12},{12,8},{9,1... | collective-permute-start | bytes 786440 | tf_op jit(solution)/shard_map/ppermute | solution.py:14
  5.5 13.3 %collective-permute-start = (bf16[64,2048]{1,0:T(8,128)(2,1)S(1)}, bf16[64,2048]{1,0:T(8,128)(2,1)S(1)}, u32[]{:S(2)}, u32[]{:S(2)}) collective-permute-start(bf16[64,2048]{1,0:T(8,128)(2,1)S(1)} %get-tuple-element.77.refs_0_), channel_id=1, source_target_pairs={{0,3},{1,0},{2,1},{3,2},{4,7},{5,4},{6,5},{7,6},{8,11},{9,8},{10,9... | collective-permute-start | bytes 786440 | tf_op jit(solution)/shard_map/ppermute | solution.py:14
  9.6 11.1 %collective-permute-start.7 = (bf16[64,2048]{1,0:T(8,128)(2,1)S(1)}, bf16[64,2048]{1,0:T(8,128)(2,1)S(1)}, u32[]{:S(2)}, u32[]{:S(2)}) collective-permute-start(bf16[64,2048]{1,0:T(8,128)(2,1)S(1)} %get-tuple-element.76.refs_8_), channel_id=1, source_target_pairs={{0,24},{8,0},{16,8},{24,16},{1,25},{9,1},{17,9},{25,17},{2,26},{10... | collective-permute-start | bytes 786440 | tf_op jit(solution)/shard_map/ppermute | solution.py:14
  12.6 9.8 %collective-permute-start.2 = (bf16[64,2048]{1,0:T(8,128)(2,1)S(1)}, bf16[64,2048]{1,0:T(8,128)(2,1)S(1)}, u32[]{:S(2)}, u32[]{:S(2)}) collective-permute-start(bf16[64,2048]{1,0:T(8,128)(2,1)S(1)} %get-tuple-element.77.refs_0_), channel_id=1, source_target_pairs={{0,1},{1,2},{2,3},{3,0},{4,5},{5,6},{6,7},{7,4},{8,9},{9,10},{10,1... | collective-permute-start | bytes 786440 | tf_op jit(solution)/shard_map/ppermute | solution.py:14
  12.7 11.9 %collective-permute-start.9 = (bf16[64,2048]{1,0:T(8,128)(2,1)S(1)}, bf16[64,2048]{1,0:T(8,128)(2,1)S(1)}, u32[]{:S(2)}, u32[]{:S(2)}) collective-permute-start(bf16[64,2048]{1,0:T(8,128)(2,1)S(1)} %get-tuple-element.76.refs_8_), channel_id=1, source_target_pairs={{0,8},{8,16},{16,24},{24,0},{1,9},{9,17},{17,25},{25,1},{2,10},{10... | collective-permute-start | bytes 786440 | tf_op jit(solution)/shard_map/ppermute | solution.py:14
  17.0 9.5 %collective-permute-start.12 = (bf16[64,2048]{1,0:T(8,128)(2,1)S(1)}, bf16[64,2048]{1,0:T(8,128)(2,1)S(1)}, u32[]{:S(2)}, u32[]{:S(2)}) collective-permute-start(bf16[64,2048]{1,0:T(8,128)(2,1)S(1)} %collective-permute-done.10.refs_12_), channel_id=1, source_target_pairs={{0,8},{8,16},{16,24},{24,0},{1,9},{9,17},{17,25},{25,1},{2,10},{10... | collective-permute-start | bytes 786440 | tf_op jit(solution)/shard_map/ppermute | solution.py:14
  18.8 9.5 %collective-permute-start.5 = (bf16[64,2048]{1,0:T(8,128)(2,1)S(1)}, bf16[64,2048]{1,0:T(8,128)(2,1)S(1)}, u32[]{:S(2)}, u32[]{:S(2)}) collective-permute-start(bf16[64,2048]{1,0:T(8,128)(2,1)S(1)} %collective-permute-done.3.refs_4_), channel_id=1, source_target_pairs={{0,1},{1,2},{2,3},{3,0},{4,5},{5,6},{6,7},{7,4},{8,9},{9,10},{10,1... | collective-permute-start | bytes 786440 | tf_op jit(solution)/shard_map/ppermute | solution.py:14
  20.7 8.8 %collective-permute-start.11 = (bf16[64,2048]{1,0:T(8,128)(2,1)S(1)}, bf16[64,2048]{1,0:T(8,128)(2,1)S(1)}, u32[]{:S(2)}, u32[]{:S(2)}) collective-permute-start(bf16[64,2048]{1,0:T(8,128)(2,1)S(1)} %collective-permute-done.10.refs_12_), channel_id=1, source_target_pairs={{0,24},{8,0},{16,8},{24,16},{1,25},{9,1},{17,9},{25,17},{2,26},{10... | collective-permute-start | bytes 786440 | tf_op jit(solution)/shard_map/ppermute | solution.py:14
  22.4 9.3 %collective-permute-start.4 = (bf16[64,2048]{1,0:T(8,128)(2,1)S(1)}, bf16[64,2048]{1,0:T(8,128)(2,1)S(1)}, u32[]{:S(2)}, u32[]{:S(2)}) collective-permute-start(bf16[64,2048]{1,0:T(8,128)(2,1)S(1)} %collective-permute-done.3.refs_4_), channel_id=1, source_target_pairs={{0,3},{1,0},{2,1},{3,2},{4,7},{5,4},{6,5},{7,6},{8,11},{9,8},{10,9... | collective-permute-start | bytes 786440 | tf_op jit(solution)/shard_map/ppermute | solution.py:14
  24.6 10.0 %collective-permute-start.1 = (bf16[64,2048]{1,0:T(8,128)(2,1)S(1)}, bf16[64,2048]{1,0:T(8,128)(2,1)S(1)}, u32[]{:S(2)}, u32[]{:S(2)}) collective-permute-start(bf16[64,2048]{1,0:T(8,128)(2,1)S(1)} %collective-permute-done.refs_1_), channel_id=1, source_target_pairs={{0,3},{1,0},{2,1},{3,2},{4,7},{5,4},{6,5},{7,6},{8,11},{9,8},{10,9... | collective-permute-start | bytes 786440 | tf_op jit(solution)/shard_map/ppermute | solution.py:14
  26.5 8.0 %collective-permute-start.8 = (bf16[64,2048]{1,0:T(8,128)(2,1)S(1)}, bf16[64,2048]{1,0:T(8,128)(2,1)}, u32[]{:S(2)}, u32[]{:S(2)}) collective-permute-start(bf16[64,2048]{1,0:T(8,128)(2,1)S(1)} %collective-permute-done.7.refs_9_), channel_id=1, source_target_pairs={{0,24},{8,0},{16,8},{24,16},{1,25},{9,1},{17,9},{25,17},{2,26},{10... | collective-permute-start | bytes 786440 | tf_op jit(solution)/shard_map/ppermute | solution.py:14
  28.3 7.7 %collective-permute-start.13 = (bf16[64,2048]{1,0:T(8,128)(2,1)S(1)}, bf16[64,2048]{1,0:T(8,128)(2,1)}, u32[]{:S(2)}, u32[]{:S(2)}) collective-permute-start(bf16[64,2048]{1,0:T(8,128)(2,1)S(1)} %collective-permute-done.12.refs_15_), channel_id=1, source_target_pairs={{0,8},{8,16},{16,24},{24,0},{1,9},{9,17},{17,25},{25,1},{2,10},{10... | collective-permute-start | bytes 786440 | tf_op jit(solution)/shard_map/ppermute | solution.py:14
  29.6 7.7 %collective-permute-start.6 = (bf16[64,2048]{1,0:T(8,128)(2,1)S(1)}, bf16[64,2048]{1,0:T(8,128)(2,1)}, u32[]{:S(2)}, u32[]{:S(2)}) collective-permute-start(bf16[64,2048]{1,0:T(8,128)(2,1)S(1)} %collective-permute-done.5.refs_7_), channel_id=1, source_target_pairs={{0,1},{1,2},{2,3},{3,0},{4,5},{5,6},{6,7},{7,4},{8,9},{9,10},{10,1... | collective-permute-start | bytes 786440 | tf_op jit(solution)/shard_map/ppermute | solution.py:14
  39.3 22.0 %collective-permute-start.14 = (bf16[4,64,2048]{2,1,0:T(8,128)(2,1)S(1)}, bf16[4,64,2048]{2,1,0:T(8,128)(2,1)S(1)}, u32[]{:S(2)}, u32[]{:S(2)}) collective-permute-start(bf16[4,64,2048]{2,1,0:T(8,128)(2,1)S(1)} %get-tuple-element.38.refs_0_), channel_id=1, source_target_pairs={{0,24},{8,0},{16,8},{24,16},{1,25},{9,1},{17,9},{25,17},{2,26},{10... | collective-permute-start | bytes 3145736 | tf_op jit(solution)/shard_map/ppermute | solution.py:14
  41.6 25.7 %collective-permute-start.18 = (bf16[4,64,2048]{2,1,0:T(8,128)(2,1)S(1)}, bf16[4,64,2048]{2,1,0:T(8,128)(2,1)}, u32[]{:S(2)}, u32[]{:S(2)}) collective-permute-start(bf16[4,64,2048]{2,1,0:T(8,128)(2,1)S(1)} %get-tuple-element.42.refs_4_), channel_id=1, source_target_pairs={{0,8},{8,16},{16,24},{24,0},{1,9},{9,17},{17,25},{25,1},{2,10},{10... | collective-permute-start | bytes 3145736 | tf_op jit(solution)/shard_map/ppermute | solution.py:14
  41.6 25.7 %collective-permute-start.20 = (bf16[4,64,2048]{2,1,0:T(8,128)(2,1)S(1)}, bf16[4,64,2048]{2,1,0:T(8,128)(2,1)}, u32[]{:S(2)}, u32[]{:S(2)}) collective-permute-start(bf16[4,64,2048]{2,1,0:T(8,128)(2,1)S(1)} %get-tuple-element.46.refs_8_), channel_id=1, source_target_pairs={{0,3},{1,0},{2,1},{3,2},{4,7},{5,4},{6,5},{7,6},{8,11},{9,8},{10,9... | collective-permute-start | bytes 3145736 | tf_op jit(solution)/shard_map/ppermute | solution.py:14
  43.6 49.3 %collective-permute-start.26 = (bf16[1,8,64,2048]{3,2,1,0:T(8,128)(2,1)S(1)}, bf16[1,8,64,2048]{3,2,1,0:T(8,128)(2,1)S(1)}, u32[]{:S(2)}, u32[]{:S(2)}) collective-permute-start(bf16[1,8,64,2048]{3,2,1,0:T(8,128)(2,1)S(1)} %copy-done.12), channel_id=1, source_target_pairs={{32,0},{64,32},{96,64},{0,96},{33,1},{65,33},{97,65},{1,97},{34,2}... | collective-permute-start | bytes 6291464 | tf_op jit(solution)/shard_map/ppermute | solution.py:347
  43.6 27.3 %collective-permute-start.24 = (bf16[4,64,2048]{2,1,0:T(8,128)(2,1)S(1)}, bf16[4,64,2048]{2,1,0:T(8,128)(2,1)}, u32[]{:S(2)}, u32[]{:S(2)}) collective-permute-start(bf16[4,64,2048]{2,1,0:T(8,128)(2,1)S(1)} %get-tuple-element.50.refs_12_), channel_id=1, source_target_pairs={{0,1},{1,2},{2,3},{3,0},{4,5},{5,6},{6,7},{7,4},{8,9},{9,10},{10,1... | collective-permute-start | bytes 3145736 | tf_op jit(solution)/shard_map/ppermute | solution.py:14
  61.3 25.7 %collective-permute-start.16 = (bf16[4,64,2048]{2,1,0:T(8,128)(2,1)S(1)}, bf16[4,64,2048]{2,1,0:T(8,128)(2,1)S(1)}, u32[]{:S(2)}, u32[]{:S(2)}) collective-permute-start(bf16[4,64,2048]{2,1,0:T(8,128)(2,1)S(1)} %get-tuple-element.38.refs_0_), channel_id=1, source_target_pairs={{0,8},{8,16},{16,24},{24,0},{1,9},{9,17},{17,25},{25,1},{2,10},{10... | collective-permute-start | bytes 3145736 | tf_op jit(solution)/shard_map/ppermute | solution.py:14
  67.3 19.7 %collective-permute-start.17 = (bf16[4,64,2048]{2,1,0:T(8,128)(2,1)S(1)}, bf16[4,64,2048]{2,1,0:T(8,128)(2,1)S(1)}, u32[]{:S(2)}, u32[]{:S(2)}) collective-permute-start(bf16[4,64,2048]{2,1,0:T(8,128)(2,1)S(1)} %get-tuple-element.42.refs_4_), channel_id=1, source_target_pairs={{0,24},{8,0},{16,8},{24,16},{1,25},{9,1},{17,9},{25,17},{2,26},{10... | collective-permute-start | bytes 3145736 | tf_op jit(solution)/shard_map/ppermute | solution.py:14
  67.3 25.6 %collective-permute-start.22 = (bf16[4,64,2048]{2,1,0:T(8,128)(2,1)S(1)}, bf16[4,64,2048]{2,1,0:T(8,128)(2,1)S(1)}, u32[]{:S(2)}, u32[]{:S(2)}) collective-permute-start(bf16[4,64,2048]{2,1,0:T(8,128)(2,1)S(1)} %get-tuple-element.46.refs_8_), channel_id=1, source_target_pairs={{0,1},{1,2},{2,3},{3,0},{4,5},{5,6},{6,7},{7,4},{8,9},{9,10},{10,1... | collective-permute-start | bytes 3145736 | tf_op jit(solution)/shard_map/ppermute | solution.py:14
  70.9 35.1 %collective-permute-start.23 = (bf16[4,64,2048]{2,1,0:T(8,128)(2,1)S(1)}, bf16[4,64,2048]{2,1,0:T(8,128)(2,1)}, u32[]{:S(2)}, u32[]{:S(2)}) collective-permute-start(bf16[4,64,2048]{2,1,0:T(8,128)(2,1)S(1)} %get-tuple-element.50.refs_12_), channel_id=1, source_target_pairs={{0,3},{1,0},{2,1},{3,2},{4,7},{5,4},{6,5},{7,6},{8,11},{9,8},{10,9... | collective-permute-start | bytes 3145736 | tf_op jit(solution)/shard_map/ppermute | solution.py:14
  87.0 22.5 %collective-permute-start.15 = (bf16[4,64,2048]{2,1,0:T(8,128)(2,1)S(1)}, bf16[4,64,2048]{2,1,0:T(8,128)(2,1)S(1)}, u32[]{:S(2)}, u32[]{:S(2)}) collective-permute-start(bf16[4,64,2048]{2,1,0:T(8,128)(2,1)S(1)} %collective-permute-done.14.refs_1_), channel_id=1, source_target_pairs={{0,24},{8,0},{16,8},{24,16},{1,25},{9,1},{17,9},{25,17},{2,26},{10... | collective-permute-start | bytes 3145736 | tf_op jit(solution)/shard_map/ppermute | solution.py:14
  87.0 24.0 %collective-permute-start.19 = (bf16[4,64,2048]{2,1,0:T(8,128)(2,1)}, bf16[4,64,2048]{2,1,0:T(8,128)(2,1)S(1)}, u32[]{:S(2)}, u32[]{:S(2)}) collective-permute-start(bf16[4,64,2048]{2,1,0:T(8,128)(2,1)} %collective-permute-done.18.refs_7_), channel_id=1, source_target_pairs={{0,8},{8,16},{16,24},{24,0},{1,9},{9,17},{17,25},{25,1},{2,10},{10... | collective-permute-start | bytes 3145736 | tf_op jit(solution)/shard_map/ppermute | solution.py:14
  92.8 24.9 %collective-permute-start.21 = (bf16[4,64,2048]{2,1,0:T(8,128)(2,1)}, bf16[4,64,2048]{2,1,0:T(8,128)(2,1)S(1)}, u32[]{:S(2)}, u32[]{:S(2)}) collective-permute-start(bf16[4,64,2048]{2,1,0:T(8,128)(2,1)} %collective-permute-done.20.refs_9_), channel_id=1, source_target_pairs={{0,3},{1,0},{2,1},{3,2},{4,7},{5,4},{6,5},{7,6},{8,11},{9,8},{10,9... | collective-permute-start | bytes 3145736 | tf_op jit(solution)/shard_map/ppermute | solution.py:14
  92.9 25.8 %collective-permute-start.25 = (bf16[4,64,2048]{2,1,0:T(8,128)(2,1)}, bf16[4,64,2048]{2,1,0:T(8,128)(2,1)}, u32[]{:S(2)}, u32[]{:S(2)}) collective-permute-start(bf16[4,64,2048]{2,1,0:T(8,128)(2,1)} %collective-permute-done.24.refs_15_), channel_id=1, source_target_pairs={{0,1},{1,2},{2,3},{3,0},{4,5},{5,6},{6,7},{7,4},{8,9},{9,10},{10,1... | collective-permute-start | bytes 3145736 | tf_op jit(solution)/shard_map/ppermute | solution.py:14
  118.7 36.8 %all-to-all-start.1 = ((bf16[32,64,512]{2,1,0:T(8,128)(2,1)}), bf16[32,64,512]{2,1,0:T(8,128)(2,1)S(1)}, u32[]{:S(2)}, u32[]{:S(2)}) async-start(bf16[32,64,512]{2,1,0:T(8,128)(2,1)} %bond_right.1), calls=%async_computation.1 | async-start | bytes 4194304 | tf_op jit(solution)/shard_map/all_to_all | solution.py:351
  155.5 61.3 %all-to-all-start = ((bf16[32,8,64,128]{3,2,1,0:T(8,128)(2,1)}), bf16[32,8,64,128]{3,2,1,0:T(8,128)(2,1)}, u32[]{:S(2)}, u32[]{:S(2)}) async-start(bf16[32,8,64,128]{3,2,1,0:T(8,128)(2,1)} %absorb.1), calls=%async_computation | async-start | bytes 8388608 | tf_op jit(solution)/shard_map/all_to_all | solution.py:353
  250.8 16.3 %collective-permute-start.40 = (bf16[4,64,1024]{2,1,0:T(8,128)(2,1)}, bf16[4,64,1024]{2,1,0:T(8,128)(2,1)S(1)}, u32[]{:S(2)}, u32[]{:S(2)}) collective-permute-start(bf16[4,64,1024]{2,1,0:T(8,128)(2,1)} %get-tuple-element.65), channel_id=1, source_target_pairs={{0,3},{1,0},{2,1},{3,2},{4,7},{5,4},{6,5},{7,6},{8,11},{9,8},{10,9... | collective-permute-start | bytes 1572872 | tf_op jit(solution)/shard_map/ppermute | solution.py:14
  254.4 16.3 %collective-permute-start.36 = (bf16[4,64,1024]{2,1,0:T(8,128)(2,1)}, bf16[4,64,1024]{2,1,0:T(8,128)(2,1)S(1)}, u32[]{:S(2)}, u32[]{:S(2)}) collective-permute-start(bf16[4,64,1024]{2,1,0:T(8,128)(2,1)} %get-tuple-element.63), channel_id=1, source_target_pairs={{0,1},{1,2},{2,3},{3,0},{4,5},{5,6},{6,7},{7,4},{8,9},{9,10},{10,1... | collective-permute-start | bytes 1572872 | tf_op jit(solution)/shard_map/ppermute | solution.py:14
  255.6 23.6 %collective-permute-start.38 = (bf16[4,64,1024]{2,1,0:T(8,128)(2,1)S(1)}, bf16[4,64,1024]{2,1,0:T(8,128)(2,1)S(1)}, u32[]{:S(2)}, u32[]{:S(2)}) collective-permute-start(bf16[4,64,1024]{2,1,0:T(8,128)(2,1)S(1)} %slice.52), channel_id=1, source_target_pairs={{0,3},{1,0},{2,1},{3,2},{4,7},{5,4},{6,5},{7,6},{8,11},{9,8},{10,9... | collective-permute-start | bytes 1572872 | tf_op jit(solution)/shard_map/ppermute | solution.py:14
  260.0 21.9 %collective-permute-start.39 = (bf16[4,64,1024]{2,1,0:T(8,128)(2,1)S(1)}, bf16[4,64,1024]{2,1,0:T(8,128)(2,1)S(1)}, u32[]{:S(2)}, u32[]{:S(2)}) collective-permute-start(bf16[4,64,1024]{2,1,0:T(8,128)(2,1)S(1)} %slice.54), channel_id=1, source_target_pairs={{0,1},{1,2},{2,3},{3,0},{4,5},{5,6},{6,7},{7,4},{8,9},{9,10},{10,1... | collective-permute-start | bytes 1572872 | tf_op jit(solution)/shard_map/ppermute | solution.py:14
  260.1 11.3 %collective-permute-start.31 = (bf16[256,1024]{1,0:T(8,128)(2,1)}, bf16[256,1024]{1,0:T(8,128)(2,1)S(1)}, u32[]{:S(2)}, u32[]{:S(2)}) collective-permute-start(bf16[256,1024]{1,0:T(8,128)(2,1)} %get-tuple-element.60), channel_id=1, source_target_pairs={{0,24},{8,0},{16,8},{24,16},{1,25},{9,1},{17,9},{25,17},{2,26},{10... | collective-permute-start | bytes 1572872 | tf_op jit(solution)/shard_map/ppermute | solution.py:14
  267.1 10.4 %collective-permute-start.27 = (bf16[256,1024]{1,0:T(8,128)(2,1)S(1)}, bf16[256,1024]{1,0:T(8,128)(2,1)S(1)}, u32[]{:S(2)}, u32[]{:S(2)}) collective-permute-start(bf16[256,1024]{1,0:T(8,128)(2,1)S(1)} %copy-done.21), channel_id=1, source_target_pairs={{0,8},{8,16},{16,24},{24,0},{1,9},{9,17},{17,25},{25,1},{2,10},{10... | collective-permute-start | bytes 1572872 | tf_op jit(solution)/shard_map/ppermute | solution.py:14
  270.7 13.5 %collective-permute-start.41 = (bf16[4,64,1024]{2,1,0:T(8,128)(2,1)S(1)}, bf16[4,64,1024]{2,1,0:T(8,128)(2,1)S(1)}, u32[]{:S(2)}, u32[]{:S(2)}) collective-permute-start(bf16[4,64,1024]{2,1,0:T(8,128)(2,1)S(1)} %add_convert_fusion.1), channel_id=1, source_target_pairs={{0,3},{1,0},{2,1},{3,2},{4,7},{5,4},{6,5},{7,6},{8,11},{9,8},{10,9... | collective-permute-start | bytes 1572872 | tf_op jit(solution)/shard_map/ppermute | solution.py:14
  271.4 16.2 %collective-permute-start.37 = (bf16[4,64,1024]{2,1,0:T(8,128)(2,1)S(1)}, bf16[4,64,1024]{2,1,0:T(8,128)(2,1)S(1)}, u32[]{:S(2)}, u32[]{:S(2)}) collective-permute-start(bf16[4,64,1024]{2,1,0:T(8,128)(2,1)S(1)} %add_convert_fusion.3), channel_id=1, source_target_pairs={{0,1},{1,2},{2,3},{3,0},{4,5},{5,6},{6,7},{7,4},{8,9},{9,10},{10,1... | collective-permute-start | bytes 1572872 | tf_op jit(solution)/shard_map/ppermute | solution.py:14
  277.5 14.6 %collective-permute-start.29 = (bf16[256,1024]{1,0:T(8,128)(2,1)S(1)}, bf16[256,1024]{1,0:T(8,128)(2,1)S(1)}, u32[]{:S(2)}, u32[]{:S(2)}) collective-permute-start(bf16[256,1024]{1,0:T(8,128)(2,1)S(1)} %slice.46), channel_id=1, source_target_pairs={{0,24},{8,0},{16,8},{24,16},{1,25},{9,1},{17,9},{25,17},{2,26},{10... | collective-permute-start | bytes 1572872 | tf_op jit(solution)/shard_map/ppermute | solution.py:14
  279.2 15.9 %collective-permute-start.30 = (bf16[256,1024]{1,0:T(8,128)(2,1)S(1)}, bf16[256,1024]{1,0:T(8,128)(2,1)S(1)}, u32[]{:S(2)}, u32[]{:S(2)}) collective-permute-start(bf16[256,1024]{1,0:T(8,128)(2,1)S(1)} %slice.48), channel_id=1, source_target_pairs={{0,8},{8,16},{16,24},{24,0},{1,9},{9,17},{17,25},{25,1},{2,10},{10... | collective-permute-start | bytes 1572872 | tf_op jit(solution)/shard_map/ppermute | solution.py:14
  281.9 20.5 %collective-permute-start.32 = (bf16[256,1024]{1,0:T(8,128)(2,1)S(1)}, bf16[256,1024]{1,0:T(8,128)(2,1)S(1)}, u32[]{:S(2)}, u32[]{:S(2)}) collective-permute-start(bf16[256,1024]{1,0:T(8,128)(2,1)S(1)} %add_convert_fusion.5), channel_id=1, source_target_pairs={{0,24},{8,0},{16,8},{24,16},{1,25},{9,1},{17,9},{25,17},{2,26},{10... | collective-permute-start | bytes 1572872 | tf_op jit(solution)/shard_map/ppermute | solution.py:14
  284.2 18.4 %collective-permute-start.28 = (bf16[256,1024]{1,0:T(8,128)(2,1)S(1)}, bf16[256,1024]{1,0:T(8,128)(2,1)S(1)}, u32[]{:S(2)}, u32[]{:S(2)}) collective-permute-start(bf16[256,1024]{1,0:T(8,128)(2,1)S(1)} %add_convert_fusion.7), channel_id=1, source_target_pairs={{0,8},{8,16},{16,24},{24,0},{1,9},{9,17},{17,25},{25,1},{2,10},{10... | collective-permute-start | bytes 1572872 | tf_op jit(solution)/shard_map/ppermute | solution.py:14
  288.4 23.6 %collective-permute-start.42 = (bf16[2,64,1024]{2,1,0:T(8,128)(2,1)S(1)}, bf16[2,64,1024]{2,1,0:T(8,128)(2,1)S(1)}, u32[]{:S(2)}, u32[]{:S(2)}) collective-permute-start(bf16[2,64,1024]{2,1,0:T(8,128)(2,1)S(1)} %get-tuple-element.66), channel_id=1, source_target_pairs={{0,8},{8,16},{16,24},{24,0},{1,9},{9,17},{17,25},{25,1},{2,10},{10... | collective-permute-start | bytes 786440 | tf_op jit(solution)/shard_map/ppermute | solution.py:14
  292.0 21.5 %collective-permute-start.43 = (bf16[2,64,1024]{2,1,0:T(8,128)(2,1)S(1)}, bf16[2,64,1024]{2,1,0:T(8,128)(2,1)S(1)}, u32[]{:S(2)}, u32[]{:S(2)}) collective-permute-start(bf16[2,64,1024]{2,1,0:T(8,128)(2,1)S(1)} %get-tuple-element.68), channel_id=1, source_target_pairs={{0,24},{8,0},{16,8},{24,16},{1,25},{9,1},{17,9},{25,17},{2,26},{10... | collective-permute-start | bytes 786440 | tf_op jit(solution)/shard_map/ppermute | solution.py:14
  295.1 18.4 %collective-permute-start.44 = (bf16[2,64,1024]{2,1,0:T(8,128)(2,1)S(1)}, bf16[2,64,1024]{2,1,0:T(8,128)(2,1)S(1)}, u32[]{:S(2)}, u32[]{:S(2)}) collective-permute-start(bf16[2,64,1024]{2,1,0:T(8,128)(2,1)S(1)} %get-tuple-element.67), channel_id=1, source_target_pairs={{0,16},{8,24},{16,0},{24,8},{1,17},{9,25},{17,1},{25,9},{2,18},{10... | collective-permute-start | bytes 786440 | tf_op jit(solution)/shard_map/ppermute | solution.py:14
  304.2 12.5 %collective-permute-start.33 = (bf16[2,64,1024]{2,1,0:T(8,128)(2,1)}, bf16[2,64,1024]{2,1,0:T(8,128)(2,1)}, u32[]{:S(2)}, u32[]{:S(2)}) collective-permute-start(bf16[2,64,1024]{2,1,0:T(8,128)(2,1)} %get-tuple-element.71), channel_id=1, source_target_pairs={{0,1},{1,2},{2,3},{3,0},{4,5},{5,6},{6,7},{7,4},{8,9},{9,10},{10,1... | collective-permute-start | bytes 786440 | tf_op jit(solution)/shard_map/ppermute | solution.py:14
  310.2 6.7 %collective-permute-start.34 = (bf16[2,64,1024]{2,1,0:T(8,128)(2,1)}, bf16[2,64,1024]{2,1,0:T(8,128)(2,1)}, u32[]{:S(2)}, u32[]{:S(2)}) collective-permute-start(bf16[2,64,1024]{2,1,0:T(8,128)(2,1)} %get-tuple-element.73), channel_id=1, source_target_pairs={{0,3},{1,0},{2,1},{3,2},{4,7},{5,4},{6,5},{7,6},{8,11},{9,8},{10,9... | collective-permute-start | bytes 786440 | tf_op jit(solution)/shard_map/ppermute | solution.py:14
  312.0 8.9 %collective-permute-start.35 = (bf16[2,64,1024]{2,1,0:T(8,128)(2,1)}, bf16[2,64,1024]{2,1,0:T(8,128)(2,1)}, u32[]{:S(2)}, u32[]{:S(2)}) collective-permute-start(bf16[2,64,1024]{2,1,0:T(8,128)(2,1)} %get-tuple-element.72), channel_id=1, source_target_pairs={{0,2},{1,3},{2,0},{3,1},{4,6},{5,7},{6,4},{7,5},{8,10},{9,11},{10,... | collective-permute-start | bytes 786440 | tf_op jit(solution)/shard_map/ppermute | solution.py:14
  322.3 8.5 %collective-permute-start.45 = (bf16[64,2048]{1,0:T(8,128)(2,1)S(1)}, bf16[64,2048]{1,0:T(8,128)(2,1)S(1)}, u32[]{:S(2)}, u32[]{:S(2)}) collective-permute-start(bf16[64,2048]{1,0:T(8,128)(2,1)S(1)} %fusion.9), channel_id=1, source_target_pairs={{0,4},{4,0},{1,5},{5,1},{2,6},{6,2},{3,7},{7,3},{8,12},{12,8},{9,1... | collective-permute-start | bytes 786440 | tf_op jit(solution)/shard_map/ppermute | solution.py:14
  (22 other events, 386.3 us)

commit v2 on v0

v2 whole, which is shorter than its diff:
```python
import jax
import jax.numpy as jnp
from jax import lax
from jax.experimental import pallas as pl
from jax.experimental.pallas import tpu as pltpu
from jax.sharding import Mesh, PartitionSpec as P

F32, BF16 = jnp.float32, jnp.bfloat16
VMEM_LIMIT = 60 << 20


def hop(block, axis, distance):
    n = lax.axis_size(axis)
    return lax.ppermute(block, axis, [(i, (i + distance) % n) for i in range(n)])


def dot(a, b, dims):
    return lax.dot_general(a, b, (dims, ((), ())), preferred_element_type=F32)


def collect_kernel(at_ref, *refs):
    ins, outs, sem = refs[:16], refs[16:18], refs[18]
    copies = []
    for state in range(2):
        own = at_ref[2] if state == 0 else at_ref[0]
        for n, (plane, distance) in enumerate([(p, d) for p in range(2) for d in range(4)]):
            where = outs[state].at[lax.rem(plane + at_ref[1], 2), lax.rem(own + distance, 4)]
            copies.append(pltpu.make_async_copy(ins[8 * state + n], where, sem.at[8 * state + n]))
    for copy in copies:
        copy.start()
    for copy in copies:
        copy.wait()


def collect(at, blocks):
    shape = jax.ShapeDtypeStruct((2, 4) + blocks[0].shape, blocks[0].dtype)
    return pl.pallas_call(
        collect_kernel,
        out_shape=(shape,) * 2,
        in_specs=[pl.BlockSpec(memory_space=pltpu.SMEM)] + [pl.BlockSpec(memory_space=pl.ANY)] * 16,
        out_specs=(pl.BlockSpec(memory_space=pltpu.VMEM),) * 2,
        scratch_shapes=[pltpu.SemaphoreType.DMA((16,))],
        compiler_params=pltpu.CompilerParams(vmem_limit_bytes=VMEM_LIMIT),
        cost_estimate=pl.CostEstimate(flops=0, bytes_accessed=8 << 20, transcendentals=0),
        name="collect",
    )(at, *blocks)


def around(near, other, axis):
    near_1, near_3 = hop(near, axis, -1), hop(near, axis, 1)
    other_3, other_1 = hop(other, axis, 1), hop(other, axis, -1)
    near_2 = hop(near_1, axis, -1)
    other_2 = hop(other_3, axis, 1)
    return [near, near_1, near_2, near_3, other, other_1, other_2, other_3]


def halves_kernel(*refs):
    outs, sem = refs[-5:-1], refs[-1]
    copies = [pltpu.make_async_copy(refs[n].at[n % 2], outs[n], sem.at[n]) for n in range(4)]
    for copy in copies:
        copy.start()
    for copy in copies:
        copy.wait()


def halves(blocks, before):
    shape = jax.ShapeDtypeStruct(blocks[0].shape[1:], blocks[0].dtype)
    return pl.pallas_call(
        halves_kernel,
        out_shape=(shape,) * 4,
        in_specs=[pl.BlockSpec(memory_space=pl.ANY)] * (4 + len(before)),
        out_specs=(pl.BlockSpec(memory_space=pltpu.VMEM),) * 4,
        scratch_shapes=[pltpu.SemaphoreType.DMA((4,))],
        compiler_params=pltpu.CompilerParams(vmem_limit_bytes=VMEM_LIMIT),
        cost_estimate=pl.CostEstimate(flops=0, bytes_accessed=8 << 20, transcendentals=0),
        name="halves",
    )(*blocks, *before)


def gather_site(at, rows, before):
    first, second = rows[0], rows[1]
    first_other, second_other = hop(first, "x", 1), hop(second, "x", 1)
    a, b = collect(at, around(first, first_other, "z") + around(second, second_other, "y"))
    right_a, left_a, right_b, left_b = hop(a, "y", -1), hop(a, "y", 1), hop(b, "z", -1), hop(b, "z", 1)
    to_left_a, to_right_a, to_left_b, to_right_b = halves((right_a, left_a, right_b, left_b), before)
    return [
        *(a, right_a, left_a, hop(to_left_a, "y", -1), hop(to_right_a, "y", 1)),
        *(b, right_b, left_b, hop(to_left_b, "z", -1), hop(to_right_b, "z", 1)),
    ]


def site_copies(at_ref, blocks, buffer, sem, column, tile):
    made = []
    columns = pl.ds(pl.multiple_of(column, tile), tile)
    for x in range(2):
        for distance, place in ((0, 0), (1, 1), (3, 2), (2, 3 + x)):
            y, z = lax.rem(at_ref[0] + distance, 4), lax.rem(at_ref[2] + distance, 4)
            a, b = (ref if distance == 2 else ref.at[x] for ref in (blocks[place], blocks[5 + place]))
            n = 4 * x + distance
            made.append(pltpu.make_async_copy(a.at[:, :, columns], buffer.at[y, x, :, 0], sem.at[n]))
            made.append(pltpu.make_async_copy(b.at[:, :, columns], buffer.at[:, x, z, 1], sem.at[8 + n]))
    return made


def bond_kernel(r_ref, b_ref, o_ref):
    rows = o_ref.shape[1]
    full = dot(r_ref[...], b_ref[...], ((1,), (1,)))
    low = lax.broadcasted_iota(jnp.int32, (rows, 128), 1) < 64
    for j in range(o_ref.shape[0] // 2):
        for w in range(full.shape[0] // rows // 2):
            a = full[2 * w * rows : (2 * w + 1) * rows, 128 * j : 128 * j + 128]
            b = full[(2 * w + 1) * rows : (2 * w + 2) * rows, 128 * j : 128 * j + 128]
            lanes = pl.ds(128 * w, 128)
            o_ref[2 * j, :, lanes] = jnp.where(low, a, pltpu.roll(b, 64, 1)).astype(BF16)
            o_ref[2 * j + 1, :, lanes] = jnp.where(low, pltpu.roll(a, 64, 1), b).astype(BF16)


def bond_right(right_next, bond):
    w, rows, c = right_next.shape
    k = bond.shape[0]
    tile = 256
    return pl.pallas_call(
        bond_kernel,
        out_shape=jax.ShapeDtypeStruct((k // 64, rows, w * 64), BF16),
        grid=(k // tile,),
        in_specs=[
            pl.BlockSpec((w * rows, c), lambda i: (0, 0)),
            pl.BlockSpec((tile, c), lambda i: (i, 0)),
        ],
        out_specs=pl.BlockSpec((tile // 64, rows, w * 64), lambda i: (i, 0, 0)),
        compiler_params=pltpu.CompilerParams(vmem_limit_bytes=VMEM_LIMIT),
        cost_estimate=pl.CostEstimate(flops=2 * w * rows * c * k, bytes_accessed=12 << 20, transcendentals=0),
        name="bond_right",
    )(right_next.reshape(w * rows, c), bond)


def stacked(refs):
    return jnp.concatenate([ref[...].reshape(-1, ref.shape[-1]) for ref in refs], 0)


def begin_kernel(at_ref, first_ref, second_ref, *refs):
    blocks, h_ref, left_ref = refs[:6], refs[6], refs[7]

    @pl.when(pl.program_id(0) == 0)
    def _():
        for t, (source, own) in enumerate(((first_ref, at_ref[0]), (second_ref, at_ref[2]))):
            for n, distance in enumerate((0, 1, 3)):
                start = pl.multiple_of(512 * lax.rem(own + distance, 4), 512)
                left_ref[t, :, 512 * n : 512 * (n + 1)] = source[:, pl.ds(start, 512)]

    for t in range(2):
        h_ref[t] = dot(left_ref[t], stacked(blocks[3 * t : 3 * t + 3]), ((1,), (0,)))


def begin(at, first, second, blocks):
    rows, k = first.shape
    columns, tile = blocks[0].shape[-1], 256
    whole = pl.BlockSpec((rows, k), lambda i: (0, 0))
    return pl.pallas_call(
        begin_kernel,
        out_shape=jax.ShapeDtypeStruct((2, rows, columns), F32),
        grid=(columns // tile,),
        in_specs=[pl.BlockSpec(memory_space=pltpu.SMEM), whole, whole]
        + [pl.BlockSpec((2, 4, 64, tile), lambda i: (0, 0, 0, i))] * 6,
        out_specs=pl.BlockSpec((2, rows, tile), lambda i: (0, 0, i)),
        scratch_shapes=[pltpu.VMEM((2, rows, 3 * k // 4), BF16)],
        compiler_params=pltpu.CompilerParams(vmem_limit_bytes=VMEM_LIMIT),
        cost_estimate=pl.CostEstimate(flops=3 * rows * k * columns, bytes_accessed=24 << 20, transcendentals=0),
        name="begin",
    )(at, first, second, *blocks)


def hold(value, *before):
    anywhere = pl.BlockSpec(memory_space=pl.ANY)
    return pl.pallas_call(
        lambda *refs: None,
        out_shape=jax.ShapeDtypeStruct(value.shape, value.dtype),
        in_specs=[anywhere] * (1 + len(before)),
        out_specs=anywhere,
        input_output_aliases={0: 0},
        name="hold",
    )(value, *before)


def absorb_kernel(at_ref, m_ref, first_ref, second_ref, part_ref, *refs):
    blocks, o_ref, left_ref, h_ref = refs[:4], *refs[4:]
    w, tile = o_ref.shape[1], part_ref.shape[-1]
    rows = first_ref.shape[0] // w

    @pl.when(pl.program_id(0) == 0)
    def _():
        for t, (source, own) in enumerate(((first_ref, at_ref[0]), (second_ref, at_ref[2]))):
            left_ref[t] = source[:, pl.ds(pl.multiple_of(512 * lax.rem(own + 2, 4), 512), 512)]

    for t in range(2):
        h_ref[t] = part_ref[t] + dot(left_ref[t], stacked(blocks[2 * t : 2 * t + 2]), ((1,), (0,)))
    for v in range(w):
        sums = []
        for s in range(2):
            total = None
            for u in range(w):
                for t in range(2):
                    term = m_ref[((u * w + v) * 2 + s) * 2 + t] * h_ref[t, u * rows : (u + 1) * rows, :]
                    total = term if total is None else total + term
            sums.append(total)
        turned = jnp.concatenate(sums, 0).T
        o_ref[:, v] = turned.reshape(tile // 64, 64, 2 * rows).astype(BF16)


def absorb(at, mpo, first, second, part, blocks, w):
    rows, k = first.shape
    columns, tile = blocks[0].shape[-1], 256
    scalars = pl.BlockSpec(memory_space=pltpu.SMEM)
    whole = pl.BlockSpec((rows, k), lambda i: (0, 0))
    return pl.pallas_call(
        absorb_kernel,
        out_shape=jax.ShapeDtypeStruct((columns // 64, w, 64, 2 * rows // w), BF16),
        grid=(columns // tile,),
        in_specs=[scalars, scalars, whole, whole, pl.BlockSpec((2, rows, tile), lambda i: (0, 0, i))]
        + [pl.BlockSpec((4, 64, tile), lambda i: (0, 0, i))] * 4,
        out_specs=pl.BlockSpec((tile // 64, w, 64, 2 * rows // w), lambda i: (i, 0, 0, 0)),
        scratch_shapes=[pltpu.VMEM((2, rows, k // 4), BF16), pltpu.VMEM((2, rows, tile), F32)],
        compiler_params=pltpu.CompilerParams(vmem_limit_bytes=VMEM_LIMIT),
        cost_estimate=pl.CostEstimate(flops=rows * k * columns, bytes_accessed=20 << 20, transcendentals=0),
        name="absorb",
    )(at, mpo.reshape(-1), first, second, part, *blocks)


def step_kernel(at_ref, c_ref, *refs):
    blocks, e_ref, t_ref = refs[:10], refs[10], refs[11]
    buffer, lhs_ref, sem, lhs_sem = refs[12:]
    parts, depth = c_ref.shape[0], c_ref.shape[2]
    tile = buffer.shape[-1]
    i, count = pl.program_id(0), pl.num_programs(0)

    def copies(step):
        slot = lax.rem(step, 2)
        return site_copies(at_ref, blocks, buffer.at[slot], sem.at[slot], step * tile, tile)

    def sides():
        return [
            pltpu.make_async_copy(c_ref.at[p], lhs_ref.at[:, pl.ds(depth * p, depth)], lhs_sem.at[p])
            for p in range(parts)
        ]

    @pl.when(i == 0)
    def _():
        for copy in sides() + copies(i):
            copy.start()

    @pl.when(i + 1 < count)
    def _():
        for copy in copies(i + 1):
            copy.start()

    @pl.when(i == 0)
    def _():
        for copy in sides():
            copy.wait()

    for copy in copies(i):
        copy.wait()
    env = dot(lhs_ref[...], buffer[lax.rem(i, 2)].reshape(lhs_ref.shape[1], tile), ((1,), (0,)))
    e_ref[...] = env.astype(BF16)
    t_ref[...] = env.T.astype(BF16)


def step(at, carried, site):
    parts, rows, depth = carried.shape
    columns, tile = site[0].shape[-1], 256
    anywhere = pl.BlockSpec(memory_space=pl.ANY)
    return pl.pallas_call(
        step_kernel,
        out_shape=(jax.ShapeDtypeStruct((rows, columns), BF16), jax.ShapeDtypeStruct((columns, rows), BF16)),
        grid=(columns // tile,),
        in_specs=[pl.BlockSpec(memory_space=pltpu.SMEM)] + [anywhere] * 11,
        out_specs=(pl.BlockSpec((rows, tile), lambda i: (0, i)), pl.BlockSpec((tile, rows), lambda i: (i, 0))),
        scratch_shapes=[
            pltpu.VMEM((2, 4, 2, 4, 2, 64, tile), BF16),
            pltpu.VMEM((rows, parts * depth), BF16),
            pltpu.SemaphoreType.DMA((2, 16)),
            pltpu.SemaphoreType.DMA((parts,)),
        ],
        compiler_params=pltpu.CompilerParams(vmem_limit_bytes=VMEM_LIMIT),
        cost_estimate=pl.CostEstimate(flops=2 * rows * columns * parts * depth, bytes_accessed=24 << 20, transcendentals=0),
        name="step",
    )(at, carried, *site)


def terms_kernel(distances, at_ref, t_ref, b_ref, *outs):
    half = b_ref.shape[1] // 2
    n = len(distances)
    for m, distance in enumerate(distances):
        y, z = lax.rem(at_ref[0] + distance, 4), lax.rem(at_ref[2] + distance, 4)
        for side in range(2):
            for part in range(2):
                if side == 0:
                    rows = t_ref[pl.ds(2 * y + part, 1), :].reshape(256, -1)
                else:
                    rows = t_ref[4 * part : 4 * part + 4, pl.ds(z, 1)].reshape(256, -1)
                columns = b_ref[:, half * side : half * (side + 1)]
                outs[2 * n * side + 2 * m + part][...] = dot(rows, columns, ((1,), (0,))).astype(BF16)


def terms(distances, at, turned, bond):
    depth, columns = bond.shape
    half = columns // 2
    vmem = pl.BlockSpec(memory_space=pltpu.VMEM)
    count = 4 * len(distances)
    return pl.pallas_call(
        lambda *refs: terms_kernel(distances, *refs),
        out_shape=(jax.ShapeDtypeStruct((256, half), BF16),) * count,
        in_specs=[pl.BlockSpec(memory_space=pltpu.SMEM), vmem, vmem],
        out_specs=(vmem,) * count,
        compiler_params=pltpu.CompilerParams(vmem_limit_bytes=24 << 20),
        cost_estimate=pl.CostEstimate(flops=count * 2 * 256 * half * depth, bytes_accessed=count << 19, transcendentals=0),
        name="terms_%d" % len(distances),
    )(at, turned.reshape(8, 4, 64, depth), bond)


def add(*terms):
    total = terms[0].astype(F32)
    for term in terms[1:]:
        total = total + term.astype(F32)
    return total.astype(BF16)


def sum_line(far, right, left, own, axis):
    up, down = hop(far[0], axis, 1), hop(far[1], axis, -1)
    right = hop(jnp.stack([add(right[0], up), right[1]]), axis, 1)
    left = hop(jnp.stack([left[0], add(left[1], down)]), axis, -1)
    return add(jnp.stack(own), right, left)


def sum_short(blocks, axis):
    own = lax.axis_index(axis)
    right, far, left, mine = (lax.dynamic_index_in_dim(blocks, (own + d) % 4, 0, keepdims=False) for d in (1, 2, 3, 0))
    return add(mine, hop(right, axis, 1), hop(left, axis, -1), hop(far, axis, 2))


def scatter_image(far, rest):
    half = far[0].shape[-1]
    a = sum_line(far[:2], rest[0:2], rest[2:4], rest[4:6], "y")
    b = sum_line(far[2:], rest[6:8], rest[8:10], rest[10:12], "z")
    a = sum_short(a.reshape(2, 4, 64, half).transpose(1, 0, 2, 3), "z")
    b = sum_short(b.reshape(4, 2, 64, half), "y")
    both = jnp.concatenate([a, b], 2)
    own = lax.axis_index("x")
    theirs = hop(lax.dynamic_index_in_dim(both, 1 - own, 0, keepdims=False), "x", 1)
    return add(lax.dynamic_index_in_dim(both, own, 0, keepdims=False), theirs)


def local(env_left, site_tensor, mpo_tensor, env_right, bond_tensor):
    sector = ("y", "x", "z")
    at = jnp.stack([lax.axis_index(name) for name in sector]).astype(jnp.int32)
    route = [((i + 1) % 4, i) for i in range(4)]
    right_next = lax.ppermute(env_right, "region", route)[0]
    bond = bond_right(right_next, bond_tensor[0])
    w, rows, k = env_left.shape[1:]
    first = env_left.reshape(w * rows, k)
    second = first.reshape(w * rows, 4, 2, 4, 64).transpose(0, 3, 2, 1, 4).reshape(w * rows, k)
    site = gather_site(at, site_tensor[0].transpose(1, 0, 2), (bond, second))
    near, far = site[0:3] + site[5:8], site[3:5] + site[8:10]
    part = begin(at, first, second, near)
    bond = hold(bond, part, *site)
    bond = lax.all_to_all(bond, sector, split_axis=0, concat_axis=0, tiled=True)
    carried = absorb(at, mpo_tensor[0], first, second, part, far, w)
    carried = lax.all_to_all(carried, sector, split_axis=0, concat_axis=0, tiled=True)
    parts, w, columns, depth = carried.shape
    env_new, turned = step(at, carried.reshape(parts, w * columns, depth), site)
    bond = bond.reshape(-1, bond.shape[-1]).T
    far_terms = terms((2,), at, turned, bond)
    rest_terms = terms((1, 3, 0), at, turned, bond)
    return (env_new.reshape(1, w, columns, -1), scatter_image(far_terms, rest_terms)[None])


def solution(mesh):
    fine = Mesh(mesh.devices.reshape(4, 4, 2, 4), ("region", "y", "x", "z"))
    sector = ("y", "x", "z")
    return jax.shard_map(
        local,
        mesh=fine,
        in_specs=(
            P("region", None, sector, None),
            P("region", sector, None, None),
            P("region", None, None, None, None),
            P("region", None, sector, None),
            P("region", None, None),
        ),
        out_specs=(P("region", None, sector, None), P("region", sector, None)),
        check_vma=False,
    )
```

time: 605 us -> 309 us (0.51)
  waiting for transfers between devices: 418 us -> 110 us
  Pallas kernels: 0 us -> 74.2 us
  local copies, waits for them, and re-layouts: 100 us -> 29.8 us
  starting transfers between devices: 17.9 us -> 76.1 us
  matrix products: 51.1 us -> 0 us
  between operations: 14.1 us -> 1.01 us
  other arithmetic: 1.77 us -> 12.3 us
    reduce_scatter x1 -> x0, waiting for transfers between devices: 229 us -> none  [local(): lax.psum_scatter(jnp.einsum('wka,wbk->ab', env_new, bond_moved, preferred...]
    all_gather x1 -> x0, waiting for transfers between devices: 127 us -> none  [absorb_side(): gathered = lax.all_gather(site_tensor, 'sector', axis=1, tiled=True)[0]]
    pallas_call x0 -> x9, Pallas kernels: none -> 74.2 us  [the longest x1 16.9 us: step(): pl.pallas_call(step_kernel, out_shape=(jax.ShapeDtypeStruct((rows, column...]
    ppermute x1 -> x38, starting transfers between devices: 1.08 us -> 63.5 us  [the longest x37 63.5 us: hop(): lax.ppermute(block, axis, [(i, (i + distance) % n) for i in range(n)])]
    dot_general x5 -> x0, matrix products: 51.1 us -> none  [the longest x1 13.6 us: local(): jnp.einsum('wsac,asb->wcb', carried_moved, gathered, preferred_element_ty...]
    unnamed x7 -> x52, local copies, waits for them, and re-layouts: 42.8 us -> 5.26 us
    ppermute x1 -> x38, waiting for transfers between devices: 26.9 us -> 56.8 us  [the longest x37 56.8 us: hop(): lax.ppermute(block, axis, [(i, (i + distance) % n) for i in range(n)])]
    all_to_all x3 -> x0, local copies, waits for them, and re-layouts: 24.6 us -> none  [the longest x2 12.6 us: local(): lax.all_to_all(bond_right, 'sector', split_axis=2, concat_axis=1, tiled=T...]
  transfers between devices with their start and end apart: 5 -> 40, of which waited for: 4 -> 22; matrix products, arithmetic and copies ran while one was open for 14% -> 12% of each run, Pallas kernels for 0% -> 17%
where the time goes in v2:
time: 309 us; the launch traced here: 304 us
  waiting for transfers between devices  110 us (36%)
  starting transfers between devices  76.1 us (25%)
  Pallas kernels  74.2 us (24%)
  local copies, waits for them, and re-layouts  29.8 us (10%)
  other arithmetic  12.3 us (4%)
    ppermute x37, starting transfers between devices, hop(): lax.ppermute(block, axis, [(i, (i + distance) % n) for i in range(n)])  63.5 us
    ppermute x37, waiting for transfers between devices, hop(): lax.ppermute(block, axis, [(i, (i + distance) % n) for i in range(n)])  56.8 us
    all_to_all x1, waiting for transfers between devices, local(): lax.all_to_all(carried, sector, split_axis=0, concat_axis=0, tiled=True)  47.6 us
    pallas_call x1, Pallas kernels, step(): pl.pallas_call(step_kernel, out_shape=(jax.ShapeDtypeStruct((rows, column...  16.9 us
    pallas_call x1, Pallas kernels, absorb(): pl.pallas_call(absorb_kernel, out_shape=jax.ShapeDtypeStruct((columns //...  16.7 us
    pallas_call x1, Pallas kernels, begin(): pl.pallas_call(begin_kernel, out_shape=jax.ShapeDtypeStruct((2, rows, col...  14.8 us
    pallas_call x1, Pallas kernels, bond_right(): pl.pallas_call(bond_kernel, out_shape=jax.ShapeDtypeStruct((k // 64, rows...  11 us
    another operation x1, local copies, waits for them, and re-layouts, local(): first.reshape(w * rows, 4, 2, 4, 64).transpose(0, 3, 2, 1, 4)  8.44 us
  transfers between devices with their start and end apart: 40, of which 22 were waited for; matrix products, arithmetic and copies ran while one was open for 12% of the time, Pallas kernels for 17%

profile of v2, /device:TPU:0, one launch (start us, length us, event | category | flops | bytes accessed | tf_op | source)
XLA Modules:
  0.0 303.8 jit_solution(4649074568436942981)
XLA Ops:
  1.9 3.2 %collective-permute-start.10 = (bf16[64,2048]{1,0:T(8,128)(2,1)S(1)}, bf16[64,2048]{1,0:T(8,128)(2,1)S(1)}, u32[]{:S(2)}, u32[]{:S(2)}) collective-permute-start(bf16[64,2048]{1,0:T(8,128)(2,1)S(1)} %get-tuple-element.56.refs_8_), channel_id=1, source_target_pairs={{0,4},{4,0},{1,5},{5,1},{2,6},{6,2},{3,7},{7,3},{8,12},{12,8},{9,1... | collective-permute-start | bytes 786440 | tf_op jit(solution)/shard_map/ppermute | solution.py:14
  5.5 4.1 %collective-permute-start = (bf16[64,2048]{1,0:T(8,128)(2,1)S(1)}, bf16[64,2048]{1,0:T(8,128)(2,1)S(1)}, u32[]{:S(2)}, u32[]{:S(2)}) collective-permute-start(bf16[64,2048]{1,0:T(8,128)(2,1)S(1)} %get-tuple-element.57.refs_0_), channel_id=1, source_target_pairs={{0,3},{1,0},{2,1},{3,2},{4,7},{5,4},{6,5},{7,6},{8,11},{9,8},{10,9... | collective-permute-start | bytes 786440 | tf_op jit(solution)/shard_map/ppermute | solution.py:14
  9.6 3.0 collective-permute-start.7
  14.3 2.7 collective-permute-done.3.refs_4_
  17.0 1.8 collective-permute-start.12
  18.8 1.9 collective-permute-start.5
  22.4 2.2 collective-permute-start.4
  24.6 1.9 collective-permute-done.12.refs_15_
  26.5 3.5 %collective-permute-start.1 = (bf16[64,2048]{1,0:T(8,128)(2,1)S(1)}, bf16[64,2048]{1,0:T(8,128)(2,1)S(1)}, u32[]{:S(2)}, u32[]{:S(2)}) collective-permute-start(bf16[64,2048]{1,0:T(8,128)(2,1)S(1)} %collective-permute-done.refs_1_), channel_id=1, source_target_pairs={{0,3},{1,0},{2,1},{3,2},{4,7},{5,4},{6,5},{7,6},{8,11},{9,8},{10,9... | collective-permute-start | bytes 786440 | tf_op jit(solution)/shard_map/ppermute | solution.py:14
  30.0 1.8 collective-permute-start.8
  34.7 1.8 collective-permute-done.8.refs_10_
  36.5 3.0 collective-permute-done.13.refs_14_
  39.8 4.9 %collect.1 = (bf16[2,4,64,2048]{3,2,1,0:T(8,128)(2,1)}, bf16[2,4,64,2048]{3,2,1,0:T(8,128)(2,1)}) custom-call(s32[3]{0:T(128)} %pad_add_fusion.at_ref.refs_0_, bf16[64,2048]{1,0:T(8,128)(2,1)} %copy-done.12, bf16[64,2048]{1,0:T(8,128)(2,1)} %copy-done.15, bf16[64,2048]{1,0:T(8,128)(2,1)} %copy-done.23, bf16[64,2048]{1,0:T(8,128)(2,1)} %copy-done.17, ...), custom_call_target="tpu_custom_call" | custom-call | bytes 8388608 | tf_op jit(solution)/shard_map/collect/pallas_call | solution.py:37
  44.8 3.1 %collective-permute-start.14 = (bf16[2,4,64,2048]{3,2,1,0:T(8,128)(2,1)}, bf16[2,4,64,2048]{3,2,1,0:T(8,128)(2,1)S(1)}, u32[]{:S(2)}, u32[]{:S(2)}) collective-permute-start(bf16[2,4,64,2048]{3,2,1,0:T(8,128)(2,1)} %get-tuple-element.26.refs_0_.refs_2_), channel_id=1, source_target_pairs={{0,24},{8,0},{16,8},{24,16},{1,25},{9,1},{17,9},{25,17},{2,26},{10... | collective-permute-start | bytes 6291464 | tf_op jit(solution)/shard_map/ppermute | solution.py:14
  47.8 2.0 collective-permute-start.17
  49.9 8.4 %reshape.54 = bf16[512,4,2,4,64]{4,3,2,1,0:T(4,128)(2,1)} reshape(bf16[1,8,64,2048]{3,2,1,0:T(8,128)(2,1)} %param.5) | data formatting | bytes 4194304 | tf_op jit(solution)/shard_map/reshape;reshape | solution.py:361
  58.3 6.9 %copy.22 = bf16[512,4,2,4,64]{0,4,1,2,3:T(8,128)(2,1)} copy(bf16[512,4,2,4,64]{4,3,2,1,0:T(4,128)(2,1)} %reshape.54) | data formatting | bytes 4194304 | tf_op jit(solution)/shard_map/transpose | solution.py:361
  65.2 3.9 %copy.18.second_ref.refs_5_ = bf16[512,2048]{1,0:T(8,128)(2,1)} copy(bf16[512,2048]{0,1:T(8,128)(2,1)} %bitcast.87) | data formatting | bytes 4194304 | tf_op jit(solution)/shard_map/reshape | solution.py:361
  69.2 11.0 %bond_right.1.refs_4_.refs_0_ = bf16[32,64,512]{2,1,0:T(8,128)(2,1)} custom-call(bf16[512,2048]{1,0:T(8,128)(2,1)} %bitcast.12.r_ref, bf16[2048,2048]{1,0:T(8,128)(2,1)} %bitcast.94), custom_call_target="tpu_custom_call" | custom-call | flops 4294967296 | bytes 12582912 | tf_op jit(solution)/shard_map/bond_right/pallas_call | solution.py:122
  80.1 9.8 %collective-permute-done.14.refs_1_.refs_0_.refs_3_ = bf16[2,4,64,2048]{3,2,1,0:T(8,128)(2,1)S(1)} collective-permute-done((bf16[2,4,64,2048]{3,2,1,0:T(8,128)(2,1)}, bf16[2,4,64,2048]{3,2,1,0:T(8,128)(2,1)S(1)}, u32[]{:S(2)}, u32[]{:S(2)}) %collective-permute-start.14) | collective-permute-done | bytes 2097184 | tf_op jit(solution)/shard_map/ppermute | solution.py:14
  89.9 3.4 %collective-permute-done.15.refs_2_.refs_1_.refs_4_ = bf16[2,4,64,2048]{3,2,1,0:T(8,128)(2,1)} collective-permute-done((bf16[2,4,64,2048]{3,2,1,0:T(8,128)(2,1)}, bf16[2,4,64,2048]{3,2,1,0:T(8,128)(2,1)}, u32[]{:S(2)}, u32[]{:S(2)}) %collective-permute-start.15) | collective-permute-done | bytes 2097184 | tf_op jit(solution)/shard_map/ppermute | solution.py:14
  93.3 4.3 %halves.1 = (bf16[4,64,2048]{2,1,0:T(8,128)(2,1)}, bf16[4,64,2048]{2,1,0:T(8,128)(2,1)}, bf16[4,64,2048]{2,1,0:T(8,128)(2,1)}, bf16[4,64,2048]{2,1,0:T(8,128)(2,1)}) custom-call(bf16[2,4,64,2048]{3,2,1,0:T(8,128)(2,1)} %copy-done.6, bf16[2,4,64,2048]{3,2,1,0:T(8,128)(2,1)} %collective-permute-done.15.refs_2_.refs_1_.refs_4_, ...), custom_call_target="tpu_custom_call" | custom-call | bytes 8388608 | tf_op jit(solution)/shard_map/halves/pallas_call | solution.py:68
  97.6 3.0 collective-permute-start.19
  102.6 14.8 %begin.1.part_ref.refs_1_ = f32[2,512,2048]{2,1,0:T(8,128)} custom-call(s32[3]{0:T(128)} %pad_add_fusion.at_ref.refs_0_, bf16[512,2048]{1,0:T(8,128)(2,1)} %bitcast.85, bf16[512,2048]{1,0:T(8,128)(2,1)} %copy.18.second_ref.refs_5_, bf16[2,4,64,2048]{3,2,1,0:T(8,128)(2,1)} %get-tuple-element.26.refs_0_.refs_2_, bf16[2,4,64,2048]{3,2,1,0:T(8,128)(2,1)} %copy-done.6, ...), custom_call_target="tpu_custom_call" | custom-call | flops 6442450944 | bytes 25165824 | tf_op jit(solution)/shard_map/begin/pallas_call | solution.py:159
  118.7 3.3 %collective-permute-done.20.refs_1_.refs_4_.refs_6_ = bf16[4,64,2048]{2,1,0:T(8,128)(2,1)S(1)} collective-permute-done((bf16[4,64,2048]{2,1,0:T(8,128)(2,1)}, bf16[4,64,2048]{2,1,0:T(8,128)(2,1)S(1)}, u32[]{:S(2)}, u32[]{:S(2)}) %collective-permute-start.20) | collective-permute-done | bytes 1048608 | tf_op jit(solution)/shard_map/ppermute | solution.py:14
  123.3 6.9 %all-to-all-start.1 = ((bf16[32,64,512]{2,1,0:T(8,128)(2,1)}), bf16[32,64,512]{2,1,0:T(8,128)(2,1)S(1)}, u32[]{:S(2)}, u32[]{:S(2)}) async-start(bf16[32,64,512]{2,1,0:T(8,128)(2,1)} %hold.1), calls=%async_computation.1 | async-start | bytes 4194304 | tf_op jit(solution)/shard_map/all_to_all | solution.py:366
  131.1 16.7 %absorb.1 = bf16[32,8,64,128]{3,2,1,0:T(8,128)(2,1)} custom-call(s32[3]{0:T(128)} %pad_add_fusion.at_ref.refs_0_, f32[256]{0:T(256)} %reshape_squeeze.6.m_ref, bf16[512,2048]{1,0:T(8,128)(2,1)} %bitcast.86, bf16[512,2048]{1,0:T(8,128)(2,1)} %copy.18.second_ref.refs_5_, f32[2,512,2048]{2,1,0:T(8,128)} %begin.1.part_ref.refs_1_, ...), custom_call_target="tpu_custom_call" | custom-call | flops 2147483648 | bytes 20971520 | tf_op jit(solution)/shard_map/absorb/pallas_call | solution.py:215
  147.8 6.0 %all-to-all-done.1 = bf16[32,64,512]{2,1,0:T(8,128)(2,1)S(1)} async-done(((bf16[32,64,512]{2,1,0:T(8,128)(2,1)}), bf16[32,64,512]{2,1,0:T(8,128)(2,1)S(1)}, u32[]{:S(2)}, u32[]{:S(2)}) %all-to-all-start.1) | async-done | bytes 2097184 | tf_op jit(solution)/shard_map/all_to_all | solution.py:366
  155.1 5.7 %all-to-all-start = ((bf16[32,8,64,128]{3,2,1,0:T(8,128)(2,1)}), bf16[32,8,64,128]{3,2,1,0:T(8,128)(2,1)}, u32[]{:S(2)}, u32[]{:S(2)}) async-start(bf16[32,8,64,128]{3,2,1,0:T(8,128)(2,1)} %absorb.1), calls=%async_computation | async-start | bytes 8388608 | tf_op jit(solution)/shard_map/all_to_all | solution.py:368
  160.8 2.9 copy.19
  163.7 47.6 %all-to-all-done = bf16[32,8,64,128]{3,2,1,0:T(8,128)(2,1)} async-done(((bf16[32,8,64,128]{3,2,1,0:T(8,128)(2,1)}), bf16[32,8,64,128]{3,2,1,0:T(8,128)(2,1)}, u32[]{:S(2)}, u32[]{:S(2)}) %all-to-all-start) | async-done | bytes 4194336 | tf_op jit(solution)/shard_map/all_to_all | solution.py:368
  211.3 16.9 %step.1 = (bf16[512,2048]{1,0:T(8,128)(2,1)}, bf16[2048,512]{1,0:T(8,128)(2,1)}) custom-call(s32[3]{0:T(128)} %pad_add_fusion.at_ref.refs_0_, bf16[32,512,128]{2,1,0:T(8,128)(2,1)} %bitcast.14.c_ref, bf16[2,4,64,2048]{3,2,1,0:T(8,128)(2,1)} %get-tuple-element.26.refs_0_.refs_2_, bf16[2,4,64,2048]{3,2,1,0:T(8,128)(2,1)} %copy-done.6, ...), custom_call_target="tpu_custom_call" | custom-call | flops 8589934592 | bytes 25165824 | tf_op jit(solution)/shard_map/step/pallas_call | solution.py:272
  229.8 1.8 terms_1.1
  231.7 3.2 %collective-permute-start.32 = (bf16[256,1024]{1,0:T(8,128)(2,1)S(1)}, bf16[256,1024]{1,0:T(8,128)(2,1)S(1)}, u32[]{:S(2)}, u32[]{:S(2)}) collective-permute-start(bf16[256,1024]{1,0:T(8,128)(2,1)S(1)} %get-tuple-element.49), channel_id=1, source_target_pairs={{0,3},{1,0},{2,1},{3,2},{4,7},{5,4},{6,5},{7,6},{8,11},{9,8},{10,9... | collective-permute-start | bytes 1572872 | tf_op jit(solution)/shard_map/ppermute | solution.py:14
  234.9 4.0 %terms_3.1 = (bf16[256,1024]{1,0:T(8,128)(2,1)S(1)}, bf16[256,1024]{1,0:T(8,128)(2,1)S(1)}, bf16[256,1024]{1,0:T(8,128)(2,1)S(1)}, bf16[256,1024]{1,0:T(8,128)(2...) custom-call(s32[3]{0:T(128)S(1)} %copy-done.5, ...), custom_call_target="tpu_custom_call" | custom-call | flops 3221225472 | bytes 6291456 | tf_op jit(solution)/shard_map/terms_3/pallas_call | solution.py:310
  239.6 2.7 collective-permute-start.25
  244.1 3.2 %collective-permute-start.33 = (bf16[2,256,1024]{2,1,0:T(8,128)(2,1)}, bf16[2,256,1024]{2,1,0:T(8,128)(2,1)}, u32[]{:S(2)}, u32[]{:S(2)}) collective-permute-start(bf16[2,256,1024]{2,1,0:T(8,128)(2,1)} %pad_maximum_fusion.3), channel_id=1, source_target_pairs={{0,3},{1,0},{2,1},{3,2},{4,7},{5,4},{6,5},{7,6},{8,11},{9,8},{10,9... | collective-permute-start | bytes 3145736 | tf_op jit(solution)/shard_map/ppermute | solution.py:14
  247.3 3.6 %collective-permute-done.23 = bf16[256,1024]{1,0:T(8,128)(2,1)S(1)} collective-permute-done((bf16[256,1024]{1,0:T(8,128)(2,1)S(1)}, bf16[256,1024]{1,0:T(8,128)(2,1)S(1)}, u32[]{:S(2)}, u32[]{:S(2)}) %collective-permute-start.23) | collective-permute-done | bytes 524320 | tf_op jit(solution)/shard_map/ppermute | solution.py:14
  253.9 2.8 collective-permute-start.26
  256.6 8.7 %collective-permute-done.31 = bf16[2,256,1024]{2,1,0:T(8,128)(2,1)} collective-permute-done((bf16[2,256,1024]{2,1,0:T(8,128)(2,1)S(1)}, bf16[2,256,1024]{2,1,0:T(8,128)(2,1)}, u32[]{:S(2)}, u32[]{:S(2)}) %collective-permute-start.31) | collective-permute-done | bytes 1048608 | tf_op jit(solution)/shard_map/ppermute | solution.py:14
  266.2 2.2 add_convert_fusion
  269.1 5.2 %collective-permute-start.34 = (bf16[2,64,1024]{2,1,0:T(8,128)(2,1)S(1)}, bf16[2,64,1024]{2,1,0:T(8,128)(2,1)}, u32[]{:S(2)}, u32[]{:S(2)}) collective-permute-start(bf16[2,64,1024]{2,1,0:T(8,128)(2,1)S(1)} %get-tuple-element.50), channel_id=1, source_target_pairs={{0,8},{8,16},{16,24},{24,0},{1,9},{9,17},{17,25},{25,1},{2,10},{10... | collective-permute-start | bytes 786440 | tf_op jit(solution)/shard_map/ppermute | solution.py:14
  274.4 3.5 %collective-permute-start.36 = (bf16[2,64,1024]{2,1,0:T(8,128)(2,1)S(1)}, bf16[2,64,1024]{2,1,0:T(8,128)(2,1)}, u32[]{:S(2)}, u32[]{:S(2)}) collective-permute-start(bf16[2,64,1024]{2,1,0:T(8,128)(2,1)S(1)} %get-tuple-element.51), channel_id=1, source_target_pairs={{0,16},{8,24},{16,0},{24,8},{1,17},{9,25},{17,1},{25,9},{2,18},{10... | collective-permute-start | bytes 786440 | tf_op jit(solution)/shard_map/ppermute | solution.py:14
  278.1 2.2 add_convert_fusion.1
  281.1 3.4 %collective-permute-start.28 = (bf16[2,64,1024]{2,1,0:T(8,128)(2,1)S(1)}, bf16[2,64,1024]{2,1,0:T(8,128)(2,1)}, u32[]{:S(2)}, u32[]{:S(2)}) collective-permute-start(bf16[2,64,1024]{2,1,0:T(8,128)(2,1)S(1)} %get-tuple-element.55), channel_id=1, source_target_pairs={{0,3},{1,0},{2,1},{3,2},{4,7},{5,4},{6,5},{7,6},{8,11},{9,8},{10,9... | collective-permute-start | bytes 786440 | tf_op jit(solution)/shard_map/ppermute | solution.py:14
  287.6 3.4 %collective-permute-done.27 = bf16[2,64,1024]{2,1,0:T(8,128)(2,1)S(1)} collective-permute-done((bf16[2,64,1024]{2,1,0:T(8,128)(2,1)}, bf16[2,64,1024]{2,1,0:T(8,128)(2,1)S(1)}, u32[]{:S(2)}, u32[]{:S(2)}) %collective-permute-start.27) | collective-permute-done | bytes 262176 | tf_op jit(solution)/shard_map/ppermute | solution.py:14
  291.7 2.2 collective-permute-done.29
  295.7 7.4 %collective-permute-done.37 = bf16[64,2048]{1,0:T(8,128)(2,1)S(1)} collective-permute-done((bf16[64,2048]{1,0:T(8,128)(2,1)S(1)}, bf16[64,2048]{1,0:T(8,128)(2,1)S(1)}, u32[]{:S(2)}, u32[]{:S(2)}) %collective-permute-start.37) | collective-permute-done | bytes 262176 | tf_op jit(solution)/shard_map/ppermute | solution.py:14
  (116 shorter events, 31.1 us)
Async XLA Ops:
  1.9 37.9 %copy-start.11 = (bf16[64,2048]{1,0:T(8,128)(2,1)}, bf16[64,2048]{1,0:T(8,128)(2,1)S(1)}, u32[]{:S(2)}) copy-start(bf16[64,2048]{1,0:T(8,128)(2,1)S(1)} %get-tuple-element.56.refs_8_) | copy-start | bytes 786436
  1.9 37.9 %copy-start.12 = (bf16[64,2048]{1,0:T(8,128)(2,1)}, bf16[64,2048]{1,0:T(8,128)(2,1)S(1)}, u32[]{:S(2)}) copy-start(bf16[64,2048]{1,0:T(8,128)(2,1)S(1)} %get-tuple-element.57.refs_0_) | copy-start | bytes 786436
  1.9 10.8 %collective-permute-start.10 = (bf16[64,2048]{1,0:T(8,128)(2,1)S(1)}, bf16[64,2048]{1,0:T(8,128)(2,1)S(1)}, u32[]{:S(2)}, u32[]{:S(2)}) collective-permute-start(bf16[64,2048]{1,0:T(8,128)(2,1)S(1)} %get-tuple-element.56.refs_8_), channel_id=1, source_target_pairs={{0,4},{4,0},{1,5},{5,1},{2,6},{6,2},{3,7},{7,3},{8,12},{12,8},{9,1... | collective-permute-start | bytes 786440 | tf_op jit(solution)/shard_map/ppermute | solution.py:14
  5.1 11.9 %collective-permute-start.3 = (bf16[64,2048]{1,0:T(8,128)(2,1)S(1)}, bf16[64,2048]{1,0:T(8,128)(2,1)S(1)}, u32[]{:S(2)}, u32[]{:S(2)}) collective-permute-start(bf16[64,2048]{1,0:T(8,128)(2,1)S(1)} %get-tuple-element.57.refs_0_), channel_id=1, source_target_pairs={{0,4},{4,0},{1,5},{5,1},{2,6},{6,2},{3,7},{7,3},{8,12},{12,8},{9,1... | collective-permute-start | bytes 786440 | tf_op jit(solution)/shard_map/ppermute | solution.py:14
  5.5 13.3 %collective-permute-start = (bf16[64,2048]{1,0:T(8,128)(2,1)S(1)}, bf16[64,2048]{1,0:T(8,128)(2,1)S(1)}, u32[]{:S(2)}, u32[]{:S(2)}) collective-permute-start(bf16[64,2048]{1,0:T(8,128)(2,1)S(1)} %get-tuple-element.57.refs_0_), channel_id=1, source_target_pairs={{0,3},{1,0},{2,1},{3,2},{4,7},{5,4},{6,5},{7,6},{8,11},{9,8},{10,9... | collective-permute-start | bytes 786440 | tf_op jit(solution)/shard_map/ppermute | solution.py:14
  9.6 11.1 %collective-permute-start.7 = (bf16[64,2048]{1,0:T(8,128)(2,1)S(1)}, bf16[64,2048]{1,0:T(8,128)(2,1)S(1)}, u32[]{:S(2)}, u32[]{:S(2)}) collective-permute-start(bf16[64,2048]{1,0:T(8,128)(2,1)S(1)} %get-tuple-element.56.refs_8_), channel_id=1, source_target_pairs={{0,24},{8,0},{16,8},{24,16},{1,25},{9,1},{17,9},{25,17},{2,26},{10... | collective-permute-start | bytes 786440 | tf_op jit(solution)/shard_map/ppermute | solution.py:14
  12.6 9.8 %collective-permute-start.2 = (bf16[64,2048]{1,0:T(8,128)(2,1)S(1)}, bf16[64,2048]{1,0:T(8,128)(2,1)S(1)}, u32[]{:S(2)}, u32[]{:S(2)}) collective-permute-start(bf16[64,2048]{1,0:T(8,128)(2,1)S(1)} %get-tuple-element.57.refs_0_), channel_id=1, source_target_pairs={{0,1},{1,2},{2,3},{3,0},{4,5},{5,6},{6,7},{7,4},{8,9},{9,10},{10,1... | collective-permute-start | bytes 786440 | tf_op jit(solution)/shard_map/ppermute | solution.py:14
  12.7 27.0 %copy-start.13 = (bf16[64,2048]{1,0:T(8,128)(2,1)}, bf16[64,2048]{1,0:T(8,128)(2,1)S(1)}, u32[]{:S(2)}) copy-start(bf16[64,2048]{1,0:T(8,128)(2,1)S(1)} %collective-permute-done.10.refs_12_) | copy-start | bytes 786436
  12.7 11.9 %collective-permute-start.9 = (bf16[64,2048]{1,0:T(8,128)(2,1)S(1)}, bf16[64,2048]{1,0:T(8,128)(2,1)S(1)}, u32[]{:S(2)}, u32[]{:S(2)}) collective-permute-start(bf16[64,2048]{1,0:T(8,128)(2,1)S(1)} %get-tuple-element.56.refs_8_), channel_id=1, source_target_pairs={{0,8},{8,16},{16,24},{24,0},{1,9},{9,17},{17,25},{25,1},{2,10},{10... | collective-permute-start | bytes 786440 | tf_op jit(solution)/shard_map/ppermute | solution.py:14
  17.0 22.7 %copy-start.14 = (bf16[64,2048]{1,0:T(8,128)(2,1)}, bf16[64,2048]{1,0:T(8,128)(2,1)S(1)}, u32[]{:S(2)}) copy-start(bf16[64,2048]{1,0:T(8,128)(2,1)S(1)} %collective-permute-done.3.refs_4_) | copy-start | bytes 786436
  17.0 9.5 %collective-permute-start.12 = (bf16[64,2048]{1,0:T(8,128)(2,1)S(1)}, bf16[64,2048]{1,0:T(8,128)(2,1)S(1)}, u32[]{:S(2)}, u32[]{:S(2)}) collective-permute-start(bf16[64,2048]{1,0:T(8,128)(2,1)S(1)} %collective-permute-done.10.refs_12_), channel_id=1, source_target_pairs={{0,8},{8,16},{16,24},{24,0},{1,9},{9,17},{17,25},{25,1},{2,10},{10... | collective-permute-start | bytes 786440 | tf_op jit(solution)/shard_map/ppermute | solution.py:14
  18.8 20.9 %copy-start.15 = (bf16[64,2048]{1,0:T(8,128)(2,1)}, bf16[64,2048]{1,0:T(8,128)(2,1)S(1)}, u32[]{:S(2)}) copy-start(bf16[64,2048]{1,0:T(8,128)(2,1)S(1)} %collective-permute-done.refs_1_) | copy-start | bytes 786436
  18.8 11.2 %collective-permute-start.5 = (bf16[64,2048]{1,0:T(8,128)(2,1)S(1)}, bf16[64,2048]{1,0:T(8,128)(2,1)S(1)}, u32[]{:S(2)}, u32[]{:S(2)}) collective-permute-start(bf16[64,2048]{1,0:T(8,128)(2,1)S(1)} %collective-permute-done.3.refs_4_), channel_id=1, source_target_pairs={{0,1},{1,2},{2,3},{3,0},{4,5},{5,6},{6,7},{7,4},{8,9},{9,10},{10,1... | collective-permute-start | bytes 786440 | tf_op jit(solution)/shard_map/ppermute | solution.py:14
  20.7 19.0 %copy-start.16 = (bf16[64,2048]{1,0:T(8,128)(2,1)}, bf16[64,2048]{1,0:T(8,128)(2,1)S(1)}, u32[]{:S(2)}) copy-start(bf16[64,2048]{1,0:T(8,128)(2,1)S(1)} %collective-permute-done.7.refs_9_) | copy-start | bytes 786436
  20.7 11.1 %collective-permute-start.11 = (bf16[64,2048]{1,0:T(8,128)(2,1)S(1)}, bf16[64,2048]{1,0:T(8,128)(2,1)S(1)}, u32[]{:S(2)}, u32[]{:S(2)}) collective-permute-start(bf16[64,2048]{1,0:T(8,128)(2,1)S(1)} %collective-permute-done.10.refs_12_), channel_id=1, source_target_pairs={{0,24},{8,0},{16,8},{24,16},{1,25},{9,1},{17,9},{25,17},{2,26},{10... | collective-permute-start | bytes 786440 | tf_op jit(solution)/shard_map/ppermute | solution.py:14
  22.4 17.4 %copy-start.17 = (bf16[64,2048]{1,0:T(8,128)(2,1)}, bf16[64,2048]{1,0:T(8,128)(2,1)S(1)}, u32[]{:S(2)}) copy-start(bf16[64,2048]{1,0:T(8,128)(2,1)S(1)} %collective-permute-done.2.refs_3_) | copy-start | bytes 786436
  22.4 9.6 %collective-permute-start.4 = (bf16[64,2048]{1,0:T(8,128)(2,1)S(1)}, bf16[64,2048]{1,0:T(8,128)(2,1)S(1)}, u32[]{:S(2)}, u32[]{:S(2)}) collective-permute-start(bf16[64,2048]{1,0:T(8,128)(2,1)S(1)} %collective-permute-done.3.refs_4_), channel_id=1, source_target_pairs={{0,3},{1,0},{2,1},{3,2},{4,7},{5,4},{6,5},{7,6},{8,11},{9,8},{10,9... | collective-permute-start | bytes 786440 | tf_op jit(solution)/shard_map/ppermute | solution.py:14
  24.6 44.6 %collective-permute-start.18 = (bf16[1,8,64,2048]{3,2,1,0:T(8,128)(2,1)}, bf16[1,8,64,2048]{3,2,1,0:T(8,128)(2,1)}, u32[]{:S(2)}, u32[]{:S(2)}) collective-permute-start(bf16[1,8,64,2048]{3,2,1,0:T(8,128)(2,1)} %param.8), channel_id=1, source_target_pairs={{32,0},{64,32},{96,64},{0,96},{33,1},{65,33},{97,65},{1,97},{34,2}... | collective-permute-start | bytes 6291464 | tf_op jit(solution)/shard_map/ppermute | solution.py:357
  26.5 8.2 %collective-permute-start.1 = (bf16[64,2048]{1,0:T(8,128)(2,1)S(1)}, bf16[64,2048]{1,0:T(8,128)(2,1)S(1)}, u32[]{:S(2)}, u32[]{:S(2)}) collective-permute-start(bf16[64,2048]{1,0:T(8,128)(2,1)S(1)} %collective-permute-done.refs_1_), channel_id=1, source_target_pairs={{0,3},{1,0},{2,1},{3,2},{4,7},{5,4},{6,5},{7,6},{8,11},{9,8},{10,9... | collective-permute-start | bytes 786440 | tf_op jit(solution)/shard_map/ppermute | solution.py:14
  30.0 6.5 %collective-permute-start.8 = (bf16[64,2048]{1,0:T(8,128)(2,1)S(1)}, bf16[64,2048]{1,0:T(8,128)(2,1)}, u32[]{:S(2)}, u32[]{:S(2)}) collective-permute-start(bf16[64,2048]{1,0:T(8,128)(2,1)S(1)} %collective-permute-done.7.refs_9_), channel_id=1, source_target_pairs={{0,24},{8,0},{16,8},{24,16},{1,25},{9,1},{17,9},{25,17},{2,26},{10... | collective-permute-start | bytes 786440 | tf_op jit(solution)/shard_map/ppermute | solution.py:14
  31.8 7.7 %collective-permute-start.13 = (bf16[64,2048]{1,0:T(8,128)(2,1)S(1)}, bf16[64,2048]{1,0:T(8,128)(2,1)}, u32[]{:S(2)}, u32[]{:S(2)}) collective-permute-start(bf16[64,2048]{1,0:T(8,128)(2,1)S(1)} %collective-permute-done.12.refs_15_), channel_id=1, source_target_pairs={{0,8},{8,16},{16,24},{24,0},{1,9},{9,17},{17,25},{25,1},{2,10},{10... | collective-permute-start | bytes 786440 | tf_op jit(solution)/shard_map/ppermute | solution.py:14
  32.0 7.7 %collective-permute-start.6 = (bf16[64,2048]{1,0:T(8,128)(2,1)S(1)}, bf16[64,2048]{1,0:T(8,128)(2,1)}, u32[]{:S(2)}, u32[]{:S(2)}) collective-permute-start(bf16[64,2048]{1,0:T(8,128)(2,1)S(1)} %collective-permute-done.5.refs_7_), channel_id=1, source_target_pairs={{0,1},{1,2},{2,3},{3,0},{4,5},{5,6},{6,7},{7,4},{8,9},{9,10},{10,1... | collective-permute-start | bytes 786440 | tf_op jit(solution)/shard_map/ppermute | solution.py:14
  44.8 45.1 %collective-permute-start.14 = (bf16[2,4,64,2048]{3,2,1,0:T(8,128)(2,1)}, bf16[2,4,64,2048]{3,2,1,0:T(8,128)(2,1)S(1)}, u32[]{:S(2)}, u32[]{:S(2)}) collective-permute-start(bf16[2,4,64,2048]{3,2,1,0:T(8,128)(2,1)} %get-tuple-element.26.refs_0_.refs_2_), channel_id=1, source_target_pairs={{0,24},{8,0},{16,8},{24,16},{1,25},{9,1},{17,9},{25,17},{2,26},{10... | collective-permute-start | bytes 6291464 | tf_op jit(solution)/shard_map/ppermute | solution.py:14
  47.8 45.5 %collective-permute-start.15 = (bf16[2,4,64,2048]{3,2,1,0:T(8,128)(2,1)}, bf16[2,4,64,2048]{3,2,1,0:T(8,128)(2,1)}, u32[]{:S(2)}, u32[]{:S(2)}) collective-permute-start(bf16[2,4,64,2048]{3,2,1,0:T(8,128)(2,1)} %get-tuple-element.26.refs_0_.refs_2_), channel_id=1, source_target_pairs={{0,8},{8,16},{16,24},{24,0},{1,9},{9,17},{17,25},{25,1},{2,10},{10... | collective-permute-start | bytes 6291464 | tf_op jit(solution)/shard_map/ppermute | solution.py:14
  47.8 45.5 %collective-permute-start.16 = (bf16[2,4,64,2048]{3,2,1,0:T(8,128)(2,1)}, bf16[2,4,64,2048]{3,2,1,0:T(8,128)(2,1)}, u32[]{:S(2)}, u32[]{:S(2)}) collective-permute-start(bf16[2,4,64,2048]{3,2,1,0:T(8,128)(2,1)} %get-tuple-element.27.refs_3_.refs_5_.refs_7_), channel_id=1, source_target_pairs={{0,3},{1,0},{2,1},{3,2},{4,7},{5,4},{6,5},{7,6},{8,11},{9,8},{10,9... | collective-permute-start | bytes 6291464 | tf_op jit(solution)/shard_map/ppermute | solution.py:14
  47.8 45.5 %collective-permute-start.17 = (bf16[2,4,64,2048]{3,2,1,0:T(8,128)(2,1)}, bf16[2,4,64,2048]{3,2,1,0:T(8,128)(2,1)}, u32[]{:S(2)}, u32[]{:S(2)}) collective-permute-start(bf16[2,4,64,2048]{3,2,1,0:T(8,128)(2,1)} %get-tuple-element.27.refs_3_.refs_5_.refs_7_), channel_id=1, source_target_pairs={{0,1},{1,2},{2,3},{3,0},{4,5},{5,6},{6,7},{7,4},{8,9},{9,10},{10,1... | collective-permute-start | bytes 6291464 | tf_op jit(solution)/shard_map/ppermute | solution.py:14
  97.6 21.1 %collective-permute-start.19 = (bf16[4,64,2048]{2,1,0:T(8,128)(2,1)}, bf16[4,64,2048]{2,1,0:T(8,128)(2,1)S(1)}, u32[]{:S(2)}, u32[]{:S(2)}) collective-permute-start(bf16[4,64,2048]{2,1,0:T(8,128)(2,1)} %get-tuple-element.28), channel_id=1, source_target_pairs={{0,24},{8,0},{16,8},{24,16},{1,25},{9,1},{17,9},{25,17},{2,26},{10... | collective-permute-start | bytes 3145736 | tf_op jit(solution)/shard_map/ppermute | solution.py:14
  100.6 21.4 %collective-permute-start.20 = (bf16[4,64,2048]{2,1,0:T(8,128)(2,1)}, bf16[4,64,2048]{2,1,0:T(8,128)(2,1)S(1)}, u32[]{:S(2)}, u32[]{:S(2)}) collective-permute-start(bf16[4,64,2048]{2,1,0:T(8,128)(2,1)} %get-tuple-element.29), channel_id=1, source_target_pairs={{0,8},{8,16},{16,24},{24,0},{1,9},{9,17},{17,25},{25,1},{2,10},{10... | collective-permute-start | bytes 3145736 | tf_op jit(solution)/shard_map/ppermute | solution.py:14
  100.6 21.4 %collective-permute-start.21 = (bf16[4,64,2048]{2,1,0:T(8,128)(2,1)}, bf16[4,64,2048]{2,1,0:T(8,128)(2,1)S(1)}, u32[]{:S(2)}, u32[]{:S(2)}) collective-permute-start(bf16[4,64,2048]{2,1,0:T(8,128)(2,1)} %get-tuple-element.30), channel_id=1, source_target_pairs={{0,3},{1,0},{2,1},{3,2},{4,7},{5,4},{6,5},{7,6},{8,11},{9,8},{10,9... | collective-permute-start | bytes 3145736 | tf_op jit(solution)/shard_map/ppermute | solution.py:14
  100.9 21.5 %collective-permute-start.22 = (bf16[4,64,2048]{2,1,0:T(8,128)(2,1)}, bf16[4,64,2048]{2,1,0:T(8,128)(2,1)}, u32[]{:S(2)}, u32[]{:S(2)}) collective-permute-start(bf16[4,64,2048]{2,1,0:T(8,128)(2,1)} %get-tuple-element.31), channel_id=1, source_target_pairs={{0,1},{1,2},{2,3},{3,0},{4,5},{5,6},{6,7},{7,4},{8,9},{9,10},{10,1... | collective-permute-start | bytes 3145736 | tf_op jit(solution)/shard_map/ppermute | solution.py:14
  123.3 30.4 %all-to-all-start.1 = ((bf16[32,64,512]{2,1,0:T(8,128)(2,1)}), bf16[32,64,512]{2,1,0:T(8,128)(2,1)S(1)}, u32[]{:S(2)}, u32[]{:S(2)}) async-start(bf16[32,64,512]{2,1,0:T(8,128)(2,1)} %hold.1), calls=%async_computation.1 | async-start | bytes 4194304 | tf_op jit(solution)/shard_map/all_to_all | solution.py:366
  155.1 56.2 %all-to-all-start = ((bf16[32,8,64,128]{3,2,1,0:T(8,128)(2,1)}), bf16[32,8,64,128]{3,2,1,0:T(8,128)(2,1)}, u32[]{:S(2)}, u32[]{:S(2)}) async-start(bf16[32,8,64,128]{3,2,1,0:T(8,128)(2,1)} %absorb.1), calls=%async_computation | async-start | bytes 8388608 | tf_op jit(solution)/shard_map/all_to_all | solution.py:368
  211.3 16.9 %copy-start.5 = (s32[3]{0:T(128)S(1)}, s32[3]{0:T(128)}, u32[]{:S(2)}) copy-start(s32[3]{0:T(128)} %pad_add_fusion.at_ref.refs_0_) | copy-start | bytes 40
  231.6 10.7 %collective-permute-start.30 = (bf16[256,1024]{1,0:T(8,128)(2,1)S(1)}, bf16[256,1024]{1,0:T(8,128)(2,1)S(1)}, u32[]{:S(2)}, u32[]{:S(2)}) collective-permute-start(bf16[256,1024]{1,0:T(8,128)(2,1)S(1)} %get-tuple-element.45), channel_id=1, source_target_pairs={{0,1},{1,2},{2,3},{3,0},{4,5},{5,6},{6,7},{7,4},{8,9},{9,10},{10,1... | collective-permute-start | bytes 1572872 | tf_op jit(solution)/shard_map/ppermute | solution.py:14
  231.7 11.0 %collective-permute-start.32 = (bf16[256,1024]{1,0:T(8,128)(2,1)S(1)}, bf16[256,1024]{1,0:T(8,128)(2,1)S(1)}, u32[]{:S(2)}, u32[]{:S(2)}) collective-permute-start(bf16[256,1024]{1,0:T(8,128)(2,1)S(1)} %get-tuple-element.49), channel_id=1, source_target_pairs={{0,3},{1,0},{2,1},{3,2},{4,7},{5,4},{6,5},{7,6},{8,11},{9,8},{10,9... | collective-permute-start | bytes 1572872 | tf_op jit(solution)/shard_map/ppermute | solution.py:14
  238.9 12.0 %collective-permute-start.23 = (bf16[256,1024]{1,0:T(8,128)(2,1)S(1)}, bf16[256,1024]{1,0:T(8,128)(2,1)S(1)}, u32[]{:S(2)}, u32[]{:S(2)}) collective-permute-start(bf16[256,1024]{1,0:T(8,128)(2,1)S(1)} %get-tuple-element.37), channel_id=1, source_target_pairs={{0,8},{8,16},{16,24},{24,0},{1,9},{9,17},{17,25},{25,1},{2,10},{10... | collective-permute-start | bytes 1572872 | tf_op jit(solution)/shard_map/ppermute | solution.py:14
  239.6 13.0 %collective-permute-start.25 = (bf16[256,1024]{1,0:T(8,128)(2,1)S(1)}, bf16[256,1024]{1,0:T(8,128)(2,1)S(1)}, u32[]{:S(2)}, u32[]{:S(2)}) collective-permute-start(bf16[256,1024]{1,0:T(8,128)(2,1)S(1)} %get-tuple-element.41), channel_id=1, source_target_pairs={{0,24},{8,0},{16,8},{24,16},{1,25},{9,1},{17,9},{25,17},{2,26},{10... | collective-permute-start | bytes 1572872 | tf_op jit(solution)/shard_map/ppermute | solution.py:14
  242.6 22.7 %collective-permute-start.31 = (bf16[2,256,1024]{2,1,0:T(8,128)(2,1)S(1)}, bf16[2,256,1024]{2,1,0:T(8,128)(2,1)}, u32[]{:S(2)}, u32[]{:S(2)}) collective-permute-start(bf16[2,256,1024]{2,1,0:T(8,128)(2,1)S(1)} %pad_maximum_fusion.2), channel_id=1, source_target_pairs={{0,1},{1,2},{2,3},{3,0},{4,5},{5,6},{6,7},{7,4},{8,9},{9,10},{10,1... | collective-permute-start | bytes 3145736 | tf_op jit(solution)/shard_map/ppermute | solution.py:14
  244.1 22.1 %collective-permute-start.33 = (bf16[2,256,1024]{2,1,0:T(8,128)(2,1)}, bf16[2,256,1024]{2,1,0:T(8,128)(2,1)}, u32[]{:S(2)}, u32[]{:S(2)}) collective-permute-start(bf16[2,256,1024]{2,1,0:T(8,128)(2,1)} %pad_maximum_fusion.3), channel_id=1, source_target_pairs={{0,3},{1,0},{2,1},{3,2},{4,7},{5,4},{6,5},{7,6},{8,11},{9,8},{10,9... | collective-permute-start | bytes 3145736 | tf_op jit(solution)/shard_map/ppermute | solution.py:14
  252.2 25.7 %collective-permute-start.24 = (bf16[2,256,1024]{2,1,0:T(8,128)(2,1)}, bf16[2,256,1024]{2,1,0:T(8,128)(2,1)}, u32[]{:S(2)}, u32[]{:S(2)}) collective-permute-start(bf16[2,256,1024]{2,1,0:T(8,128)(2,1)} %pad_maximum_fusion), channel_id=1, source_target_pairs={{0,8},{8,16},{16,24},{24,0},{1,9},{9,17},{17,25},{25,1},{2,10},{10... | collective-permute-start | bytes 3145736 | tf_op jit(solution)/shard_map/ppermute | solution.py:14
  253.9 24.3 %collective-permute-start.26 = (bf16[2,256,1024]{2,1,0:T(8,128)(2,1)}, bf16[2,256,1024]{2,1,0:T(8,128)(2,1)}, u32[]{:S(2)}, u32[]{:S(2)}) collective-permute-start(bf16[2,256,1024]{2,1,0:T(8,128)(2,1)} %pad_maximum_fusion.1), channel_id=1, source_target_pairs={{0,24},{8,0},{16,8},{24,16},{1,25},{9,1},{17,9},{25,17},{2,26},{10... | collective-permute-start | bytes 3145736 | tf_op jit(solution)/shard_map/ppermute | solution.py:14
  269.1 15.4 %collective-permute-start.34 = (bf16[2,64,1024]{2,1,0:T(8,128)(2,1)S(1)}, bf16[2,64,1024]{2,1,0:T(8,128)(2,1)}, u32[]{:S(2)}, u32[]{:S(2)}) collective-permute-start(bf16[2,64,1024]{2,1,0:T(8,128)(2,1)S(1)} %get-tuple-element.50), channel_id=1, source_target_pairs={{0,8},{8,16},{16,24},{24,0},{1,9},{9,17},{17,25},{25,1},{2,10},{10... | collective-permute-start | bytes 786440 | tf_op jit(solution)/shard_map/ppermute | solution.py:14
  274.4 11.6 %collective-permute-start.35 = (bf16[2,64,1024]{2,1,0:T(8,128)(2,1)}, bf16[2,64,1024]{2,1,0:T(8,128)(2,1)}, u32[]{:S(2)}, u32[]{:S(2)}) collective-permute-start(bf16[2,64,1024]{2,1,0:T(8,128)(2,1)} %get-tuple-element.52), channel_id=1, source_target_pairs={{0,24},{8,0},{16,8},{24,16},{1,25},{9,1},{17,9},{25,17},{2,26},{10... | collective-permute-start | bytes 786440 | tf_op jit(solution)/shard_map/ppermute | solution.py:14
  274.4 11.9 %collective-permute-start.36 = (bf16[2,64,1024]{2,1,0:T(8,128)(2,1)S(1)}, bf16[2,64,1024]{2,1,0:T(8,128)(2,1)}, u32[]{:S(2)}, u32[]{:S(2)}) collective-permute-start(bf16[2,64,1024]{2,1,0:T(8,128)(2,1)S(1)} %get-tuple-element.51), channel_id=1, source_target_pairs={{0,16},{8,24},{16,0},{24,8},{1,17},{9,25},{17,1},{25,9},{2,18},{10... | collective-permute-start | bytes 786440 | tf_op jit(solution)/shard_map/ppermute | solution.py:14
  281.1 9.9 %collective-permute-start.27 = (bf16[2,64,1024]{2,1,0:T(8,128)(2,1)}, bf16[2,64,1024]{2,1,0:T(8,128)(2,1)S(1)}, u32[]{:S(2)}, u32[]{:S(2)}) collective-permute-start(bf16[2,64,1024]{2,1,0:T(8,128)(2,1)} %get-tuple-element.53), channel_id=1, source_target_pairs={{0,1},{1,2},{2,3},{3,0},{4,5},{5,6},{6,7},{7,4},{8,9},{9,10},{10,1... | collective-permute-start | bytes 786440 | tf_op jit(solution)/shard_map/ppermute | solution.py:14
  281.1 10.6 %collective-permute-start.28 = (bf16[2,64,1024]{2,1,0:T(8,128)(2,1)S(1)}, bf16[2,64,1024]{2,1,0:T(8,128)(2,1)}, u32[]{:S(2)}, u32[]{:S(2)}) collective-permute-start(bf16[2,64,1024]{2,1,0:T(8,128)(2,1)S(1)} %get-tuple-element.55), channel_id=1, source_target_pairs={{0,3},{1,0},{2,1},{3,2},{4,7},{5,4},{6,5},{7,6},{8,11},{9,8},{10,9... | collective-permute-start | bytes 786440 | tf_op jit(solution)/shard_map/ppermute | solution.py:14
  284.5 9.4 %collective-permute-start.29 = (bf16[2,64,1024]{2,1,0:T(8,128)(2,1)S(1)}, bf16[2,64,1024]{2,1,0:T(8,128)(2,1)}, u32[]{:S(2)}, u32[]{:S(2)}) collective-permute-start(bf16[2,64,1024]{2,1,0:T(8,128)(2,1)S(1)} %get-tuple-element.54), channel_id=1, source_target_pairs={{0,2},{1,3},{2,0},{3,1},{4,6},{5,7},{6,4},{7,5},{8,10},{9,11},{10,... | collective-permute-start | bytes 786440 | tf_op jit(solution)/shard_map/ppermute | solution.py:14
  295.1 8.0 %collective-permute-start.37 = (bf16[64,2048]{1,0:T(8,128)(2,1)S(1)}, bf16[64,2048]{1,0:T(8,128)(2,1)S(1)}, u32[]{:S(2)}, u32[]{:S(2)}) collective-permute-start(bf16[64,2048]{1,0:T(8,128)(2,1)S(1)} %fusion.13), channel_id=1, source_target_pairs={{0,4},{4,0},{1,5},{5,1},{2,6},{6,2},{3,7},{7,3},{8,12},{12,8},{9,1... | collective-permute-start | bytes 786440 | tf_op jit(solution)/shard_map/ppermute | solution.py:14
  (17 other events, 114.5 us)

commit v3 on v2

--- a/solution.py
+++ b/solution.py
@@ -18,18 +18,32 @@
     return lax.dot_general(a, b, (dims, ((), ())), preferred_element_type=F32)
 
 
+def relay(source, target, held, sem, out_sem, n):
+    return (
+        pltpu.make_async_copy(source, held.at[n], sem.at[n]),
+        pltpu.make_async_copy(held.at[n], target, out_sem.at[n]),
+    )
+
+
+def run_relays(relays):
+    for inward, _ in relays:
+        inward.start()
+    for inward, outward in relays:
+        inward.wait()
+        outward.start()
+    for _, outward in relays:
+        outward.wait()
+
+
 def collect_kernel(at_ref, *refs):
-    ins, outs, sem = refs[:16], refs[16:18], refs[18]
+    ins, outs, (held, sem, out_sem) = refs[:16], refs[16:18], refs[18:]
     copies = []
     for state in range(2):
         own = at_ref[2] if state == 0 else at_ref[0]
         for n, (plane, distance) in enumerate([(p, d) for p in range(2) for d in range(4)]):
             where = outs[state].at[lax.rem(plane + at_ref[1], 2), lax.rem(own + distance, 4)]
-            copies.append(pltpu.make_async_copy(ins[8 * state + n], where, sem.at[8 * state + n]))
-    for copy in copies:
-        copy.start()
-    for copy in copies:
-        copy.wait()
+            copies.append(relay(ins[8 * state + n], where, held, sem, out_sem, 8 * state + n))
+    run_relays(copies)
 
 
 def collect(at, blocks):
@@ -38,8 +52,12 @@
         collect_kernel,
         out_shape=(shape,) * 2,
         in_specs=[pl.BlockSpec(memory_space=pltpu.SMEM)] + [pl.BlockSpec(memory_space=pl.ANY)] * 16,
-        out_specs=(pl.BlockSpec(memory_space=pltpu.VMEM),) * 2,
-        scratch_shapes=[pltpu.SemaphoreType.DMA((16,))],
+        out_specs=(pl.BlockSpec(memory_space=pl.ANY),) * 2,
+        scratch_shapes=[
+            pltpu.VMEM((16,) + blocks[0].shape, blocks[0].dtype),
+            pltpu.SemaphoreType.DMA((16,)),
+            pltpu.SemaphoreType.DMA((16,)),
+        ],
         compiler_params=pltpu.CompilerParams(vmem_limit_bytes=VMEM_LIMIT),
         cost_estimate=pl.CostEstimate(flops=0, bytes_accessed=8 << 20, transcendentals=0),
         name="collect",
@@ -55,12 +73,9 @@
 
 
 def halves_kernel(*refs):
-    outs, sem = refs[-5:-1], refs[-1]
-    copies = [pltpu.make_async_copy(refs[n].at[n % 2], outs[n], sem.at[n]) for n in range(4)]
-    for copy in copies:
-        copy.start()
-    for copy in copies:
-        copy.wait()
+    outs, (held, sem, out_sem) = refs[-7:-3], refs[-3:]
+    parts = [(n, z) for n in range(4) for z in range(4)]
+    run_relays([relay(refs[n].at[n % 2, z], outs[n].at[z], held, sem, out_sem, 4 * n + z) for n, z in parts])
 
 
 def halves(blocks, before):
@@ -69,8 +84,12 @@
         halves_kernel,
         out_shape=(shape,) * 4,
         in_specs=[pl.BlockSpec(memory_space=pl.ANY)] * (4 + len(before)),
-        out_specs=(pl.BlockSpec(memory_space=pltpu.VMEM),) * 4,
-        scratch_shapes=[pltpu.SemaphoreType.DMA((4,))],
+        out_specs=(pl.BlockSpec(memory_space=pl.ANY),) * 4,
+        scratch_shapes=[
+            pltpu.VMEM((16,) + blocks[0].shape[2:], blocks[0].dtype),
+            pltpu.SemaphoreType.DMA((16,)),
+            pltpu.SemaphoreType.DMA((16,)),
+        ],
         compiler_params=pltpu.CompilerParams(vmem_limit_bytes=VMEM_LIMIT),
         cost_estimate=pl.CostEstimate(flops=0, bytes_accessed=8 << 20, transcendentals=0),
         name="halves",

time: 309 us -> 308 us (level)
  transfers between devices with their start and end apart: 40 -> 40, of which waited for: 22 -> 21; matrix products, arithmetic and copies ran while one was open for 12% -> 12% of each run, Pallas kernels for 17% -> 17%
where the time goes in v3:
time: 308 us; the launch traced here: 303 us
  waiting for transfers between devices  110 us (36%)
  starting transfers between devices  76.4 us (25%)
  Pallas kernels  73.5 us (24%)
  local copies, waits for them, and re-layouts  29.8 us (10%)
  other arithmetic  12.3 us (4%)
    ppermute x37, starting transfers between devices, hop(): lax.ppermute(block, axis, [(i, (i + distance) % n) for i in range(n)])  63.8 us
    ppermute x37, waiting for transfers between devices, hop(): lax.ppermute(block, axis, [(i, (i + distance) % n) for i in range(n)])  56.7 us
    all_to_all x1, waiting for transfers between devices, local(): lax.all_to_all(carried, sector, split_axis=0, concat_axis=0, tiled=True)  47.6 us
    pallas_call x1, Pallas kernels, step(): pl.pallas_call(step_kernel, out_shape=(jax.ShapeDtypeStruct((rows, column...  16.9 us
    pallas_call x1, Pallas kernels, absorb(): pl.pallas_call(absorb_kernel, out_shape=jax.ShapeDtypeStruct((columns //...  16.7 us
    pallas_call x1, Pallas kernels, begin(): pl.pallas_call(begin_kernel, out_shape=jax.ShapeDtypeStruct((2, rows, col...  14.8 us
    pallas_call x1, Pallas kernels, bond_right(): pl.pallas_call(bond_kernel, out_shape=jax.ShapeDtypeStruct((k // 64, rows...  11 us
    another operation x1, local copies, waits for them, and re-layouts, local(): first.reshape(w * rows, 4, 2, 4, 64).transpose(0, 3, 2, 1, 4)  8.44 us
  transfers between devices with their start and end apart: 40, of which 21 were waited for; matrix products, arithmetic and copies ran while one was open for 12% of the time, Pallas kernels for 17%

profile of v3, /device:TPU:0, one launch (start us, length us, event | category | flops | bytes accessed | tf_op | source)
XLA Modules:
  0.0 303.3 jit_solution(18002556273642423917)
XLA Ops:
  1.9 3.2 %collective-permute-start.10 = (bf16[64,2048]{1,0:T(8,128)(2,1)S(1)}, bf16[64,2048]{1,0:T(8,128)(2,1)S(1)}, u32[]{:S(2)}, u32[]{:S(2)}) collective-permute-start(bf16[64,2048]{1,0:T(8,128)(2,1)S(1)} %get-tuple-element.56.refs_8_), channel_id=1, source_target_pairs={{0,4},{4,0},{1,5},{5,1},{2,6},{6,2},{3,7},{7,3},{8,12},{12,8},{9,1... | collective-permute-start | bytes 786440 | tf_op jit(solution)/shard_map/ppermute | solution.py:14
  5.5 4.1 %collective-permute-start = (bf16[64,2048]{1,0:T(8,128)(2,1)S(1)}, bf16[64,2048]{1,0:T(8,128)(2,1)S(1)}, u32[]{:S(2)}, u32[]{:S(2)}) collective-permute-start(bf16[64,2048]{1,0:T(8,128)(2,1)S(1)} %get-tuple-element.57.refs_0_), channel_id=1, source_target_pairs={{0,3},{1,0},{2,1},{3,2},{4,7},{5,4},{6,5},{7,6},{8,11},{9,8},{10,9... | collective-permute-start | bytes 786440 | tf_op jit(solution)/shard_map/ppermute | solution.py:14
  9.6 3.0 collective-permute-start.7
  14.3 2.7 collective-permute-done.3.refs_4_
  17.0 1.8 collective-permute-start.12
  18.8 1.9 collective-permute-start.5
  22.4 2.2 collective-permute-start.4
  24.6 1.9 collective-permute-done.12.refs_15_
  26.5 3.5 %collective-permute-start.1 = (bf16[64,2048]{1,0:T(8,128)(2,1)S(1)}, bf16[64,2048]{1,0:T(8,128)(2,1)S(1)}, u32[]{:S(2)}, u32[]{:S(2)}) collective-permute-start(bf16[64,2048]{1,0:T(8,128)(2,1)S(1)} %collective-permute-done.refs_1_), channel_id=1, source_target_pairs={{0,3},{1,0},{2,1},{3,2},{4,7},{5,4},{6,5},{7,6},{8,11},{9,8},{10,9... | collective-permute-start | bytes 786440 | tf_op jit(solution)/shard_map/ppermute | solution.py:14
  30.0 1.8 collective-permute-start.8
  34.7 1.8 collective-permute-done.8.refs_10_
  36.5 3.0 collective-permute-done.13.refs_14_
  39.8 4.5 %collect.1 = (bf16[2,4,64,2048]{3,2,1,0:T(8,128)(2,1)}, bf16[2,4,64,2048]{3,2,1,0:T(8,128)(2,1)}) custom-call(s32[3]{0:T(128)} %pad_add_fusion.at_ref.refs_0_, bf16[64,2048]{1,0:T(8,128)(2,1)} %copy-done.12, bf16[64,2048]{1,0:T(8,128)(2,1)} %copy-done.15, bf16[64,2048]{1,0:T(8,128)(2,1)} %copy-done.23, bf16[64,2048]{1,0:T(8,128)(2,1)} %copy-done.17, ...), custom_call_target="tpu_custom_call" | custom-call | bytes 8388608 | tf_op jit(solution)/shard_map/collect/pallas_call | solution.py:51
  44.4 3.1 %collective-permute-start.14 = (bf16[2,4,64,2048]{3,2,1,0:T(8,128)(2,1)}, bf16[2,4,64,2048]{3,2,1,0:T(8,128)(2,1)S(1)}, u32[]{:S(2)}, u32[]{:S(2)}) collective-permute-start(bf16[2,4,64,2048]{3,2,1,0:T(8,128)(2,1)} %get-tuple-element.26.refs_0_.refs_2_), channel_id=1, source_target_pairs={{0,24},{8,0},{16,8},{24,16},{1,25},{9,1},{17,9},{25,17},{2,26},{10... | collective-permute-start | bytes 6291464 | tf_op jit(solution)/shard_map/ppermute | solution.py:14
  47.5 2.0 collective-permute-start.17
  49.5 8.4 %reshape.54 = bf16[512,4,2,4,64]{4,3,2,1,0:T(4,128)(2,1)} reshape(bf16[1,8,64,2048]{3,2,1,0:T(8,128)(2,1)} %param.5) | data formatting | bytes 4194304 | tf_op jit(solution)/shard_map/reshape;reshape | solution.py:380
  57.9 6.9 %copy.22 = bf16[512,4,2,4,64]{0,4,1,2,3:T(8,128)(2,1)} copy(bf16[512,4,2,4,64]{4,3,2,1,0:T(4,128)(2,1)} %reshape.54) | data formatting | bytes 4194304 | tf_op jit(solution)/shard_map/transpose | solution.py:380
  64.9 3.9 %copy.18.second_ref.refs_5_ = bf16[512,2048]{1,0:T(8,128)(2,1)} copy(bf16[512,2048]{0,1:T(8,128)(2,1)} %bitcast.87) | data formatting | bytes 4194304 | tf_op jit(solution)/shard_map/reshape | solution.py:380
  68.8 11.0 %bond_right.1.refs_4_.refs_0_ = bf16[32,64,512]{2,1,0:T(8,128)(2,1)} custom-call(bf16[512,2048]{1,0:T(8,128)(2,1)} %bitcast.12.r_ref, bf16[2048,2048]{1,0:T(8,128)(2,1)} %bitcast.94), custom_call_target="tpu_custom_call" | custom-call | flops 4294967296 | bytes 12582912 | tf_op jit(solution)/shard_map/bond_right/pallas_call | solution.py:141
  79.8 9.8 %collective-permute-done.14.refs_1_.refs_0_.refs_3_ = bf16[2,4,64,2048]{3,2,1,0:T(8,128)(2,1)S(1)} collective-permute-done((bf16[2,4,64,2048]{3,2,1,0:T(8,128)(2,1)}, bf16[2,4,64,2048]{3,2,1,0:T(8,128)(2,1)S(1)}, u32[]{:S(2)}, u32[]{:S(2)}) %collective-permute-start.14) | collective-permute-done | bytes 2097184 | tf_op jit(solution)/shard_map/ppermute | solution.py:14
  89.5 3.4 %collective-permute-done.15.refs_2_.refs_1_.refs_4_ = bf16[2,4,64,2048]{3,2,1,0:T(8,128)(2,1)} collective-permute-done((bf16[2,4,64,2048]{3,2,1,0:T(8,128)(2,1)}, bf16[2,4,64,2048]{3,2,1,0:T(8,128)(2,1)}, u32[]{:S(2)}, u32[]{:S(2)}) %collective-permute-start.15) | collective-permute-done | bytes 2097184 | tf_op jit(solution)/shard_map/ppermute | solution.py:14
  93.0 3.9 %halves.1 = (bf16[4,64,2048]{2,1,0:T(8,128)(2,1)}, bf16[4,64,2048]{2,1,0:T(8,128)(2,1)}, bf16[4,64,2048]{2,1,0:T(8,128)(2,1)}, bf16[4,64,2048]{2,1,0:T(8,128)(2,1)}) custom-call(bf16[2,4,64,2048]{3,2,1,0:T(8,128)(2,1)} %copy-done.6, bf16[2,4,64,2048]{3,2,1,0:T(8,128)(2,1)} %collective-permute-done.15.refs_2_.refs_1_.refs_4_, ...), custom_call_target="tpu_custom_call" | custom-call | bytes 8388608 | tf_op jit(solution)/shard_map/halves/pallas_call | solution.py:83
  96.8 3.0 collective-permute-start.19
  101.9 14.8 %begin.1.part_ref.refs_1_ = f32[2,512,2048]{2,1,0:T(8,128)} custom-call(s32[3]{0:T(128)} %pad_add_fusion.at_ref.refs_0_, bf16[512,2048]{1,0:T(8,128)(2,1)} %bitcast.85, bf16[512,2048]{1,0:T(8,128)(2,1)} %copy.18.second_ref.refs_5_, bf16[2,4,64,2048]{3,2,1,0:T(8,128)(2,1)} %get-tuple-element.26.refs_0_.refs_2_, bf16[2,4,64,2048]{3,2,1,0:T(8,128)(2,1)} %copy-done.6, ...), custom_call_target="tpu_custom_call" | custom-call | flops 6442450944 | bytes 25165824 | tf_op jit(solution)/shard_map/begin/pallas_call | solution.py:178
  118.0 3.3 %collective-permute-done.20.refs_1_.refs_4_.refs_6_ = bf16[4,64,2048]{2,1,0:T(8,128)(2,1)S(1)} collective-permute-done((bf16[4,64,2048]{2,1,0:T(8,128)(2,1)}, bf16[4,64,2048]{2,1,0:T(8,128)(2,1)S(1)}, u32[]{:S(2)}, u32[]{:S(2)}) %collective-permute-start.20) | collective-permute-done | bytes 1048608 | tf_op jit(solution)/shard_map/ppermute | solution.py:14
  122.6 6.9 %all-to-all-start.1 = ((bf16[32,64,512]{2,1,0:T(8,128)(2,1)}), bf16[32,64,512]{2,1,0:T(8,128)(2,1)S(1)}, u32[]{:S(2)}, u32[]{:S(2)}) async-start(bf16[32,64,512]{2,1,0:T(8,128)(2,1)} %hold.1), calls=%async_computation.1 | async-start | bytes 4194304 | tf_op jit(solution)/shard_map/all_to_all | solution.py:385
  130.4 16.7 %absorb.1 = bf16[32,8,64,128]{3,2,1,0:T(8,128)(2,1)} custom-call(s32[3]{0:T(128)} %pad_add_fusion.at_ref.refs_0_, f32[256]{0:T(256)} %reshape_squeeze.6.m_ref, bf16[512,2048]{1,0:T(8,128)(2,1)} %bitcast.86, bf16[512,2048]{1,0:T(8,128)(2,1)} %copy.18.second_ref.refs_5_, f32[2,512,2048]{2,1,0:T(8,128)} %begin.1.part_ref.refs_1_, ...), custom_call_target="tpu_custom_call" | custom-call | flops 2147483648 | bytes 20971520 | tf_op jit(solution)/shard_map/absorb/pallas_call | solution.py:234
  147.0 6.0 %all-to-all-done.1 = bf16[32,64,512]{2,1,0:T(8,128)(2,1)S(1)} async-done(((bf16[32,64,512]{2,1,0:T(8,128)(2,1)}), bf16[32,64,512]{2,1,0:T(8,128)(2,1)S(1)}, u32[]{:S(2)}, u32[]{:S(2)}) %all-to-all-start.1) | async-done | bytes 2097184 | tf_op jit(solution)/shard_map/all_to_all | solution.py:385
  154.3 5.7 %all-to-all-start = ((bf16[32,8,64,128]{3,2,1,0:T(8,128)(2,1)}), bf16[32,8,64,128]{3,2,1,0:T(8,128)(2,1)}, u32[]{:S(2)}, u32[]{:S(2)}) async-start(bf16[32,8,64,128]{3,2,1,0:T(8,128)(2,1)} %absorb.1), calls=%async_computation | async-start | bytes 8388608 | tf_op jit(solution)/shard_map/all_to_all | solution.py:387
  160.0 2.9 copy.19
  163.0 47.6 %all-to-all-done = bf16[32,8,64,128]{3,2,1,0:T(8,128)(2,1)} async-done(((bf16[32,8,64,128]{3,2,1,0:T(8,128)(2,1)}), bf16[32,8,64,128]{3,2,1,0:T(8,128)(2,1)}, u32[]{:S(2)}, u32[]{:S(2)}) %all-to-all-start) | async-done | bytes 4194336 | tf_op jit(solution)/shard_map/all_to_all | solution.py:387
  210.6 16.9 %step.1 = (bf16[512,2048]{1,0:T(8,128)(2,1)}, bf16[2048,512]{1,0:T(8,128)(2,1)}) custom-call(s32[3]{0:T(128)} %pad_add_fusion.at_ref.refs_0_, bf16[32,512,128]{2,1,0:T(8,128)(2,1)} %bitcast.14.c_ref, bf16[2,4,64,2048]{3,2,1,0:T(8,128)(2,1)} %get-tuple-element.26.refs_0_.refs_2_, bf16[2,4,64,2048]{3,2,1,0:T(8,128)(2,1)} %copy-done.6, ...), custom_call_target="tpu_custom_call" | custom-call | flops 8589934592 | bytes 25165824 | tf_op jit(solution)/shard_map/step/pallas_call | solution.py:291
  229.1 1.8 terms_1.1
  231.0 3.2 %collective-permute-start.32 = (bf16[256,1024]{1,0:T(8,128)(2,1)S(1)}, bf16[256,1024]{1,0:T(8,128)(2,1)S(1)}, u32[]{:S(2)}, u32[]{:S(2)}) collective-permute-start(bf16[256,1024]{1,0:T(8,128)(2,1)S(1)} %get-tuple-element.49), channel_id=1, source_target_pairs={{0,3},{1,0},{2,1},{3,2},{4,7},{5,4},{6,5},{7,6},{8,11},{9,8},{10,9... | collective-permute-start | bytes 1572872 | tf_op jit(solution)/shard_map/ppermute | solution.py:14
  234.2 4.0 %terms_3.1 = (bf16[256,1024]{1,0:T(8,128)(2,1)S(1)}, bf16[256,1024]{1,0:T(8,128)(2,1)S(1)}, bf16[256,1024]{1,0:T(8,128)(2,1)S(1)}, bf16[256,1024]{1,0:T(8,128)(2...) custom-call(s32[3]{0:T(128)S(1)} %copy-done.5, ...), custom_call_target="tpu_custom_call" | custom-call | flops 3221225472 | bytes 6291456 | tf_op jit(solution)/shard_map/terms_3/pallas_call | solution.py:329
  238.9 2.7 collective-permute-start.25
  243.5 3.2 %collective-permute-start.33 = (bf16[2,256,1024]{2,1,0:T(8,128)(2,1)}, bf16[2,256,1024]{2,1,0:T(8,128)(2,1)}, u32[]{:S(2)}, u32[]{:S(2)}) collective-permute-start(bf16[2,256,1024]{2,1,0:T(8,128)(2,1)} %pad_maximum_fusion.3), channel_id=1, source_target_pairs={{0,3},{1,0},{2,1},{3,2},{4,7},{5,4},{6,5},{7,6},{8,11},{9,8},{10,9... | collective-permute-start | bytes 3145736 | tf_op jit(solution)/shard_map/ppermute | solution.py:14
  246.7 3.4 %collective-permute-done.23 = bf16[256,1024]{1,0:T(8,128)(2,1)S(1)} collective-permute-done((bf16[256,1024]{1,0:T(8,128)(2,1)S(1)}, bf16[256,1024]{1,0:T(8,128)(2,1)S(1)}, u32[]{:S(2)}, u32[]{:S(2)}) %collective-permute-start.23) | collective-permute-done | bytes 524320 | tf_op jit(solution)/shard_map/ppermute | solution.py:14
  253.1 2.8 collective-permute-start.26
  255.9 8.9 %collective-permute-done.31 = bf16[2,256,1024]{2,1,0:T(8,128)(2,1)} collective-permute-done((bf16[2,256,1024]{2,1,0:T(8,128)(2,1)S(1)}, bf16[2,256,1024]{2,1,0:T(8,128)(2,1)}, u32[]{:S(2)}, u32[]{:S(2)}) %collective-permute-start.31) | collective-permute-done | bytes 1048608 | tf_op jit(solution)/shard_map/ppermute | solution.py:14
  265.6 2.2 add_convert_fusion
  268.6 5.2 %collective-permute-start.34 = (bf16[2,64,1024]{2,1,0:T(8,128)(2,1)S(1)}, bf16[2,64,1024]{2,1,0:T(8,128)(2,1)}, u32[]{:S(2)}, u32[]{:S(2)}) collective-permute-start(bf16[2,64,1024]{2,1,0:T(8,128)(2,1)S(1)} %get-tuple-element.50), channel_id=1, source_target_pairs={{0,8},{8,16},{16,24},{24,0},{1,9},{9,17},{17,25},{25,1},{2,10},{10... | collective-permute-start | bytes 786440 | tf_op jit(solution)/shard_map/ppermute | solution.py:14
  273.8 3.4 %collective-permute-start.36 = (bf16[2,64,1024]{2,1,0:T(8,128)(2,1)S(1)}, bf16[2,64,1024]{2,1,0:T(8,128)(2,1)}, u32[]{:S(2)}, u32[]{:S(2)}) collective-permute-start(bf16[2,64,1024]{2,1,0:T(8,128)(2,1)S(1)} %get-tuple-element.51), channel_id=1, source_target_pairs={{0,16},{8,24},{16,0},{24,8},{1,17},{9,25},{17,1},{25,9},{2,18},{10... | collective-permute-start | bytes 786440 | tf_op jit(solution)/shard_map/ppermute | solution.py:14
  277.3 2.2 add_convert_fusion.1
  280.3 3.7 %collective-permute-start.28 = (bf16[2,64,1024]{2,1,0:T(8,128)(2,1)S(1)}, bf16[2,64,1024]{2,1,0:T(8,128)(2,1)}, u32[]{:S(2)}, u32[]{:S(2)}) collective-permute-start(bf16[2,64,1024]{2,1,0:T(8,128)(2,1)S(1)} %get-tuple-element.55), channel_id=1, source_target_pairs={{0,3},{1,0},{2,1},{3,2},{4,7},{5,4},{6,5},{7,6},{8,11},{9,8},{10,9... | collective-permute-start | bytes 786440 | tf_op jit(solution)/shard_map/ppermute | solution.py:14
  286.8 3.6 %collective-permute-done.27 = bf16[2,64,1024]{2,1,0:T(8,128)(2,1)S(1)} collective-permute-done((bf16[2,64,1024]{2,1,0:T(8,128)(2,1)}, bf16[2,64,1024]{2,1,0:T(8,128)(2,1)S(1)}, u32[]{:S(2)}, u32[]{:S(2)}) %collective-permute-start.27) | collective-permute-done | bytes 262176 | tf_op jit(solution)/shard_map/ppermute | solution.py:14
  291.2 2.2 collective-permute-done.29
  294.9 7.6 %collective-permute-done.37 = bf16[64,2048]{1,0:T(8,128)(2,1)S(1)} collective-permute-done((bf16[64,2048]{1,0:T(8,128)(2,1)S(1)}, bf16[64,2048]{1,0:T(8,128)(2,1)S(1)}, u32[]{:S(2)}, u32[]{:S(2)}) %collective-permute-start.37) | collective-permute-done | bytes 262176 | tf_op jit(solution)/shard_map/ppermute | solution.py:14
  (116 shorter events, 30.6 us)
Async XLA Ops:
  1.9 37.9 %copy-start.11 = (bf16[64,2048]{1,0:T(8,128)(2,1)}, bf16[64,2048]{1,0:T(8,128)(2,1)S(1)}, u32[]{:S(2)}) copy-start(bf16[64,2048]{1,0:T(8,128)(2,1)S(1)} %get-tuple-element.56.refs_8_) | copy-start | bytes 786436
  1.9 37.9 %copy-start.12 = (bf16[64,2048]{1,0:T(8,128)(2,1)}, bf16[64,2048]{1,0:T(8,128)(2,1)S(1)}, u32[]{:S(2)}) copy-start(bf16[64,2048]{1,0:T(8,128)(2,1)S(1)} %get-tuple-element.57.refs_0_) | copy-start | bytes 786436
  1.9 10.8 %collective-permute-start.10 = (bf16[64,2048]{1,0:T(8,128)(2,1)S(1)}, bf16[64,2048]{1,0:T(8,128)(2,1)S(1)}, u32[]{:S(2)}, u32[]{:S(2)}) collective-permute-start(bf16[64,2048]{1,0:T(8,128)(2,1)S(1)} %get-tuple-element.56.refs_8_), channel_id=1, source_target_pairs={{0,4},{4,0},{1,5},{5,1},{2,6},{6,2},{3,7},{7,3},{8,12},{12,8},{9,1... | collective-permute-start | bytes 786440 | tf_op jit(solution)/shard_map/ppermute | solution.py:14
  5.1 11.9 %collective-permute-start.3 = (bf16[64,2048]{1,0:T(8,128)(2,1)S(1)}, bf16[64,2048]{1,0:T(8,128)(2,1)S(1)}, u32[]{:S(2)}, u32[]{:S(2)}) collective-permute-start(bf16[64,2048]{1,0:T(8,128)(2,1)S(1)} %get-tuple-element.57.refs_0_), channel_id=1, source_target_pairs={{0,4},{4,0},{1,5},{5,1},{2,6},{6,2},{3,7},{7,3},{8,12},{12,8},{9,1... | collective-permute-start | bytes 786440 | tf_op jit(solution)/shard_map/ppermute | solution.py:14
  5.5 13.3 %collective-permute-start = (bf16[64,2048]{1,0:T(8,128)(2,1)S(1)}, bf16[64,2048]{1,0:T(8,128)(2,1)S(1)}, u32[]{:S(2)}, u32[]{:S(2)}) collective-permute-start(bf16[64,2048]{1,0:T(8,128)(2,1)S(1)} %get-tuple-element.57.refs_0_), channel_id=1, source_target_pairs={{0,3},{1,0},{2,1},{3,2},{4,7},{5,4},{6,5},{7,6},{8,11},{9,8},{10,9... | collective-permute-start | bytes 786440 | tf_op jit(solution)/shard_map/ppermute | solution.py:14
  9.6 11.1 %collective-permute-start.7 = (bf16[64,2048]{1,0:T(8,128)(2,1)S(1)}, bf16[64,2048]{1,0:T(8,128)(2,1)S(1)}, u32[]{:S(2)}, u32[]{:S(2)}) collective-permute-start(bf16[64,2048]{1,0:T(8,128)(2,1)S(1)} %get-tuple-element.56.refs_8_), channel_id=1, source_target_pairs={{0,24},{8,0},{16,8},{24,16},{1,25},{9,1},{17,9},{25,17},{2,26},{10... | collective-permute-start | bytes 786440 | tf_op jit(solution)/shard_map/ppermute | solution.py:14
  12.6 9.8 %collective-permute-start.2 = (bf16[64,2048]{1,0:T(8,128)(2,1)S(1)}, bf16[64,2048]{1,0:T(8,128)(2,1)S(1)}, u32[]{:S(2)}, u32[]{:S(2)}) collective-permute-start(bf16[64,2048]{1,0:T(8,128)(2,1)S(1)} %get-tuple-element.57.refs_0_), channel_id=1, source_target_pairs={{0,1},{1,2},{2,3},{3,0},{4,5},{5,6},{6,7},{7,4},{8,9},{9,10},{10,1... | collective-permute-start | bytes 786440 | tf_op jit(solution)/shard_map/ppermute | solution.py:14
  12.7 27.0 %copy-start.13 = (bf16[64,2048]{1,0:T(8,128)(2,1)}, bf16[64,2048]{1,0:T(8,128)(2,1)S(1)}, u32[]{:S(2)}) copy-start(bf16[64,2048]{1,0:T(8,128)(2,1)S(1)} %collective-permute-done.10.refs_12_) | copy-start | bytes 786436
  12.7 11.9 %collective-permute-start.9 = (bf16[64,2048]{1,0:T(8,128)(2,1)S(1)}, bf16[64,2048]{1,0:T(8,128)(2,1)S(1)}, u32[]{:S(2)}, u32[]{:S(2)}) collective-permute-start(bf16[64,2048]{1,0:T(8,128)(2,1)S(1)} %get-tuple-element.56.refs_8_), channel_id=1, source_target_pairs={{0,8},{8,16},{16,24},{24,0},{1,9},{9,17},{17,25},{25,1},{2,10},{10... | collective-permute-start | bytes 786440 | tf_op jit(solution)/shard_map/ppermute | solution.py:14
  17.0 22.7 %copy-start.14 = (bf16[64,2048]{1,0:T(8,128)(2,1)}, bf16[64,2048]{1,0:T(8,128)(2,1)S(1)}, u32[]{:S(2)}) copy-start(bf16[64,2048]{1,0:T(8,128)(2,1)S(1)} %collective-permute-done.3.refs_4_) | copy-start | bytes 786436
  17.0 9.5 %collective-permute-start.12 = (bf16[64,2048]{1,0:T(8,128)(2,1)S(1)}, bf16[64,2048]{1,0:T(8,128)(2,1)S(1)}, u32[]{:S(2)}, u32[]{:S(2)}) collective-permute-start(bf16[64,2048]{1,0:T(8,128)(2,1)S(1)} %collective-permute-done.10.refs_12_), channel_id=1, source_target_pairs={{0,8},{8,16},{16,24},{24,0},{1,9},{9,17},{17,25},{25,1},{2,10},{10... | collective-permute-start | bytes 786440 | tf_op jit(solution)/shard_map/ppermute | solution.py:14
  18.8 20.9 %copy-start.15 = (bf16[64,2048]{1,0:T(8,128)(2,1)}, bf16[64,2048]{1,0:T(8,128)(2,1)S(1)}, u32[]{:S(2)}) copy-start(bf16[64,2048]{1,0:T(8,128)(2,1)S(1)} %collective-permute-done.refs_1_) | copy-start | bytes 786436
  18.8 11.2 %collective-permute-start.5 = (bf16[64,2048]{1,0:T(8,128)(2,1)S(1)}, bf16[64,2048]{1,0:T(8,128)(2,1)S(1)}, u32[]{:S(2)}, u32[]{:S(2)}) collective-permute-start(bf16[64,2048]{1,0:T(8,128)(2,1)S(1)} %collective-permute-done.3.refs_4_), channel_id=1, source_target_pairs={{0,1},{1,2},{2,3},{3,0},{4,5},{5,6},{6,7},{7,4},{8,9},{9,10},{10,1... | collective-permute-start | bytes 786440 | tf_op jit(solution)/shard_map/ppermute | solution.py:14
  20.7 19.0 %copy-start.16 = (bf16[64,2048]{1,0:T(8,128)(2,1)}, bf16[64,2048]{1,0:T(8,128)(2,1)S(1)}, u32[]{:S(2)}) copy-start(bf16[64,2048]{1,0:T(8,128)(2,1)S(1)} %collective-permute-done.7.refs_9_) | copy-start | bytes 786436
  20.7 11.1 %collective-permute-start.11 = (bf16[64,2048]{1,0:T(8,128)(2,1)S(1)}, bf16[64,2048]{1,0:T(8,128)(2,1)S(1)}, u32[]{:S(2)}, u32[]{:S(2)}) collective-permute-start(bf16[64,2048]{1,0:T(8,128)(2,1)S(1)} %collective-permute-done.10.refs_12_), channel_id=1, source_target_pairs={{0,24},{8,0},{16,8},{24,16},{1,25},{9,1},{17,9},{25,17},{2,26},{10... | collective-permute-start | bytes 786440 | tf_op jit(solution)/shard_map/ppermute | solution.py:14
  22.4 17.4 %copy-start.17 = (bf16[64,2048]{1,0:T(8,128)(2,1)}, bf16[64,2048]{1,0:T(8,128)(2,1)S(1)}, u32[]{:S(2)}) copy-start(bf16[64,2048]{1,0:T(8,128)(2,1)S(1)} %collective-permute-done.2.refs_3_) | copy-start | bytes 786436
  22.4 9.6 %collective-permute-start.4 = (bf16[64,2048]{1,0:T(8,128)(2,1)S(1)}, bf16[64,2048]{1,0:T(8,128)(2,1)S(1)}, u32[]{:S(2)}, u32[]{:S(2)}) collective-permute-start(bf16[64,2048]{1,0:T(8,128)(2,1)S(1)} %collective-permute-done.3.refs_4_), channel_id=1, source_target_pairs={{0,3},{1,0},{2,1},{3,2},{4,7},{5,4},{6,5},{7,6},{8,11},{9,8},{10,9... | collective-permute-start | bytes 786440 | tf_op jit(solution)/shard_map/ppermute | solution.py:14
  24.6 44.2 %collective-permute-start.18 = (bf16[1,8,64,2048]{3,2,1,0:T(8,128)(2,1)}, bf16[1,8,64,2048]{3,2,1,0:T(8,128)(2,1)}, u32[]{:S(2)}, u32[]{:S(2)}) collective-permute-start(bf16[1,8,64,2048]{3,2,1,0:T(8,128)(2,1)} %param.8), channel_id=1, source_target_pairs={{32,0},{64,32},{96,64},{0,96},{33,1},{65,33},{97,65},{1,97},{34,2}... | collective-permute-start | bytes 6291464 | tf_op jit(solution)/shard_map/ppermute | solution.py:376
  26.5 8.2 %collective-permute-start.1 = (bf16[64,2048]{1,0:T(8,128)(2,1)S(1)}, bf16[64,2048]{1,0:T(8,128)(2,1)S(1)}, u32[]{:S(2)}, u32[]{:S(2)}) collective-permute-start(bf16[64,2048]{1,0:T(8,128)(2,1)S(1)} %collective-permute-done.refs_1_), channel_id=1, source_target_pairs={{0,3},{1,0},{2,1},{3,2},{4,7},{5,4},{6,5},{7,6},{8,11},{9,8},{10,9... | collective-permute-start | bytes 786440 | tf_op jit(solution)/shard_map/ppermute | solution.py:14
  30.0 6.5 %collective-permute-start.8 = (bf16[64,2048]{1,0:T(8,128)(2,1)S(1)}, bf16[64,2048]{1,0:T(8,128)(2,1)}, u32[]{:S(2)}, u32[]{:S(2)}) collective-permute-start(bf16[64,2048]{1,0:T(8,128)(2,1)S(1)} %collective-permute-done.7.refs_9_), channel_id=1, source_target_pairs={{0,24},{8,0},{16,8},{24,16},{1,25},{9,1},{17,9},{25,17},{2,26},{10... | collective-permute-start | bytes 786440 | tf_op jit(solution)/shard_map/ppermute | solution.py:14
  31.8 7.7 %collective-permute-start.13 = (bf16[64,2048]{1,0:T(8,128)(2,1)S(1)}, bf16[64,2048]{1,0:T(8,128)(2,1)}, u32[]{:S(2)}, u32[]{:S(2)}) collective-permute-start(bf16[64,2048]{1,0:T(8,128)(2,1)S(1)} %collective-permute-done.12.refs_15_), channel_id=1, source_target_pairs={{0,8},{8,16},{16,24},{24,0},{1,9},{9,17},{17,25},{25,1},{2,10},{10... | collective-permute-start | bytes 786440 | tf_op jit(solution)/shard_map/ppermute | solution.py:14
  32.0 7.7 %collective-permute-start.6 = (bf16[64,2048]{1,0:T(8,128)(2,1)S(1)}, bf16[64,2048]{1,0:T(8,128)(2,1)}, u32[]{:S(2)}, u32[]{:S(2)}) collective-permute-start(bf16[64,2048]{1,0:T(8,128)(2,1)S(1)} %collective-permute-done.5.refs_7_), channel_id=1, source_target_pairs={{0,1},{1,2},{2,3},{3,0},{4,5},{5,6},{6,7},{7,4},{8,9},{9,10},{10,1... | collective-permute-start | bytes 786440 | tf_op jit(solution)/shard_map/ppermute | solution.py:14
  44.4 45.1 %collective-permute-start.14 = (bf16[2,4,64,2048]{3,2,1,0:T(8,128)(2,1)}, bf16[2,4,64,2048]{3,2,1,0:T(8,128)(2,1)S(1)}, u32[]{:S(2)}, u32[]{:S(2)}) collective-permute-start(bf16[2,4,64,2048]{3,2,1,0:T(8,128)(2,1)} %get-tuple-element.26.refs_0_.refs_2_), channel_id=1, source_target_pairs={{0,24},{8,0},{16,8},{24,16},{1,25},{9,1},{17,9},{25,17},{2,26},{10... | collective-permute-start | bytes 6291464 | tf_op jit(solution)/shard_map/ppermute | solution.py:14
  47.5 45.5 %collective-permute-start.15 = (bf16[2,4,64,2048]{3,2,1,0:T(8,128)(2,1)}, bf16[2,4,64,2048]{3,2,1,0:T(8,128)(2,1)}, u32[]{:S(2)}, u32[]{:S(2)}) collective-permute-start(bf16[2,4,64,2048]{3,2,1,0:T(8,128)(2,1)} %get-tuple-element.26.refs_0_.refs_2_), channel_id=1, source_target_pairs={{0,8},{8,16},{16,24},{24,0},{1,9},{9,17},{17,25},{25,1},{2,10},{10... | collective-permute-start | bytes 6291464 | tf_op jit(solution)/shard_map/ppermute | solution.py:14
  47.5 45.5 %collective-permute-start.16 = (bf16[2,4,64,2048]{3,2,1,0:T(8,128)(2,1)}, bf16[2,4,64,2048]{3,2,1,0:T(8,128)(2,1)}, u32[]{:S(2)}, u32[]{:S(2)}) collective-permute-start(bf16[2,4,64,2048]{3,2,1,0:T(8,128)(2,1)} %get-tuple-element.27.refs_3_.refs_5_.refs_7_), channel_id=1, source_target_pairs={{0,3},{1,0},{2,1},{3,2},{4,7},{5,4},{6,5},{7,6},{8,11},{9,8},{10,9... | collective-permute-start | bytes 6291464 | tf_op jit(solution)/shard_map/ppermute | solution.py:14
  47.5 45.5 %collective-permute-start.17 = (bf16[2,4,64,2048]{3,2,1,0:T(8,128)(2,1)}, bf16[2,4,64,2048]{3,2,1,0:T(8,128)(2,1)}, u32[]{:S(2)}, u32[]{:S(2)}) collective-permute-start(bf16[2,4,64,2048]{3,2,1,0:T(8,128)(2,1)} %get-tuple-element.27.refs_3_.refs_5_.refs_7_), channel_id=1, source_target_pairs={{0,1},{1,2},{2,3},{3,0},{4,5},{5,6},{6,7},{7,4},{8,9},{9,10},{10,1... | collective-permute-start | bytes 6291464 | tf_op jit(solution)/shard_map/ppermute | solution.py:14
  96.8 21.1 %collective-permute-start.19 = (bf16[4,64,2048]{2,1,0:T(8,128)(2,1)}, bf16[4,64,2048]{2,1,0:T(8,128)(2,1)S(1)}, u32[]{:S(2)}, u32[]{:S(2)}) collective-permute-start(bf16[4,64,2048]{2,1,0:T(8,128)(2,1)} %get-tuple-element.28), channel_id=1, source_target_pairs={{0,24},{8,0},{16,8},{24,16},{1,25},{9,1},{17,9},{25,17},{2,26},{10... | collective-permute-start | bytes 3145736 | tf_op jit(solution)/shard_map/ppermute | solution.py:14
  99.8 21.4 %collective-permute-start.20 = (bf16[4,64,2048]{2,1,0:T(8,128)(2,1)}, bf16[4,64,2048]{2,1,0:T(8,128)(2,1)S(1)}, u32[]{:S(2)}, u32[]{:S(2)}) collective-permute-start(bf16[4,64,2048]{2,1,0:T(8,128)(2,1)} %get-tuple-element.29), channel_id=1, source_target_pairs={{0,8},{8,16},{16,24},{24,0},{1,9},{9,17},{17,25},{25,1},{2,10},{10... | collective-permute-start | bytes 3145736 | tf_op jit(solution)/shard_map/ppermute | solution.py:14
  99.9 21.4 %collective-permute-start.21 = (bf16[4,64,2048]{2,1,0:T(8,128)(2,1)}, bf16[4,64,2048]{2,1,0:T(8,128)(2,1)S(1)}, u32[]{:S(2)}, u32[]{:S(2)}) collective-permute-start(bf16[4,64,2048]{2,1,0:T(8,128)(2,1)} %get-tuple-element.30), channel_id=1, source_target_pairs={{0,3},{1,0},{2,1},{3,2},{4,7},{5,4},{6,5},{7,6},{8,11},{9,8},{10,9... | collective-permute-start | bytes 3145736 | tf_op jit(solution)/shard_map/ppermute | solution.py:14
  100.1 21.5 %collective-permute-start.22 = (bf16[4,64,2048]{2,1,0:T(8,128)(2,1)}, bf16[4,64,2048]{2,1,0:T(8,128)(2,1)}, u32[]{:S(2)}, u32[]{:S(2)}) collective-permute-start(bf16[4,64,2048]{2,1,0:T(8,128)(2,1)} %get-tuple-element.31), channel_id=1, source_target_pairs={{0,1},{1,2},{2,3},{3,0},{4,5},{5,6},{6,7},{7,4},{8,9},{9,10},{10,1... | collective-permute-start | bytes 3145736 | tf_op jit(solution)/shard_map/ppermute | solution.py:14
  122.6 30.4 %all-to-all-start.1 = ((bf16[32,64,512]{2,1,0:T(8,128)(2,1)}), bf16[32,64,512]{2,1,0:T(8,128)(2,1)S(1)}, u32[]{:S(2)}, u32[]{:S(2)}) async-start(bf16[32,64,512]{2,1,0:T(8,128)(2,1)} %hold.1), calls=%async_computation.1 | async-start | bytes 4194304 | tf_op jit(solution)/shard_map/all_to_all | solution.py:385
  154.3 56.2 %all-to-all-start = ((bf16[32,8,64,128]{3,2,1,0:T(8,128)(2,1)}), bf16[32,8,64,128]{3,2,1,0:T(8,128)(2,1)}, u32[]{:S(2)}, u32[]{:S(2)}) async-start(bf16[32,8,64,128]{3,2,1,0:T(8,128)(2,1)} %absorb.1), calls=%async_computation | async-start | bytes 8388608 | tf_op jit(solution)/shard_map/all_to_all | solution.py:387
  210.6 16.9 %copy-start.5 = (s32[3]{0:T(128)S(1)}, s32[3]{0:T(128)}, u32[]{:S(2)}) copy-start(s32[3]{0:T(128)} %pad_add_fusion.at_ref.refs_0_) | copy-start | bytes 40
  230.9 10.7 %collective-permute-start.30 = (bf16[256,1024]{1,0:T(8,128)(2,1)S(1)}, bf16[256,1024]{1,0:T(8,128)(2,1)S(1)}, u32[]{:S(2)}, u32[]{:S(2)}) collective-permute-start(bf16[256,1024]{1,0:T(8,128)(2,1)S(1)} %get-tuple-element.45), channel_id=1, source_target_pairs={{0,1},{1,2},{2,3},{3,0},{4,5},{5,6},{6,7},{7,4},{8,9},{9,10},{10,1... | collective-permute-start | bytes 1572872 | tf_op jit(solution)/shard_map/ppermute | solution.py:14
  231.0 11.2 %collective-permute-start.32 = (bf16[256,1024]{1,0:T(8,128)(2,1)S(1)}, bf16[256,1024]{1,0:T(8,128)(2,1)S(1)}, u32[]{:S(2)}, u32[]{:S(2)}) collective-permute-start(bf16[256,1024]{1,0:T(8,128)(2,1)S(1)} %get-tuple-element.49), channel_id=1, source_target_pairs={{0,3},{1,0},{2,1},{3,2},{4,7},{5,4},{6,5},{7,6},{8,11},{9,8},{10,9... | collective-permute-start | bytes 1572872 | tf_op jit(solution)/shard_map/ppermute | solution.py:14
  238.2 12.0 %collective-permute-start.23 = (bf16[256,1024]{1,0:T(8,128)(2,1)S(1)}, bf16[256,1024]{1,0:T(8,128)(2,1)S(1)}, u32[]{:S(2)}, u32[]{:S(2)}) collective-permute-start(bf16[256,1024]{1,0:T(8,128)(2,1)S(1)} %get-tuple-element.37), channel_id=1, source_target_pairs={{0,8},{8,16},{16,24},{24,0},{1,9},{9,17},{17,25},{25,1},{2,10},{10... | collective-permute-start | bytes 1572872 | tf_op jit(solution)/shard_map/ppermute | solution.py:14
  238.9 13.0 %collective-permute-start.25 = (bf16[256,1024]{1,0:T(8,128)(2,1)S(1)}, bf16[256,1024]{1,0:T(8,128)(2,1)S(1)}, u32[]{:S(2)}, u32[]{:S(2)}) collective-permute-start(bf16[256,1024]{1,0:T(8,128)(2,1)S(1)} %get-tuple-element.41), channel_id=1, source_target_pairs={{0,24},{8,0},{16,8},{24,16},{1,25},{9,1},{17,9},{25,17},{2,26},{10... | collective-permute-start | bytes 1572872 | tf_op jit(solution)/shard_map/ppermute | solution.py:14
  241.9 23.0 %collective-permute-start.31 = (bf16[2,256,1024]{2,1,0:T(8,128)(2,1)S(1)}, bf16[2,256,1024]{2,1,0:T(8,128)(2,1)}, u32[]{:S(2)}, u32[]{:S(2)}) collective-permute-start(bf16[2,256,1024]{2,1,0:T(8,128)(2,1)S(1)} %pad_maximum_fusion.2), channel_id=1, source_target_pairs={{0,1},{1,2},{2,3},{3,0},{4,5},{5,6},{6,7},{7,4},{8,9},{9,10},{10,1... | collective-permute-start | bytes 3145736 | tf_op jit(solution)/shard_map/ppermute | solution.py:14
  243.5 22.1 %collective-permute-start.33 = (bf16[2,256,1024]{2,1,0:T(8,128)(2,1)}, bf16[2,256,1024]{2,1,0:T(8,128)(2,1)}, u32[]{:S(2)}, u32[]{:S(2)}) collective-permute-start(bf16[2,256,1024]{2,1,0:T(8,128)(2,1)} %pad_maximum_fusion.3), channel_id=1, source_target_pairs={{0,3},{1,0},{2,1},{3,2},{4,7},{5,4},{6,5},{7,6},{8,11},{9,8},{10,9... | collective-permute-start | bytes 3145736 | tf_op jit(solution)/shard_map/ppermute | solution.py:14
  251.4 25.9 %collective-permute-start.24 = (bf16[2,256,1024]{2,1,0:T(8,128)(2,1)}, bf16[2,256,1024]{2,1,0:T(8,128)(2,1)}, u32[]{:S(2)}, u32[]{:S(2)}) collective-permute-start(bf16[2,256,1024]{2,1,0:T(8,128)(2,1)} %pad_maximum_fusion), channel_id=1, source_target_pairs={{0,8},{8,16},{16,24},{24,0},{1,9},{9,17},{17,25},{25,1},{2,10},{10... | collective-permute-start | bytes 3145736 | tf_op jit(solution)/shard_map/ppermute | solution.py:14
  253.1 24.2 %collective-permute-start.26 = (bf16[2,256,1024]{2,1,0:T(8,128)(2,1)}, bf16[2,256,1024]{2,1,0:T(8,128)(2,1)}, u32[]{:S(2)}, u32[]{:S(2)}) collective-permute-start(bf16[2,256,1024]{2,1,0:T(8,128)(2,1)} %pad_maximum_fusion.1), channel_id=1, source_target_pairs={{0,24},{8,0},{16,8},{24,16},{1,25},{9,1},{17,9},{25,17},{2,26},{10... | collective-permute-start | bytes 3145736 | tf_op jit(solution)/shard_map/ppermute | solution.py:14
  268.6 15.4 %collective-permute-start.34 = (bf16[2,64,1024]{2,1,0:T(8,128)(2,1)S(1)}, bf16[2,64,1024]{2,1,0:T(8,128)(2,1)}, u32[]{:S(2)}, u32[]{:S(2)}) collective-permute-start(bf16[2,64,1024]{2,1,0:T(8,128)(2,1)S(1)} %get-tuple-element.50), channel_id=1, source_target_pairs={{0,8},{8,16},{16,24},{24,0},{1,9},{9,17},{17,25},{25,1},{2,10},{10... | collective-permute-start | bytes 786440 | tf_op jit(solution)/shard_map/ppermute | solution.py:14
  273.8 11.6 %collective-permute-start.35 = (bf16[2,64,1024]{2,1,0:T(8,128)(2,1)}, bf16[2,64,1024]{2,1,0:T(8,128)(2,1)}, u32[]{:S(2)}, u32[]{:S(2)}) collective-permute-start(bf16[2,64,1024]{2,1,0:T(8,128)(2,1)} %get-tuple-element.52), channel_id=1, source_target_pairs={{0,24},{8,0},{16,8},{24,16},{1,25},{9,1},{17,9},{25,17},{2,26},{10... | collective-permute-start | bytes 786440 | tf_op jit(solution)/shard_map/ppermute | solution.py:14
  273.8 11.7 %collective-permute-start.36 = (bf16[2,64,1024]{2,1,0:T(8,128)(2,1)S(1)}, bf16[2,64,1024]{2,1,0:T(8,128)(2,1)}, u32[]{:S(2)}, u32[]{:S(2)}) collective-permute-start(bf16[2,64,1024]{2,1,0:T(8,128)(2,1)S(1)} %get-tuple-element.51), channel_id=1, source_target_pairs={{0,16},{8,24},{16,0},{24,8},{1,17},{9,25},{17,1},{25,9},{2,18},{10... | collective-permute-start | bytes 786440 | tf_op jit(solution)/shard_map/ppermute | solution.py:14
  280.3 10.2 %collective-permute-start.27 = (bf16[2,64,1024]{2,1,0:T(8,128)(2,1)}, bf16[2,64,1024]{2,1,0:T(8,128)(2,1)S(1)}, u32[]{:S(2)}, u32[]{:S(2)}) collective-permute-start(bf16[2,64,1024]{2,1,0:T(8,128)(2,1)} %get-tuple-element.53), channel_id=1, source_target_pairs={{0,1},{1,2},{2,3},{3,0},{4,5},{5,6},{6,7},{7,4},{8,9},{9,10},{10,1... | collective-permute-start | bytes 786440 | tf_op jit(solution)/shard_map/ppermute | solution.py:14
  280.3 10.9 %collective-permute-start.28 = (bf16[2,64,1024]{2,1,0:T(8,128)(2,1)S(1)}, bf16[2,64,1024]{2,1,0:T(8,128)(2,1)}, u32[]{:S(2)}, u32[]{:S(2)}) collective-permute-start(bf16[2,64,1024]{2,1,0:T(8,128)(2,1)S(1)} %get-tuple-element.55), channel_id=1, source_target_pairs={{0,3},{1,0},{2,1},{3,2},{4,7},{5,4},{6,5},{7,6},{8,11},{9,8},{10,9... | collective-permute-start | bytes 786440 | tf_op jit(solution)/shard_map/ppermute | solution.py:14
  284.0 9.4 %collective-permute-start.29 = (bf16[2,64,1024]{2,1,0:T(8,128)(2,1)S(1)}, bf16[2,64,1024]{2,1,0:T(8,128)(2,1)}, u32[]{:S(2)}, u32[]{:S(2)}) collective-permute-start(bf16[2,64,1024]{2,1,0:T(8,128)(2,1)S(1)} %get-tuple-element.54), channel_id=1, source_target_pairs={{0,2},{1,3},{2,0},{3,1},{4,6},{5,7},{6,4},{7,5},{8,10},{9,11},{10,... | collective-permute-start | bytes 786440 | tf_op jit(solution)/shard_map/ppermute | solution.py:14
  294.6 8.0 %collective-permute-start.37 = (bf16[64,2048]{1,0:T(8,128)(2,1)S(1)}, bf16[64,2048]{1,0:T(8,128)(2,1)S(1)}, u32[]{:S(2)}, u32[]{:S(2)}) collective-permute-start(bf16[64,2048]{1,0:T(8,128)(2,1)S(1)} %fusion.13), channel_id=1, source_target_pairs={{0,4},{4,0},{1,5},{5,1},{2,6},{6,2},{3,7},{7,3},{8,12},{12,8},{9,1... | collective-permute-start | bytes 786440 | tf_op jit(solution)/shard_map/ppermute | solution.py:14
  (17 other events, 115.4 us)

commit v4 on v3

--- a/solution.py
+++ b/solution.py
@@ -239,7 +239,7 @@
         + [pl.BlockSpec((4, 64, tile), lambda i: (0, 0, i))] * 4,
         out_specs=pl.BlockSpec((tile // 64, w, 64, 2 * rows // w), lambda i: (i, 0, 0, 0)),
         scratch_shapes=[pltpu.VMEM((2, rows, k // 4), BF16), pltpu.VMEM((2, rows, tile), F32)],
-        compiler_params=pltpu.CompilerParams(vmem_limit_bytes=VMEM_LIMIT),
+        compiler_params=pltpu.CompilerParams(vmem_limit_bytes=63 << 20),
         cost_estimate=pl.CostEstimate(flops=rows * k * columns, bytes_accessed=20 << 20, transcendentals=0),
         name="absorb",
     )(at, mpo.reshape(-1), first, second, part, *blocks)

time: 308 us -> 307 us (level)
  transfers between devices with their start and end apart: 40 -> 40, of which waited for: 21 -> 22; matrix products, arithmetic and copies ran while one was open for 12% -> 12% of each run, Pallas kernels for 17% -> 17%
where the time goes in v4:
time: 307 us; the launch traced here: 302 us
  waiting for transfers between devices  111 us (36%)
  starting transfers between devices  76.4 us (25%)
  Pallas kernels  73.5 us (24%)
  local copies, waits for them, and re-layouts  28.5 us (9%)
  other arithmetic  12.3 us (4%)
    ppermute x37, starting transfers between devices, hop(): lax.ppermute(block, axis, [(i, (i + distance) % n) for i in range(n)])  63.7 us
    ppermute x37, waiting for transfers between devices, hop(): lax.ppermute(block, axis, [(i, (i + distance) % n) for i in range(n)])  57.1 us
    all_to_all x1, waiting for transfers between devices, local(): lax.all_to_all(carried, sector, split_axis=0, concat_axis=0, tiled=True)  47.5 us
    pallas_call x1, Pallas kernels, step(): pl.pallas_call(step_kernel, out_shape=(jax.ShapeDtypeStruct((rows, column...  16.9 us
    pallas_call x1, Pallas kernels, absorb(): pl.pallas_call(absorb_kernel, out_shape=jax.ShapeDtypeStruct((columns //...  16.6 us
    pallas_call x1, Pallas kernels, begin(): pl.pallas_call(begin_kernel, out_shape=jax.ShapeDtypeStruct((2, rows, col...  14.8 us
    pallas_call x1, Pallas kernels, bond_right(): pl.pallas_call(bond_kernel, out_shape=jax.ShapeDtypeStruct((k // 64, rows...  11 us
    another operation x1, local copies, waits for them, and re-layouts, local(): first.reshape(w * rows, 4, 2, 4, 64).transpose(0, 3, 2, 1, 4)  8.44 us
  transfers between devices with their start and end apart: 40, of which 22 were waited for; matrix products, arithmetic and copies ran while one was open for 12% of the time, Pallas kernels for 17%

profile of v4, /device:TPU:0, one launch (start us, length us, event | category | flops | bytes accessed | tf_op | source)
XLA Modules:
  0.0 302.4 jit_solution(12561902987637706745)
XLA Ops:
  1.9 3.2 %collective-permute-start.10 = (bf16[64,2048]{1,0:T(8,128)(2,1)S(1)}, bf16[64,2048]{1,0:T(8,128)(2,1)S(1)}, u32[]{:S(2)}, u32[]{:S(2)}) collective-permute-start(bf16[64,2048]{1,0:T(8,128)(2,1)S(1)} %get-tuple-element.56.refs_8_), channel_id=1, source_target_pairs={{0,4},{4,0},{1,5},{5,1},{2,6},{6,2},{3,7},{7,3},{8,12},{12,8},{9,1... | collective-permute-start | bytes 786440 | tf_op jit(solution)/shard_map/ppermute | solution.py:14
  5.5 4.1 %collective-permute-start = (bf16[64,2048]{1,0:T(8,128)(2,1)S(1)}, bf16[64,2048]{1,0:T(8,128)(2,1)S(1)}, u32[]{:S(2)}, u32[]{:S(2)}) collective-permute-start(bf16[64,2048]{1,0:T(8,128)(2,1)S(1)} %get-tuple-element.57.refs_0_), channel_id=1, source_target_pairs={{0,3},{1,0},{2,1},{3,2},{4,7},{5,4},{6,5},{7,6},{8,11},{9,8},{10,9... | collective-permute-start | bytes 786440 | tf_op jit(solution)/shard_map/ppermute | solution.py:14
  9.6 3.0 collective-permute-start.7
  14.3 2.7 collective-permute-done.3.refs_4_
  17.0 1.8 collective-permute-start.12
  18.8 1.9 collective-permute-start.5
  22.4 2.2 collective-permute-start.4
  24.6 1.9 collective-permute-done.12.refs_15_
  26.5 3.5 %collective-permute-start.1 = (bf16[64,2048]{1,0:T(8,128)(2,1)S(1)}, bf16[64,2048]{1,0:T(8,128)(2,1)S(1)}, u32[]{:S(2)}, u32[]{:S(2)}) collective-permute-start(bf16[64,2048]{1,0:T(8,128)(2,1)S(1)} %collective-permute-done.refs_1_), channel_id=1, source_target_pairs={{0,3},{1,0},{2,1},{3,2},{4,7},{5,4},{6,5},{7,6},{8,11},{9,8},{10,9... | collective-permute-start | bytes 786440 | tf_op jit(solution)/shard_map/ppermute | solution.py:14
  30.0 1.8 collective-permute-start.8
  34.7 1.8 collective-permute-done.8.refs_10_
  36.5 3.0 collective-permute-done.13.refs_14_
  39.8 4.5 %collect.1 = (bf16[2,4,64,2048]{3,2,1,0:T(8,128)(2,1)}, bf16[2,4,64,2048]{3,2,1,0:T(8,128)(2,1)}) custom-call(s32[3]{0:T(128)} %pad_add_fusion.at_ref.refs_0_, bf16[64,2048]{1,0:T(8,128)(2,1)} %copy-done.11, bf16[64,2048]{1,0:T(8,128)(2,1)} %copy-done.14, bf16[64,2048]{1,0:T(8,128)(2,1)} %copy-done.22, bf16[64,2048]{1,0:T(8,128)(2,1)} %copy-done.16, ...), custom_call_target="tpu_custom_call" | custom-call | bytes 8388608 | tf_op jit(solution)/shard_map/collect/pallas_call | solution.py:51
  44.4 3.1 %collective-permute-start.14 = (bf16[2,4,64,2048]{3,2,1,0:T(8,128)(2,1)}, bf16[2,4,64,2048]{3,2,1,0:T(8,128)(2,1)S(1)}, u32[]{:S(2)}, u32[]{:S(2)}) collective-permute-start(bf16[2,4,64,2048]{3,2,1,0:T(8,128)(2,1)} %get-tuple-element.26.refs_0_.refs_2_), channel_id=1, source_target_pairs={{0,24},{8,0},{16,8},{24,16},{1,25},{9,1},{17,9},{25,17},{2,26},{10... | collective-permute-start | bytes 6291464 | tf_op jit(solution)/shard_map/ppermute | solution.py:14
  47.5 2.0 collective-permute-start.17
  49.5 8.4 %reshape.54 = bf16[512,4,2,4,64]{4,3,2,1,0:T(4,128)(2,1)} reshape(bf16[1,8,64,2048]{3,2,1,0:T(8,128)(2,1)} %param.5) | data formatting | bytes 4194304 | tf_op jit(solution)/shard_map/reshape;reshape | solution.py:380
  57.9 6.9 %copy.22 = bf16[512,4,2,4,64]{0,4,1,2,3:T(8,128)(2,1)} copy(bf16[512,4,2,4,64]{4,3,2,1,0:T(4,128)(2,1)} %reshape.54) | data formatting | bytes 4194304 | tf_op jit(solution)/shard_map/transpose | solution.py:380
  64.9 3.9 %copy.18.second_ref.refs_5_ = bf16[512,2048]{1,0:T(8,128)(2,1)} copy(bf16[512,2048]{0,1:T(8,128)(2,1)} %bitcast.87) | data formatting | bytes 4194304 | tf_op jit(solution)/shard_map/reshape | solution.py:380
  68.8 11.0 %bond_right.1.refs_4_.refs_0_ = bf16[32,64,512]{2,1,0:T(8,128)(2,1)} custom-call(bf16[512,2048]{1,0:T(8,128)(2,1)} %bitcast.12.r_ref, bf16[2048,2048]{1,0:T(8,128)(2,1)} %bitcast.93), custom_call_target="tpu_custom_call" | custom-call | flops 4294967296 | bytes 12582912 | tf_op jit(solution)/shard_map/bond_right/pallas_call | solution.py:141
  79.8 9.8 %collective-permute-done.14.refs_1_.refs_0_.refs_3_ = bf16[2,4,64,2048]{3,2,1,0:T(8,128)(2,1)S(1)} collective-permute-done((bf16[2,4,64,2048]{3,2,1,0:T(8,128)(2,1)}, bf16[2,4,64,2048]{3,2,1,0:T(8,128)(2,1)S(1)}, u32[]{:S(2)}, u32[]{:S(2)}) %collective-permute-start.14) | collective-permute-done | bytes 2097184 | tf_op jit(solution)/shard_map/ppermute | solution.py:14
  89.5 3.4 %collective-permute-done.15.refs_2_.refs_1_.refs_4_ = bf16[2,4,64,2048]{3,2,1,0:T(8,128)(2,1)} collective-permute-done((bf16[2,4,64,2048]{3,2,1,0:T(8,128)(2,1)}, bf16[2,4,64,2048]{3,2,1,0:T(8,128)(2,1)}, u32[]{:S(2)}, u32[]{:S(2)}) %collective-permute-start.15) | collective-permute-done | bytes 2097184 | tf_op jit(solution)/shard_map/ppermute | solution.py:14
  93.0 3.9 %halves.1 = (bf16[4,64,2048]{2,1,0:T(8,128)(2,1)}, bf16[4,64,2048]{2,1,0:T(8,128)(2,1)}, bf16[4,64,2048]{2,1,0:T(8,128)(2,1)}, bf16[4,64,2048]{2,1,0:T(8,128)(2,1)}) custom-call(bf16[2,4,64,2048]{3,2,1,0:T(8,128)(2,1)} %copy-done.6, bf16[2,4,64,2048]{3,2,1,0:T(8,128)(2,1)} %collective-permute-done.15.refs_2_.refs_1_.refs_4_, ...), custom_call_target="tpu_custom_call" | custom-call | bytes 8388608 | tf_op jit(solution)/shard_map/halves/pallas_call | solution.py:83
  96.8 3.0 collective-permute-start.19
  101.9 14.8 %begin.1.part_ref.refs_1_ = f32[2,512,2048]{2,1,0:T(8,128)} custom-call(s32[3]{0:T(128)} %pad_add_fusion.at_ref.refs_0_, bf16[512,2048]{1,0:T(8,128)(2,1)} %bitcast.85, bf16[512,2048]{1,0:T(8,128)(2,1)} %copy.18.second_ref.refs_5_, bf16[2,4,64,2048]{3,2,1,0:T(8,128)(2,1)} %get-tuple-element.26.refs_0_.refs_2_, bf16[2,4,64,2048]{3,2,1,0:T(8,128)(2,1)} %copy-done.6, ...), custom_call_target="tpu_custom_call" | custom-call | flops 6442450944 | bytes 25165824 | tf_op jit(solution)/shard_map/begin/pallas_call | solution.py:178
  118.0 3.3 %collective-permute-done.20.refs_1_.refs_4_.refs_6_ = bf16[4,64,2048]{2,1,0:T(8,128)(2,1)S(1)} collective-permute-done((bf16[4,64,2048]{2,1,0:T(8,128)(2,1)}, bf16[4,64,2048]{2,1,0:T(8,128)(2,1)S(1)}, u32[]{:S(2)}, u32[]{:S(2)}) %collective-permute-start.20) | collective-permute-done | bytes 1048608 | tf_op jit(solution)/shard_map/ppermute | solution.py:14
  122.6 7.0 %all-to-all-start.1 = ((bf16[32,64,512]{2,1,0:T(8,128)(2,1)}), bf16[32,64,512]{2,1,0:T(8,128)(2,1)}, u32[]{:S(2)}, u32[]{:S(2)}) async-start(bf16[32,64,512]{2,1,0:T(8,128)(2,1)} %hold.1), calls=%async_computation.1 | async-start | bytes 4194304 | tf_op jit(solution)/shard_map/all_to_all | solution.py:385
  130.5 16.6 %absorb.1 = bf16[32,8,64,128]{3,2,1,0:T(8,128)(2,1)} custom-call(s32[3]{0:T(128)} %pad_add_fusion.at_ref.refs_0_, f32[256]{0:T(256)} %reshape_squeeze.6.m_ref, bf16[512,2048]{1,0:T(8,128)(2,1)} %bitcast.86, bf16[512,2048]{1,0:T(8,128)(2,1)} %copy.18.second_ref.refs_5_, f32[2,512,2048]{2,1,0:T(8,128)} %begin.1.part_ref.refs_1_, ...), custom_call_target="tpu_custom_call" | custom-call | flops 2147483648 | bytes 20971520 | tf_op jit(solution)/shard_map/absorb/pallas_call | solution.py:234
  147.1 5.9 %all-to-all-done.1 = bf16[32,64,512]{2,1,0:T(8,128)(2,1)} async-done(((bf16[32,64,512]{2,1,0:T(8,128)(2,1)}), bf16[32,64,512]{2,1,0:T(8,128)(2,1)}, u32[]{:S(2)}, u32[]{:S(2)}) %all-to-all-start.1) | async-done | bytes 2097184 | tf_op jit(solution)/shard_map/all_to_all | solution.py:385
  153.1 5.7 %all-to-all-start = ((bf16[32,8,64,128]{3,2,1,0:T(8,128)(2,1)}), bf16[32,8,64,128]{3,2,1,0:T(8,128)(2,1)}, u32[]{:S(2)}, u32[]{:S(2)}) async-start(bf16[32,8,64,128]{3,2,1,0:T(8,128)(2,1)} %absorb.1), calls=%async_computation | async-start | bytes 8388608 | tf_op jit(solution)/shard_map/all_to_all | solution.py:387
  158.8 2.9 copy.19
  161.7 47.5 %all-to-all-done = bf16[32,8,64,128]{3,2,1,0:T(8,128)(2,1)} async-done(((bf16[32,8,64,128]{3,2,1,0:T(8,128)(2,1)}), bf16[32,8,64,128]{3,2,1,0:T(8,128)(2,1)}, u32[]{:S(2)}, u32[]{:S(2)}) %all-to-all-start) | async-done | bytes 4194336 | tf_op jit(solution)/shard_map/all_to_all | solution.py:387
  209.3 16.9 %step.1 = (bf16[512,2048]{1,0:T(8,128)(2,1)}, bf16[2048,512]{1,0:T(8,128)(2,1)}) custom-call(s32[3]{0:T(128)} %pad_add_fusion.at_ref.refs_0_, bf16[32,512,128]{2,1,0:T(8,128)(2,1)} %bitcast.14.c_ref, bf16[2,4,64,2048]{3,2,1,0:T(8,128)(2,1)} %get-tuple-element.26.refs_0_.refs_2_, bf16[2,4,64,2048]{3,2,1,0:T(8,128)(2,1)} %copy-done.6, ...), custom_call_target="tpu_custom_call" | custom-call | flops 8589934592 | bytes 25165824 | tf_op jit(solution)/shard_map/step/pallas_call | solution.py:291
  227.8 1.8 terms_1.1
  229.7 3.2 %collective-permute-start.32 = (bf16[256,1024]{1,0:T(8,128)(2,1)S(1)}, bf16[256,1024]{1,0:T(8,128)(2,1)S(1)}, u32[]{:S(2)}, u32[]{:S(2)}) collective-permute-start(bf16[256,1024]{1,0:T(8,128)(2,1)S(1)} %get-tuple-element.49), channel_id=1, source_target_pairs={{0,3},{1,0},{2,1},{3,2},{4,7},{5,4},{6,5},{7,6},{8,11},{9,8},{10,9... | collective-permute-start | bytes 1572872 | tf_op jit(solution)/shard_map/ppermute | solution.py:14
  232.9 4.0 %terms_3.1 = (bf16[256,1024]{1,0:T(8,128)(2,1)S(1)}, bf16[256,1024]{1,0:T(8,128)(2,1)S(1)}, bf16[256,1024]{1,0:T(8,128)(2,1)S(1)}, bf16[256,1024]{1,0:T(8,128)(2...) custom-call(s32[3]{0:T(128)S(1)} %copy-done.5, ...), custom_call_target="tpu_custom_call" | custom-call | flops 3221225472 | bytes 6291456 | tf_op jit(solution)/shard_map/terms_3/pallas_call | solution.py:329
  237.5 2.9 collective-permute-start.25
  242.4 3.2 %collective-permute-start.33 = (bf16[2,256,1024]{2,1,0:T(8,128)(2,1)}, bf16[2,256,1024]{2,1,0:T(8,128)(2,1)}, u32[]{:S(2)}, u32[]{:S(2)}) collective-permute-start(bf16[2,256,1024]{2,1,0:T(8,128)(2,1)} %pad_maximum_fusion.3), channel_id=1, source_target_pairs={{0,3},{1,0},{2,1},{3,2},{4,7},{5,4},{6,5},{7,6},{8,11},{9,8},{10,9... | collective-permute-start | bytes 3145736 | tf_op jit(solution)/shard_map/ppermute | solution.py:14
  245.6 3.3 %collective-permute-done.23 = bf16[256,1024]{1,0:T(8,128)(2,1)S(1)} collective-permute-done((bf16[256,1024]{1,0:T(8,128)(2,1)S(1)}, bf16[256,1024]{1,0:T(8,128)(2,1)S(1)}, u32[]{:S(2)}, u32[]{:S(2)}) %collective-permute-start.23) | collective-permute-done | bytes 524320 | tf_op jit(solution)/shard_map/ppermute | solution.py:14
  251.9 2.8 collective-permute-start.26
  254.7 8.9 %collective-permute-done.31 = bf16[2,256,1024]{2,1,0:T(8,128)(2,1)} collective-permute-done((bf16[2,256,1024]{2,1,0:T(8,128)(2,1)S(1)}, bf16[2,256,1024]{2,1,0:T(8,128)(2,1)}, u32[]{:S(2)}, u32[]{:S(2)}) %collective-permute-start.31) | collective-permute-done | bytes 1048608 | tf_op jit(solution)/shard_map/ppermute | solution.py:14
  264.4 2.2 add_convert_fusion
  267.4 5.2 %collective-permute-start.34 = (bf16[2,64,1024]{2,1,0:T(8,128)(2,1)S(1)}, bf16[2,64,1024]{2,1,0:T(8,128)(2,1)}, u32[]{:S(2)}, u32[]{:S(2)}) collective-permute-start(bf16[2,64,1024]{2,1,0:T(8,128)(2,1)S(1)} %get-tuple-element.50), channel_id=1, source_target_pairs={{0,8},{8,16},{16,24},{24,0},{1,9},{9,17},{17,25},{25,1},{2,10},{10... | collective-permute-start | bytes 786440 | tf_op jit(solution)/shard_map/ppermute | solution.py:14
  272.6 3.7 %collective-permute-start.36 = (bf16[2,64,1024]{2,1,0:T(8,128)(2,1)S(1)}, bf16[2,64,1024]{2,1,0:T(8,128)(2,1)}, u32[]{:S(2)}, u32[]{:S(2)}) collective-permute-start(bf16[2,64,1024]{2,1,0:T(8,128)(2,1)S(1)} %get-tuple-element.51), channel_id=1, source_target_pairs={{0,16},{8,24},{16,0},{24,8},{1,17},{9,25},{17,1},{25,9},{2,18},{10... | collective-permute-start | bytes 786440 | tf_op jit(solution)/shard_map/ppermute | solution.py:14
  276.4 2.2 add_convert_fusion.1
  279.4 3.5 %collective-permute-start.28 = (bf16[2,64,1024]{2,1,0:T(8,128)(2,1)S(1)}, bf16[2,64,1024]{2,1,0:T(8,128)(2,1)}, u32[]{:S(2)}, u32[]{:S(2)}) collective-permute-start(bf16[2,64,1024]{2,1,0:T(8,128)(2,1)S(1)} %get-tuple-element.55), channel_id=1, source_target_pairs={{0,3},{1,0},{2,1},{3,2},{4,7},{5,4},{6,5},{7,6},{8,11},{9,8},{10,9... | collective-permute-start | bytes 786440 | tf_op jit(solution)/shard_map/ppermute | solution.py:14
  285.8 3.7 %collective-permute-done.27 = bf16[2,64,1024]{2,1,0:T(8,128)(2,1)S(1)} collective-permute-done((bf16[2,64,1024]{2,1,0:T(8,128)(2,1)}, bf16[2,64,1024]{2,1,0:T(8,128)(2,1)S(1)}, u32[]{:S(2)}, u32[]{:S(2)}) %collective-permute-start.27) | collective-permute-done | bytes 262176 | tf_op jit(solution)/shard_map/ppermute | solution.py:14
  290.3 2.2 collective-permute-done.29
  293.8 7.9 %collective-permute-done.37 = bf16[64,2048]{1,0:T(8,128)(2,1)S(1)} collective-permute-done((bf16[64,2048]{1,0:T(8,128)(2,1)S(1)}, bf16[64,2048]{1,0:T(8,128)(2,1)S(1)}, u32[]{:S(2)}, u32[]{:S(2)}) %collective-permute-start.37) | collective-permute-done | bytes 262176 | tf_op jit(solution)/shard_map/ppermute | solution.py:14
  (114 shorter events, 29.0 us)
Async XLA Ops:
  1.9 37.9 %copy-start.10 = (bf16[64,2048]{1,0:T(8,128)(2,1)}, bf16[64,2048]{1,0:T(8,128)(2,1)S(1)}, u32[]{:S(2)}) copy-start(bf16[64,2048]{1,0:T(8,128)(2,1)S(1)} %get-tuple-element.56.refs_8_) | copy-start | bytes 786436
  1.9 37.9 %copy-start.11 = (bf16[64,2048]{1,0:T(8,128)(2,1)}, bf16[64,2048]{1,0:T(8,128)(2,1)S(1)}, u32[]{:S(2)}) copy-start(bf16[64,2048]{1,0:T(8,128)(2,1)S(1)} %get-tuple-element.57.refs_0_) | copy-start | bytes 786436
  1.9 10.8 %collective-permute-start.10 = (bf16[64,2048]{1,0:T(8,128)(2,1)S(1)}, bf16[64,2048]{1,0:T(8,128)(2,1)S(1)}, u32[]{:S(2)}, u32[]{:S(2)}) collective-permute-start(bf16[64,2048]{1,0:T(8,128)(2,1)S(1)} %get-tuple-element.56.refs_8_), channel_id=1, source_target_pairs={{0,4},{4,0},{1,5},{5,1},{2,6},{6,2},{3,7},{7,3},{8,12},{12,8},{9,1... | collective-permute-start | bytes 786440 | tf_op jit(solution)/shard_map/ppermute | solution.py:14
  5.1 11.9 %collective-permute-start.3 = (bf16[64,2048]{1,0:T(8,128)(2,1)S(1)}, bf16[64,2048]{1,0:T(8,128)(2,1)S(1)}, u32[]{:S(2)}, u32[]{:S(2)}) collective-permute-start(bf16[64,2048]{1,0:T(8,128)(2,1)S(1)} %get-tuple-element.57.refs_0_), channel_id=1, source_target_pairs={{0,4},{4,0},{1,5},{5,1},{2,6},{6,2},{3,7},{7,3},{8,12},{12,8},{9,1... | collective-permute-start | bytes 786440 | tf_op jit(solution)/shard_map/ppermute | solution.py:14
  5.5 13.3 %collective-permute-start = (bf16[64,2048]{1,0:T(8,128)(2,1)S(1)}, bf16[64,2048]{1,0:T(8,128)(2,1)S(1)}, u32[]{:S(2)}, u32[]{:S(2)}) collective-permute-start(bf16[64,2048]{1,0:T(8,128)(2,1)S(1)} %get-tuple-element.57.refs_0_), channel_id=1, source_target_pairs={{0,3},{1,0},{2,1},{3,2},{4,7},{5,4},{6,5},{7,6},{8,11},{9,8},{10,9... | collective-permute-start | bytes 786440 | tf_op jit(solution)/shard_map/ppermute | solution.py:14
  9.6 11.1 %collective-permute-start.7 = (bf16[64,2048]{1,0:T(8,128)(2,1)S(1)}, bf16[64,2048]{1,0:T(8,128)(2,1)S(1)}, u32[]{:S(2)}, u32[]{:S(2)}) collective-permute-start(bf16[64,2048]{1,0:T(8,128)(2,1)S(1)} %get-tuple-element.56.refs_8_), channel_id=1, source_target_pairs={{0,24},{8,0},{16,8},{24,16},{1,25},{9,1},{17,9},{25,17},{2,26},{10... | collective-permute-start | bytes 786440 | tf_op jit(solution)/shard_map/ppermute | solution.py:14
  12.6 9.8 %collective-permute-start.2 = (bf16[64,2048]{1,0:T(8,128)(2,1)S(1)}, bf16[64,2048]{1,0:T(8,128)(2,1)S(1)}, u32[]{:S(2)}, u32[]{:S(2)}) collective-permute-start(bf16[64,2048]{1,0:T(8,128)(2,1)S(1)} %get-tuple-element.57.refs_0_), channel_id=1, source_target_pairs={{0,1},{1,2},{2,3},{3,0},{4,5},{5,6},{6,7},{7,4},{8,9},{9,10},{10,1... | collective-permute-start | bytes 786440 | tf_op jit(solution)/shard_map/ppermute | solution.py:14
  12.7 27.0 %copy-start.12 = (bf16[64,2048]{1,0:T(8,128)(2,1)}, bf16[64,2048]{1,0:T(8,128)(2,1)S(1)}, u32[]{:S(2)}) copy-start(bf16[64,2048]{1,0:T(8,128)(2,1)S(1)} %collective-permute-done.10.refs_12_) | copy-start | bytes 786436
  12.7 11.9 %collective-permute-start.9 = (bf16[64,2048]{1,0:T(8,128)(2,1)S(1)}, bf16[64,2048]{1,0:T(8,128)(2,1)S(1)}, u32[]{:S(2)}, u32[]{:S(2)}) collective-permute-start(bf16[64,2048]{1,0:T(8,128)(2,1)S(1)} %get-tuple-element.56.refs_8_), channel_id=1, source_target_pairs={{0,8},{8,16},{16,24},{24,0},{1,9},{9,17},{17,25},{25,1},{2,10},{10... | collective-permute-start | bytes 786440 | tf_op jit(solution)/shard_map/ppermute | solution.py:14
  17.0 22.7 %copy-start.13 = (bf16[64,2048]{1,0:T(8,128)(2,1)}, bf16[64,2048]{1,0:T(8,128)(2,1)S(1)}, u32[]{:S(2)}) copy-start(bf16[64,2048]{1,0:T(8,128)(2,1)S(1)} %collective-permute-done.3.refs_4_) | copy-start | bytes 786436
  17.0 9.5 %collective-permute-start.12 = (bf16[64,2048]{1,0:T(8,128)(2,1)S(1)}, bf16[64,2048]{1,0:T(8,128)(2,1)S(1)}, u32[]{:S(2)}, u32[]{:S(2)}) collective-permute-start(bf16[64,2048]{1,0:T(8,128)(2,1)S(1)} %collective-permute-done.10.refs_12_), channel_id=1, source_target_pairs={{0,8},{8,16},{16,24},{24,0},{1,9},{9,17},{17,25},{25,1},{2,10},{10... | collective-permute-start | bytes 786440 | tf_op jit(solution)/shard_map/ppermute | solution.py:14
  18.8 20.9 %copy-start.14 = (bf16[64,2048]{1,0:T(8,128)(2,1)}, bf16[64,2048]{1,0:T(8,128)(2,1)S(1)}, u32[]{:S(2)}) copy-start(bf16[64,2048]{1,0:T(8,128)(2,1)S(1)} %collective-permute-done.refs_1_) | copy-start | bytes 786436
  18.8 11.2 %collective-permute-start.5 = (bf16[64,2048]{1,0:T(8,128)(2,1)S(1)}, bf16[64,2048]{1,0:T(8,128)(2,1)S(1)}, u32[]{:S(2)}, u32[]{:S(2)}) collective-permute-start(bf16[64,2048]{1,0:T(8,128)(2,1)S(1)} %collective-permute-done.3.refs_4_), channel_id=1, source_target_pairs={{0,1},{1,2},{2,3},{3,0},{4,5},{5,6},{6,7},{7,4},{8,9},{9,10},{10,1... | collective-permute-start | bytes 786440 | tf_op jit(solution)/shard_map/ppermute | solution.py:14
  20.7 19.0 %copy-start.15 = (bf16[64,2048]{1,0:T(8,128)(2,1)}, bf16[64,2048]{1,0:T(8,128)(2,1)S(1)}, u32[]{:S(2)}) copy-start(bf16[64,2048]{1,0:T(8,128)(2,1)S(1)} %collective-permute-done.7.refs_9_) | copy-start | bytes 786436
  20.7 11.1 %collective-permute-start.11 = (bf16[64,2048]{1,0:T(8,128)(2,1)S(1)}, bf16[64,2048]{1,0:T(8,128)(2,1)S(1)}, u32[]{:S(2)}, u32[]{:S(2)}) collective-permute-start(bf16[64,2048]{1,0:T(8,128)(2,1)S(1)} %collective-permute-done.10.refs_12_), channel_id=1, source_target_pairs={{0,24},{8,0},{16,8},{24,16},{1,25},{9,1},{17,9},{25,17},{2,26},{10... | collective-permute-start | bytes 786440 | tf_op jit(solution)/shard_map/ppermute | solution.py:14
  22.4 17.4 %copy-start.16 = (bf16[64,2048]{1,0:T(8,128)(2,1)}, bf16[64,2048]{1,0:T(8,128)(2,1)S(1)}, u32[]{:S(2)}) copy-start(bf16[64,2048]{1,0:T(8,128)(2,1)S(1)} %collective-permute-done.2.refs_3_) | copy-start | bytes 786436
  22.4 9.6 %collective-permute-start.4 = (bf16[64,2048]{1,0:T(8,128)(2,1)S(1)}, bf16[64,2048]{1,0:T(8,128)(2,1)S(1)}, u32[]{:S(2)}, u32[]{:S(2)}) collective-permute-start(bf16[64,2048]{1,0:T(8,128)(2,1)S(1)} %collective-permute-done.3.refs_4_), channel_id=1, source_target_pairs={{0,3},{1,0},{2,1},{3,2},{4,7},{5,4},{6,5},{7,6},{8,11},{9,8},{10,9... | collective-permute-start | bytes 786440 | tf_op jit(solution)/shard_map/ppermute | solution.py:14
  24.6 44.2 %collective-permute-start.18 = (bf16[1,8,64,2048]{3,2,1,0:T(8,128)(2,1)}, bf16[1,8,64,2048]{3,2,1,0:T(8,128)(2,1)}, u32[]{:S(2)}, u32[]{:S(2)}) collective-permute-start(bf16[1,8,64,2048]{3,2,1,0:T(8,128)(2,1)} %param.8), channel_id=1, source_target_pairs={{32,0},{64,32},{96,64},{0,96},{33,1},{65,33},{97,65},{1,97},{34,2}... | collective-permute-start | bytes 6291464 | tf_op jit(solution)/shard_map/ppermute | solution.py:376
  26.5 8.2 %collective-permute-start.1 = (bf16[64,2048]{1,0:T(8,128)(2,1)S(1)}, bf16[64,2048]{1,0:T(8,128)(2,1)S(1)}, u32[]{:S(2)}, u32[]{:S(2)}) collective-permute-start(bf16[64,2048]{1,0:T(8,128)(2,1)S(1)} %collective-permute-done.refs_1_), channel_id=1, source_target_pairs={{0,3},{1,0},{2,1},{3,2},{4,7},{5,4},{6,5},{7,6},{8,11},{9,8},{10,9... | collective-permute-start | bytes 786440 | tf_op jit(solution)/shard_map/ppermute | solution.py:14
  30.0 6.5 %collective-permute-start.8 = (bf16[64,2048]{1,0:T(8,128)(2,1)S(1)}, bf16[64,2048]{1,0:T(8,128)(2,1)}, u32[]{:S(2)}, u32[]{:S(2)}) collective-permute-start(bf16[64,2048]{1,0:T(8,128)(2,1)S(1)} %collective-permute-done.7.refs_9_), channel_id=1, source_target_pairs={{0,24},{8,0},{16,8},{24,16},{1,25},{9,1},{17,9},{25,17},{2,26},{10... | collective-permute-start | bytes 786440 | tf_op jit(solution)/shard_map/ppermute | solution.py:14
  31.8 7.7 %collective-permute-start.13 = (bf16[64,2048]{1,0:T(8,128)(2,1)S(1)}, bf16[64,2048]{1,0:T(8,128)(2,1)}, u32[]{:S(2)}, u32[]{:S(2)}) collective-permute-start(bf16[64,2048]{1,0:T(8,128)(2,1)S(1)} %collective-permute-done.12.refs_15_), channel_id=1, source_target_pairs={{0,8},{8,16},{16,24},{24,0},{1,9},{9,17},{17,25},{25,1},{2,10},{10... | collective-permute-start | bytes 786440 | tf_op jit(solution)/shard_map/ppermute | solution.py:14
  32.0 7.7 %collective-permute-start.6 = (bf16[64,2048]{1,0:T(8,128)(2,1)S(1)}, bf16[64,2048]{1,0:T(8,128)(2,1)}, u32[]{:S(2)}, u32[]{:S(2)}) collective-permute-start(bf16[64,2048]{1,0:T(8,128)(2,1)S(1)} %collective-permute-done.5.refs_7_), channel_id=1, source_target_pairs={{0,1},{1,2},{2,3},{3,0},{4,5},{5,6},{6,7},{7,4},{8,9},{9,10},{10,1... | collective-permute-start | bytes 786440 | tf_op jit(solution)/shard_map/ppermute | solution.py:14
  44.4 45.2 %collective-permute-start.14 = (bf16[2,4,64,2048]{3,2,1,0:T(8,128)(2,1)}, bf16[2,4,64,2048]{3,2,1,0:T(8,128)(2,1)S(1)}, u32[]{:S(2)}, u32[]{:S(2)}) collective-permute-start(bf16[2,4,64,2048]{3,2,1,0:T(8,128)(2,1)} %get-tuple-element.26.refs_0_.refs_2_), channel_id=1, source_target_pairs={{0,24},{8,0},{16,8},{24,16},{1,25},{9,1},{17,9},{25,17},{2,26},{10... | collective-permute-start | bytes 6291464 | tf_op jit(solution)/shard_map/ppermute | solution.py:14
  47.5 45.5 %collective-permute-start.15 = (bf16[2,4,64,2048]{3,2,1,0:T(8,128)(2,1)}, bf16[2,4,64,2048]{3,2,1,0:T(8,128)(2,1)}, u32[]{:S(2)}, u32[]{:S(2)}) collective-permute-start(bf16[2,4,64,2048]{3,2,1,0:T(8,128)(2,1)} %get-tuple-element.26.refs_0_.refs_2_), channel_id=1, source_target_pairs={{0,8},{8,16},{16,24},{24,0},{1,9},{9,17},{17,25},{25,1},{2,10},{10... | collective-permute-start | bytes 6291464 | tf_op jit(solution)/shard_map/ppermute | solution.py:14
  47.5 45.5 %collective-permute-start.16 = (bf16[2,4,64,2048]{3,2,1,0:T(8,128)(2,1)}, bf16[2,4,64,2048]{3,2,1,0:T(8,128)(2,1)}, u32[]{:S(2)}, u32[]{:S(2)}) collective-permute-start(bf16[2,4,64,2048]{3,2,1,0:T(8,128)(2,1)} %get-tuple-element.27.refs_3_.refs_5_.refs_7_), channel_id=1, source_target_pairs={{0,3},{1,0},{2,1},{3,2},{4,7},{5,4},{6,5},{7,6},{8,11},{9,8},{10,9... | collective-permute-start | bytes 6291464 | tf_op jit(solution)/shard_map/ppermute | solution.py:14
  47.5 45.5 %collective-permute-start.17 = (bf16[2,4,64,2048]{3,2,1,0:T(8,128)(2,1)}, bf16[2,4,64,2048]{3,2,1,0:T(8,128)(2,1)}, u32[]{:S(2)}, u32[]{:S(2)}) collective-permute-start(bf16[2,4,64,2048]{3,2,1,0:T(8,128)(2,1)} %get-tuple-element.27.refs_3_.refs_5_.refs_7_), channel_id=1, source_target_pairs={{0,1},{1,2},{2,3},{3,0},{4,5},{5,6},{6,7},{7,4},{8,9},{9,10},{10,1... | collective-permute-start | bytes 6291464 | tf_op jit(solution)/shard_map/ppermute | solution.py:14
  96.8 21.1 %collective-permute-start.19 = (bf16[4,64,2048]{2,1,0:T(8,128)(2,1)}, bf16[4,64,2048]{2,1,0:T(8,128)(2,1)S(1)}, u32[]{:S(2)}, u32[]{:S(2)}) collective-permute-start(bf16[4,64,2048]{2,1,0:T(8,128)(2,1)} %get-tuple-element.28), channel_id=1, source_target_pairs={{0,24},{8,0},{16,8},{24,16},{1,25},{9,1},{17,9},{25,17},{2,26},{10... | collective-permute-start | bytes 3145736 | tf_op jit(solution)/shard_map/ppermute | solution.py:14
  99.8 21.4 %collective-permute-start.20 = (bf16[4,64,2048]{2,1,0:T(8,128)(2,1)}, bf16[4,64,2048]{2,1,0:T(8,128)(2,1)S(1)}, u32[]{:S(2)}, u32[]{:S(2)}) collective-permute-start(bf16[4,64,2048]{2,1,0:T(8,128)(2,1)} %get-tuple-element.29), channel_id=1, source_target_pairs={{0,8},{8,16},{16,24},{24,0},{1,9},{9,17},{17,25},{25,1},{2,10},{10... | collective-permute-start | bytes 3145736 | tf_op jit(solution)/shard_map/ppermute | solution.py:14
  99.8 21.4 %collective-permute-start.21 = (bf16[4,64,2048]{2,1,0:T(8,128)(2,1)}, bf16[4,64,2048]{2,1,0:T(8,128)(2,1)S(1)}, u32[]{:S(2)}, u32[]{:S(2)}) collective-permute-start(bf16[4,64,2048]{2,1,0:T(8,128)(2,1)} %get-tuple-element.30), channel_id=1, source_target_pairs={{0,3},{1,0},{2,1},{3,2},{4,7},{5,4},{6,5},{7,6},{8,11},{9,8},{10,9... | collective-permute-start | bytes 3145736 | tf_op jit(solution)/shard_map/ppermute | solution.py:14
  100.1 21.5 %collective-permute-start.22 = (bf16[4,64,2048]{2,1,0:T(8,128)(2,1)}, bf16[4,64,2048]{2,1,0:T(8,128)(2,1)}, u32[]{:S(2)}, u32[]{:S(2)}) collective-permute-start(bf16[4,64,2048]{2,1,0:T(8,128)(2,1)} %get-tuple-element.31), channel_id=1, source_target_pairs={{0,1},{1,2},{2,3},{3,0},{4,5},{5,6},{6,7},{7,4},{8,9},{9,10},{10,1... | collective-permute-start | bytes 3145736 | tf_op jit(solution)/shard_map/ppermute | solution.py:14
  122.6 30.5 %all-to-all-start.1 = ((bf16[32,64,512]{2,1,0:T(8,128)(2,1)}), bf16[32,64,512]{2,1,0:T(8,128)(2,1)}, u32[]{:S(2)}, u32[]{:S(2)}) async-start(bf16[32,64,512]{2,1,0:T(8,128)(2,1)} %hold.1), calls=%async_computation.1 | async-start | bytes 4194304 | tf_op jit(solution)/shard_map/all_to_all | solution.py:385
  153.1 56.2 %all-to-all-start = ((bf16[32,8,64,128]{3,2,1,0:T(8,128)(2,1)}), bf16[32,8,64,128]{3,2,1,0:T(8,128)(2,1)}, u32[]{:S(2)}, u32[]{:S(2)}) async-start(bf16[32,8,64,128]{3,2,1,0:T(8,128)(2,1)} %absorb.1), calls=%async_computation | async-start | bytes 8388608 | tf_op jit(solution)/shard_map/all_to_all | solution.py:387
  209.3 16.9 %copy-start.5 = (s32[3]{0:T(128)S(1)}, s32[3]{0:T(128)}, u32[]{:S(2)}) copy-start(s32[3]{0:T(128)} %pad_add_fusion.at_ref.refs_0_) | copy-start | bytes 40
  229.6 10.8 %collective-permute-start.30 = (bf16[256,1024]{1,0:T(8,128)(2,1)S(1)}, bf16[256,1024]{1,0:T(8,128)(2,1)S(1)}, u32[]{:S(2)}, u32[]{:S(2)}) collective-permute-start(bf16[256,1024]{1,0:T(8,128)(2,1)S(1)} %get-tuple-element.45), channel_id=1, source_target_pairs={{0,1},{1,2},{2,3},{3,0},{4,5},{5,6},{6,7},{7,4},{8,9},{9,10},{10,1... | collective-permute-start | bytes 1572872 | tf_op jit(solution)/shard_map/ppermute | solution.py:14
  229.7 11.4 %collective-permute-start.32 = (bf16[256,1024]{1,0:T(8,128)(2,1)S(1)}, bf16[256,1024]{1,0:T(8,128)(2,1)S(1)}, u32[]{:S(2)}, u32[]{:S(2)}) collective-permute-start(bf16[256,1024]{1,0:T(8,128)(2,1)S(1)} %get-tuple-element.49), channel_id=1, source_target_pairs={{0,3},{1,0},{2,1},{3,2},{4,7},{5,4},{6,5},{7,6},{8,11},{9,8},{10,9... | collective-permute-start | bytes 1572872 | tf_op jit(solution)/shard_map/ppermute | solution.py:14
  236.9 12.0 %collective-permute-start.23 = (bf16[256,1024]{1,0:T(8,128)(2,1)S(1)}, bf16[256,1024]{1,0:T(8,128)(2,1)S(1)}, u32[]{:S(2)}, u32[]{:S(2)}) collective-permute-start(bf16[256,1024]{1,0:T(8,128)(2,1)S(1)} %get-tuple-element.37), channel_id=1, source_target_pairs={{0,8},{8,16},{16,24},{24,0},{1,9},{9,17},{17,25},{25,1},{2,10},{10... | collective-permute-start | bytes 1572872 | tf_op jit(solution)/shard_map/ppermute | solution.py:14
  237.5 13.1 %collective-permute-start.25 = (bf16[256,1024]{1,0:T(8,128)(2,1)S(1)}, bf16[256,1024]{1,0:T(8,128)(2,1)S(1)}, u32[]{:S(2)}, u32[]{:S(2)}) collective-permute-start(bf16[256,1024]{1,0:T(8,128)(2,1)S(1)} %get-tuple-element.41), channel_id=1, source_target_pairs={{0,24},{8,0},{16,8},{24,16},{1,25},{9,1},{17,9},{25,17},{2,26},{10... | collective-permute-start | bytes 1572872 | tf_op jit(solution)/shard_map/ppermute | solution.py:14
  240.7 22.9 %collective-permute-start.31 = (bf16[2,256,1024]{2,1,0:T(8,128)(2,1)S(1)}, bf16[2,256,1024]{2,1,0:T(8,128)(2,1)}, u32[]{:S(2)}, u32[]{:S(2)}) collective-permute-start(bf16[2,256,1024]{2,1,0:T(8,128)(2,1)S(1)} %pad_maximum_fusion.2), channel_id=1, source_target_pairs={{0,1},{1,2},{2,3},{3,0},{4,5},{5,6},{6,7},{7,4},{8,9},{9,10},{10,1... | collective-permute-start | bytes 3145736 | tf_op jit(solution)/shard_map/ppermute | solution.py:14
  242.4 22.0 %collective-permute-start.33 = (bf16[2,256,1024]{2,1,0:T(8,128)(2,1)}, bf16[2,256,1024]{2,1,0:T(8,128)(2,1)}, u32[]{:S(2)}, u32[]{:S(2)}) collective-permute-start(bf16[2,256,1024]{2,1,0:T(8,128)(2,1)} %pad_maximum_fusion.3), channel_id=1, source_target_pairs={{0,3},{1,0},{2,1},{3,2},{4,7},{5,4},{6,5},{7,6},{8,11},{9,8},{10,9... | collective-permute-start | bytes 3145736 | tf_op jit(solution)/shard_map/ppermute | solution.py:14
  250.2 26.1 %collective-permute-start.24 = (bf16[2,256,1024]{2,1,0:T(8,128)(2,1)}, bf16[2,256,1024]{2,1,0:T(8,128)(2,1)}, u32[]{:S(2)}, u32[]{:S(2)}) collective-permute-start(bf16[2,256,1024]{2,1,0:T(8,128)(2,1)} %pad_maximum_fusion), channel_id=1, source_target_pairs={{0,8},{8,16},{16,24},{24,0},{1,9},{9,17},{17,25},{25,1},{2,10},{10... | collective-permute-start | bytes 3145736 | tf_op jit(solution)/shard_map/ppermute | solution.py:14
  251.9 24.5 %collective-permute-start.26 = (bf16[2,256,1024]{2,1,0:T(8,128)(2,1)}, bf16[2,256,1024]{2,1,0:T(8,128)(2,1)}, u32[]{:S(2)}, u32[]{:S(2)}) collective-permute-start(bf16[2,256,1024]{2,1,0:T(8,128)(2,1)} %pad_maximum_fusion.1), channel_id=1, source_target_pairs={{0,24},{8,0},{16,8},{24,16},{1,25},{9,1},{17,9},{25,17},{2,26},{10... | collective-permute-start | bytes 3145736 | tf_op jit(solution)/shard_map/ppermute | solution.py:14
  267.4 15.5 %collective-permute-start.34 = (bf16[2,64,1024]{2,1,0:T(8,128)(2,1)S(1)}, bf16[2,64,1024]{2,1,0:T(8,128)(2,1)}, u32[]{:S(2)}, u32[]{:S(2)}) collective-permute-start(bf16[2,64,1024]{2,1,0:T(8,128)(2,1)S(1)} %get-tuple-element.50), channel_id=1, source_target_pairs={{0,8},{8,16},{16,24},{24,0},{1,9},{9,17},{17,25},{25,1},{2,10},{10... | collective-permute-start | bytes 786440 | tf_op jit(solution)/shard_map/ppermute | solution.py:14
  272.6 11.8 %collective-permute-start.35 = (bf16[2,64,1024]{2,1,0:T(8,128)(2,1)}, bf16[2,64,1024]{2,1,0:T(8,128)(2,1)}, u32[]{:S(2)}, u32[]{:S(2)}) collective-permute-start(bf16[2,64,1024]{2,1,0:T(8,128)(2,1)} %get-tuple-element.52), channel_id=1, source_target_pairs={{0,24},{8,0},{16,8},{24,16},{1,25},{9,1},{17,9},{25,17},{2,26},{10... | collective-permute-start | bytes 786440 | tf_op jit(solution)/shard_map/ppermute | solution.py:14
  272.6 11.9 %collective-permute-start.36 = (bf16[2,64,1024]{2,1,0:T(8,128)(2,1)S(1)}, bf16[2,64,1024]{2,1,0:T(8,128)(2,1)}, u32[]{:S(2)}, u32[]{:S(2)}) collective-permute-start(bf16[2,64,1024]{2,1,0:T(8,128)(2,1)S(1)} %get-tuple-element.51), channel_id=1, source_target_pairs={{0,16},{8,24},{16,0},{24,8},{1,17},{9,25},{17,1},{25,9},{2,18},{10... | collective-permute-start | bytes 786440 | tf_op jit(solution)/shard_map/ppermute | solution.py:14
  279.4 10.2 %collective-permute-start.27 = (bf16[2,64,1024]{2,1,0:T(8,128)(2,1)}, bf16[2,64,1024]{2,1,0:T(8,128)(2,1)S(1)}, u32[]{:S(2)}, u32[]{:S(2)}) collective-permute-start(bf16[2,64,1024]{2,1,0:T(8,128)(2,1)} %get-tuple-element.53), channel_id=1, source_target_pairs={{0,1},{1,2},{2,3},{3,0},{4,5},{5,6},{6,7},{7,4},{8,9},{9,10},{10,1... | collective-permute-start | bytes 786440 | tf_op jit(solution)/shard_map/ppermute | solution.py:14
  279.4 10.9 %collective-permute-start.28 = (bf16[2,64,1024]{2,1,0:T(8,128)(2,1)S(1)}, bf16[2,64,1024]{2,1,0:T(8,128)(2,1)}, u32[]{:S(2)}, u32[]{:S(2)}) collective-permute-start(bf16[2,64,1024]{2,1,0:T(8,128)(2,1)S(1)} %get-tuple-element.55), channel_id=1, source_target_pairs={{0,3},{1,0},{2,1},{3,2},{4,7},{5,4},{6,5},{7,6},{8,11},{9,8},{10,9... | collective-permute-start | bytes 786440 | tf_op jit(solution)/shard_map/ppermute | solution.py:14
  282.9 9.5 %collective-permute-start.29 = (bf16[2,64,1024]{2,1,0:T(8,128)(2,1)S(1)}, bf16[2,64,1024]{2,1,0:T(8,128)(2,1)}, u32[]{:S(2)}, u32[]{:S(2)}) collective-permute-start(bf16[2,64,1024]{2,1,0:T(8,128)(2,1)S(1)} %get-tuple-element.54), channel_id=1, source_target_pairs={{0,2},{1,3},{2,0},{3,1},{4,6},{5,7},{6,4},{7,5},{8,10},{9,11},{10,... | collective-permute-start | bytes 786440 | tf_op jit(solution)/shard_map/ppermute | solution.py:14
  293.7 8.0 %collective-permute-start.37 = (bf16[64,2048]{1,0:T(8,128)(2,1)S(1)}, bf16[64,2048]{1,0:T(8,128)(2,1)S(1)}, u32[]{:S(2)}, u32[]{:S(2)}) collective-permute-start(bf16[64,2048]{1,0:T(8,128)(2,1)S(1)} %fusion.13), channel_id=1, source_target_pairs={{0,4},{4,0},{1,5},{5,1},{2,6},{6,2},{3,7},{7,3},{8,12},{12,8},{9,1... | collective-permute-start | bytes 786440 | tf_op jit(solution)/shard_map/ppermute | solution.py:14
  (16 other events, 114.4 us)
